TPU v7x, 128 devices: a whole 4x4x4 slice. The times are simulated.
128 devices in a mesh: row: 64 (over z, y, x), col: 2 (over core).
Axes of the slice: x: 4, y: 4, z: 4, core: 2. Of those that a mesh axis runs over, the one named last changes fastest.
Arguments:
- queries: bfloat16 [65536, 1024], P(('row', 'col')), may hold values from -150 to 150
- keys: bfloat16 [65536, 128], P(('col', 'row')), may hold values from -6.1 to 6.1
- values: bfloat16 [65536, 128], P(('col', 'row')), may hold values from -6 to 6
- row_ptr: int32 [513], replicated, may hold values from 0 to 8192, as said below
- col_blocks: int32 [8192], replicated, may hold values from 0 to 511, as said below
- w_out: bfloat16 [1024, 8192], replicated, may hold values from -0.1875 to 0.1875
Outputs:
- projected: bfloat16 [65536, 8192], P(('row', 'col'))
Inputs may be any that keep to these rules, and one draw needn't show every extreme that they name: row_ptr[0] is 0 and row_ptr never falls; block-row b lists row_ptr[b+1] - row_ptr[b] blocks, 1 to 31; row_ptr[g * 8] = g * 8 * 16 for every g; in every group of 8 consecutive block-rows some block-row lists exactly 31 blocks. col_blocks[e] lies in key group e mod 2, that is between (e mod 2) * 256 and (e mod 2) * 256 + 255; the blocks listed for one block-row are distinct.
All inputs are finite; a program needn't handle non-finite values.
Results may differ from a plain program's by a relative error of at most 0.0055.
Values may be sent and summed in bfloat16 or wider, within the bound.
No kernel may reach another device: no remote copies, remote signals or barrier semaphores. Data moves between devices by JAX's collectives and lax.ppermute only.
A program may use at most 192 MiB of HBM per device.

v0:
```python
import jax
import jax.numpy as jnp
from jax import lax
from jax.experimental import pallas as pl
from jax.experimental.pallas import tpu as pltpu
from jax.sharding import PartitionSpec as P

HEADS = 8
HEAD_DIM = 128
BLOCK = 128
RPD = 8
AVG = 16
SHARD = 512
BIG = 688
SMALL = 2 * SHARD - BIG
SPLIT = BIG - SHARD - BLOCK
QUADS = 4
SLOTS = 64
SCALE = 1.4426950408889634 * HEAD_DIM ** (-0.5)
STRIDE = {"x": 1, "y": 4, "z": 16}
BIG_AXES = ("yzx", "xyz")
SMALL_AXES = ("zxy", "zxy")


def send(array, axes, place):
    pairs = []
    for row in range(64):
        for core in range(2):
            stride = STRIDE[axes[core]]
            at = (row // stride) % 4
            pairs.append((row * 2 + core, (row + (place(at) - at) * stride) * 2 + core))
    return lax.ppermute(array, ("row", "col"), pairs)


def swap(array):
    pairs = [(row * 2 + core, row * 2 + 1 - core) for row in range(64) for core in range(2)]
    return lax.ppermute(array, ("row", "col"), pairs)


def together(*arrays):
    return lax.optimization_barrier(arrays)


def back(array, axes):
    return send(array, axes, lambda at: (at + 3) % 4)


def across(array, axes):
    return send(array, axes, lambda at: (at + 2) % 4)


def forth(array, axes):
    return send(array, axes, lambda at: (at + 1) % 4)


def gathered(both):
    big = both[:BIG].reshape(-1, 8, HEAD_DIM)
    small = both[BIG:].reshape(-1, 8, HEAD_DIM)
    big_axes = [[axes[phase] for axes in BIG_AXES] for phase in range(3)]
    small_axes = [[axes[phase] for axes in SMALL_AXES] for phase in range(3)]
    b, s = big_axes[0], small_axes[0]
    big, *others = together(
        big,
        across(big, b),
        across(small, s),
        back(big, b),
        back(small, s),
        forth(big, b),
        forth(small, s),
    )
    big = jnp.concatenate([big, others[2], others[4], others[0]], axis=0)
    small = jnp.concatenate([small, others[3], others[5], others[1]], axis=0)
    half = big.shape[0] // 2, small.shape[0] // 2
    b, s = big_axes[1], small_axes[1]
    big_after, big_before, small_after, small_before = together(
        back(big, b), forth(big, b), back(small, s), forth(small, s)
    )
    big_low, big_high, small_low, small_high = together(
        back(big_after[: half[0]], b),
        forth(big_before[half[0] :], b),
        back(small_after[: half[1]], s),
        forth(small_before[half[1] :], s),
    )
    b, s = big_axes[2], small_axes[2]
    big_first, big_second, small_first, small_second = together(
        jnp.concatenate([big, big_after], axis=0),
        jnp.concatenate([big_before, big_low, big_high], axis=0),
        jnp.concatenate([small, small_after], axis=0),
        jnp.concatenate([small_before, small_low, small_high], axis=0),
    )
    big_a, big_d, small_a, small_d = together(
        back(big_first, b), forth(big_second, b), back(small_first, s), forth(small_second, s)
    )
    big_b, big_c = back(big_second, b), forth(big_first, b)
    small_b, small_c = back(small_second, s), forth(small_first, s)
    big_low, big_high = back(big_a, b), forth(big_d, b)
    small_low, small_high = back(small_a, s), forth(small_d, s)
    flat = lambda *parts: [
        pltpu.with_memory_space_constraint(part.reshape(-1, HEAD_DIM), pltpu.HBM) for part in parts
    ]
    return (
        flat(big_first, big_second, big_a, big_b, big_c, big_d, big_low, big_high),
        flat(
            small_first, small_second, small_a, small_b, small_c, small_d, small_low, small_high
        ),
    )


def gray(number):
    return number ^ (number >> 1)


def slot_of(theirs, mine, axes):
    first, second, third = axes
    return (
        gray((theirs[first] - mine[first]) & 3)
        + 4 * gray((theirs[second] - mine[second]) & 3)
        + 16 * gray((theirs[third] - mine[third]) & 3)
    )


def choose(number, count, act):
    def between(low, high):
        if high - low == 1:
            act(low)
        else:
            middle = (low + high) // 2
            lax.cond(number < middle, lambda: between(low, middle), lambda: between(middle, high))

    between(0, count)


def aligned(row):
    return pl.multiple_of(row, 16)


def fetch(first_piece, codes, big, small, kbuf, vbuf, sems):
    count = len(big)

    def parts(index):
        code = codes[index]
        in_big, in_small, within = code & 63, (code >> 6) & 63, code >> 12
        return in_big, in_small, within, index * BLOCK

    def has(place):
        piece = (place >> 3) - first_piece
        return (piece >= 0) & (piece < count)

    def copy(source, row, rows, target, to, sem):
        return pltpu.make_async_copy(
            source.at[pl.ds(aligned(row), rows), :], target.at[pl.ds(aligned(to), rows), :], sem
        )

    def issue(index, _):
        in_big, in_small, within, at = parts(index)

        def from_big(piece):
            row = (in_big & 7) * BIG
            copy(big[piece], row + within * BLOCK, BLOCK, kbuf, at, sems.at[0, index]).start()

            @pl.when(within == 0)
            def _():
                copy(big[piece], row + SHARD, BLOCK, vbuf, at, sems.at[1, index]).start()

            @pl.when(within == 1)
            def _():
                copy(big[piece], row + SHARD + BLOCK, SPLIT, vbuf, at, sems.at[1, index]).start()

        def from_small(piece):
            row = (in_small & 7) * SMALL

            @pl.when(within == 1)
            def _():
                copy(small[piece], row, BLOCK - SPLIT, vbuf, at + SPLIT, sems.at[2, index]).start()

            @pl.when(within >= 2)
            def _():
                copy(
                    small[piece],
                    row + BLOCK - SPLIT + (within - 2) * BLOCK,
                    BLOCK,
                    vbuf,
                    at,
                    sems.at[2, index],
                ).start()

        pl.when(has(in_big))(lambda: choose((in_big >> 3) - first_piece, count, from_big))
        pl.when(has(in_small) & (within >= 1))(
            lambda: choose((in_small >> 3) - first_piece, count, from_small)
        )
        return 0

    def finish(index, _):
        in_big, in_small, within, at = parts(index)

        @pl.when(has(in_big))
        def _():
            copy(big[0], 0, BLOCK, kbuf, at, sems.at[0, index]).wait()

            @pl.when(within == 0)
            def _():
                copy(big[0], 0, BLOCK, vbuf, at, sems.at[1, index]).wait()

            @pl.when(within == 1)
            def _():
                copy(big[0], 0, SPLIT, vbuf, at, sems.at[1, index]).wait()

        @pl.when(has(in_small))
        def _():
            @pl.when(within == 1)
            def _():
                copy(small[0], 0, BLOCK - SPLIT, vbuf, at + SPLIT, sems.at[2, index]).wait()

            @pl.when(within >= 2)
            def _():
                copy(small[0], 0, BLOCK, vbuf, at, sems.at[2, index]).wait()

        return 0

    lax.fori_loop(0, SLOTS, issue, 0)
    lax.fori_loop(0, SLOTS, finish, 0)


def fetch_near(codes, *refs):
    fetch(0, codes, refs[:6], refs[6:12], *refs[12:])


def fetch_far(codes, *refs):
    fetch(6, codes, refs[:2], refs[2:4], *refs[6:])


def fetched(codes, big, small):
    vmem = pl.BlockSpec(memory_space=pltpu.VMEM)
    smem = pl.BlockSpec(memory_space=pltpu.SMEM)
    hbm = pl.BlockSpec(memory_space=pltpu.HBM)
    blocks = jax.ShapeDtypeStruct((SLOTS * BLOCK, HEAD_DIM), jnp.bfloat16)
    common = dict(
        out_shape=(blocks, blocks),
        out_specs=(vmem, vmem),
        scratch_shapes=[pltpu.SemaphoreType.DMA((3, SLOTS))],
        compiler_params=pltpu.CompilerParams(vmem_limit_bytes=10 * 2**20),
    )
    near = pl.pallas_call(
        fetch_near, name="fetch_near", in_specs=[smem, *[hbm] * 12], **common
    )(codes, *big[:6], *small[:6])
    return pl.pallas_call(
        fetch_far,
        name="fetch_far",
        in_specs=[smem, *[hbm] * 4, vmem, vmem],
        input_output_aliases={5: 0, 6: 1},
        **common,
    )(codes, *big[6:], *small[6:], *near)


def attend(place, starts, q_ref, kbuf, vbuf, o_ref, stat_ref, s_ref, m_ref, acc):
    first_row = place[0]

    def blocks_of(buf, slot, end, count):
        return [
            buf[pl.ds(aligned(jnp.minimum(slot + k, end - 1) * BLOCK), BLOCK), :]
            for k in range(count)
        ]

    def block_row(local, _):
        row = first_row + local
        begin, end = starts[row], starts[row + 1]
        number = end - begin
        quads = (number + 1) >> 2
        rest = begin + 4 * quads
        m_ref[...] = jnp.full(m_ref.shape, -1e30, jnp.float32)
        acc[...] = jnp.zeros(acc.shape, jnp.float32)

        def score(slot, into, count):
            keys = jnp.concatenate(blocks_of(kbuf, slot, end, count), axis=0)
            heads = jnp.concatenate(
                [
                    q_ref[
                        pl.ds(aligned(local * BLOCK), BLOCK),
                        head * HEAD_DIM : (head + 1) * HEAD_DIM,
                    ]
                    for head in range(HEADS)
                ],
                axis=0,
            )
            scores = lax.dot_general(
                heads, keys, (((1,), (1,)), ((), ())), preferred_element_type=jnp.float32
            )
            columns = [scores[:, k * BLOCK : (k + 1) * BLOCK] for k in range(count)]
            top = m_ref[...]
            for column in columns:
                top = jnp.maximum(top, column)
            m_ref[...] = top
            columns[-1] = jnp.where(slot + count - 1 < end, columns[-1], -1e30)
            for k in range(count):
                s_ref[into, :, k * BLOCK : (k + 1) * BLOCK] = columns[k]

        def weigh(slot, into, count):
            values = jnp.concatenate(blocks_of(vbuf, slot, end, count), axis=0)
            values = jnp.concatenate([values, jnp.ones(values.shape, values.dtype)], axis=1)
            top = m_ref[...]
            weights = jnp.concatenate(
                [
                    jnp.exp2(s_ref[into, :, k * BLOCK : (k + 1) * BLOCK] * SCALE - top).astype(
                        jnp.bfloat16
                    )
                    for k in range(count)
                ],
                axis=1,
            )
            acc[...] += jnp.dot(weights, values, preferred_element_type=jnp.float32)

        def each_quad(step):
            def body(quad, _):
                step(begin + 4 * quad, quad, 4)
                return 0

            lax.fori_loop(0, quads, body, 0)
            pl.when(rest < end)(lambda: step(rest, quads, 2))

        each_quad(score)
        m_ref[...] = jnp.broadcast_to(
            jnp.max(m_ref[...], axis=1, keepdims=True) * SCALE, m_ref.shape
        )
        each_quad(weigh)

        lane = lax.broadcasted_iota(jnp.int32, (BLOCK, HEAD_DIM), 1)
        tops = sums = jnp.zeros((BLOCK, HEAD_DIM), jnp.float32)
        for head in range(HEADS):
            rows = slice(head * BLOCK, (head + 1) * BLOCK)
            o_ref[pl.ds(aligned(local * BLOCK), BLOCK), head * HEAD_DIM : (head + 1) * HEAD_DIM] = (
                acc[rows, :HEAD_DIM].astype(jnp.bfloat16)
            )
            tops = jnp.where(lane == head, m_ref[rows, :], tops)
            sums = jnp.where(lane == head, acc[rows, HEAD_DIM:], sums)
        stat_ref[pl.ds(aligned(local * BLOCK), BLOCK), :HEAD_DIM] = tops
        stat_ref[pl.ds(aligned(local * BLOCK), BLOCK), HEAD_DIM:] = sums
        return 0

    lax.fori_loop(0, 4, block_row, 0)


def attention_call(place, starts, queries, keys, values):
    rows = queries.shape[0]
    smem = pl.BlockSpec(memory_space=pltpu.SMEM)
    vmem = pl.BlockSpec(memory_space=pltpu.VMEM)
    return pl.pallas_call(
        attend,
        name="attend",
        out_shape=(
            jax.ShapeDtypeStruct((rows, HEADS * HEAD_DIM), jnp.bfloat16),
            jax.ShapeDtypeStruct((rows, 2 * HEAD_DIM), jnp.float32),
        ),
        in_specs=[smem, smem, vmem, vmem, vmem],
        out_specs=(vmem, vmem),
        scratch_shapes=[
            pltpu.VMEM((QUADS, HEADS * BLOCK, 4 * BLOCK), jnp.float32),
            pltpu.VMEM((HEADS * BLOCK, BLOCK), jnp.float32),
            pltpu.VMEM((HEADS * BLOCK, 2 * HEAD_DIM), jnp.float32),
        ],
        compiler_params=pltpu.CompilerParams(vmem_limit_bytes=24 * 2**20),
    )(place, starts, queries, keys, values)


def project(o_a, stat_a, o_b, stat_b, w_ref, out_ref, att):
    step, tile = pl.program_id(0), out_ref.shape[1]

    @pl.when(step == 0)
    def _():
        top_a, top_b = stat_a[:, :HEAD_DIM], stat_b[:, :HEAD_DIM]
        top = jnp.maximum(top_a, top_b)
        by_a, by_b = jnp.exp2(top_a - top), jnp.exp2(top_b - top)
        total = stat_a[:, HEAD_DIM:] * by_a + stat_b[:, HEAD_DIM:] * by_b
        by_a, by_b = by_a / total, by_b / total
        for head in range(HEADS):
            columns = slice(head * HEAD_DIM, (head + 1) * HEAD_DIM)
            shape = (att.shape[0], HEAD_DIM)
            part_a = o_a[:, columns].astype(jnp.float32) * jnp.broadcast_to(
                by_a[:, head : head + 1], shape
            )
            part_b = o_b[:, columns].astype(jnp.float32) * jnp.broadcast_to(
                by_b[:, head : head + 1], shape
            )
            att[:, columns] = (part_a + part_b).astype(jnp.bfloat16)

    out_ref[...] = jnp.dot(
        att[...],
        w_ref[:, pl.ds(pl.multiple_of(step * tile, 128), tile)],
        preferred_element_type=jnp.float32,
    ).astype(jnp.bfloat16)


def projection_call(o_a, stat_a, o_b, stat_b, w_out):
    rows, depth = o_a.shape
    width, tile = w_out.shape[1], 1024
    vmem = pl.BlockSpec(memory_space=pltpu.VMEM)
    return pl.pallas_call(
        project,
        name="project",
        grid=(width // tile,),
        out_shape=jax.ShapeDtypeStruct((rows, width), jnp.bfloat16),
        in_specs=[vmem] * 5,
        out_specs=pl.BlockSpec((rows, tile), lambda i: (0, i)),
        scratch_shapes=[pltpu.VMEM((rows, depth), jnp.bfloat16)],
        compiler_params=pltpu.CompilerParams(vmem_limit_bytes=30 * 2**20),
    )(o_a, stat_a, o_b, stat_b, w_out)


def tables(row_pos, core, row_ptr, col_blocks):
    ptr = lax.dynamic_slice_in_dim(row_ptr, row_pos * RPD, RPD + 1, 0)
    cols = lax.dynamic_slice_in_dim(col_blocks, row_pos * (RPD * AVG), RPD * AVG, 0)
    starts = (ptr - row_pos * (RPD * AVG) + 1 - core) >> 1
    halves = cols.reshape(-1, 2)
    block = jnp.where(core == 0, halves[:, 0], halves[:, 1]) - 256 * core
    owner, within = block >> 2, block & 3
    mine = {axis: (row_pos // STRIDE[axis]) & 3 for axis in "xyz"}
    theirs = {axis: (owner // STRIDE[axis]) & 3 for axis in "xyz"}
    in_big = jnp.where(
        core == 0, slot_of(theirs, mine, BIG_AXES[0]), slot_of(theirs, mine, BIG_AXES[1])
    )
    in_small = slot_of(theirs, mine, SMALL_AXES[0])
    return starts.astype(jnp.int32), (in_big | in_small << 6 | within << 12).astype(jnp.int32)


def local(queries, keys, values, row_ptr, col_blocks, w_out):
    row_pos = lax.axis_index("row")
    core = lax.axis_index("col")
    big, small = gathered(jnp.concatenate([keys, values], axis=0))
    other_queries = swap(queries)
    starts, codes = tables(row_pos, core, row_ptr, col_blocks)
    listed = fetched(codes, big, small)
    place = lambda first: first.reshape(1).astype(jnp.int32)
    o_theirs, stat_theirs = attention_call(
        place(4 - 4 * core), starts, other_queries, *listed
    )
    o_got, stat_got = swap(o_theirs), swap(stat_theirs)
    o_own, stat_own = attention_call(place(4 * core), starts, queries, *listed)
    return projection_call(o_own, stat_own, o_got, stat_got, w_out)


def solution(mesh):
    in_specs = (
        P(("row", "col"), None),
        P(("col", "row"), None),
        P(("col", "row"), None),
        P(),
        P(),
        P(),
    )
    out_specs = P(("row", "col"), None)
    return jax.shard_map(local, mesh=mesh, in_specs=in_specs, out_specs=out_specs, check_vma=False)
```

profile of v0, /device:TPU:1, one launch (start us, length us, event | category | flops | bytes accessed | tf_op | source)
XLA Modules:
  0.0 146.3 jit_solution(14396760574149760080)
XLA Ops:
  0.0 0.9 fusion
  0.9 3.6 %collective-permute-start = (bf16[86,8,128]{2,1,0:T(8,128)(2,1)S(1)}, bf16[86,8,128]{2,1,0:T(8,128)(2,1)S(1)}, u32[]{:S(2)}, u32[]{:S(2)}) collective-permute-start(bf16[86,8,128]{2,1,0:T(8,128)(2,1)S(1)} %fusion), channel_id=1, source_target_pairs={{0,16},{1,5},{2,18},{3,7},{4,20},{5,1},{6,22},{7,3},{8,24},{9,13},... | collective-permute-start | bytes 528392 | tf_op jit(solution)/shard_map/ppermute | solution.py:32
  4.6 0.9 collective-permute-start.2
  5.4 0.6 collective-permute-start.4
  6.1 0.9 slice_bitcast_fusion
  7.0 3.7 %collective-permute-start.1 = (bf16[42,8,128]{2,1,0:T(8,128)(2,1)S(1)}, bf16[42,8,128]{2,1,0:T(8,128)(2,1)S(1)}, u32[]{:S(2)}, u32[]{:S(2)}) collective-permute-start(bf16[42,8,128]{2,1,0:T(8,128)(2,1)S(1)} %slice_bitcast_fusion), channel_id=1, source_target_pairs={{0,64},{1,65},{2,66},{3,67},{4,68},{5,69},{6,70},{7,71},{8,72},{9,... | collective-permute-start | bytes 258056 | tf_op jit(solution)/shard_map/ppermute | solution.py:32
  10.6 0.4 collective-permute-start.3
  11.1 1.4 collective-permute-done.1
  12.5 1.3 collective-permute-start.5
  13.8 0.6 collective-permute-done.3
  14.4 3.1 %collective-permute-done.5 = bf16[42,8,128]{2,1,0:T(8,128)(2,1)S(1)} collective-permute-done((bf16[42,8,128]{2,1,0:T(8,128)(2,1)S(1)}, bf16[42,8,128]{2,1,0:T(8,128)(2,1)S(1)}, u32[]{:S(2)}, u32[]{:S(2)}) %collective-permute-start.5) | collective-permute-done | bytes 86048 | tf_op jit(solution)/shard_map/ppermute | solution.py:32
  17.6 0.0 collective-permute-done
  17.6 0.1 constant_dynamic-update-slice_fusion.2
  17.7 0.1 constant_dynamic-update-slice_fusion.1
  17.8 0.1 constant_dynamic-update-slice_fusion
  17.8 2.8 %collective-permute-start.6 = (bf16[344,8,128]{2,1,0:T(8,128)(2,1)S(1)}, bf16[344,8,128]{2,1,0:T(8,128)(2,1)S(1)}, u32[]{:S(2)}, u32[]{:S(2)}) collective-permute-start(bf16[344,8,128]{2,1,0:T(8,128)(2,1)S(1)} %get-tuple-element.69), channel_id=1, source_target_pairs={{0,96},{1,25},{2,98},{3,27},{4,100},{5,29},{6,102},{7,31},{8,104},... | collective-permute-start | bytes 2113544 | tf_op jit(solution)/shard_map/ppermute | solution.py:32
  20.6 0.0 collective-permute-start.7
  20.7 2.1 %collective-permute-start.8 = (bf16[168,8,128]{2,1,0:T(8,128)(2,1)S(1)}, bf16[168,8,128]{2,1,0:T(8,128)(2,1)S(1)}, u32[]{:S(2)}, u32[]{:S(2)}) collective-permute-start(bf16[168,8,128]{2,1,0:T(8,128)(2,1)S(1)} %pad_maximum_fusion.2), channel_id=1, source_target_pairs={{0,6},{1,7},{2,0},{3,1},{4,2},{5,3},{6,4},{7,5},{8,14},{9,15},{10,... | collective-permute-start | bytes 1032200 | tf_op jit(solution)/shard_map/ppermute | solution.py:32
  22.9 4.5 %collective-permute-done.8 = bf16[168,8,128]{2,1,0:T(8,128)(2,1)S(1)} collective-permute-done((bf16[168,8,128]{2,1,0:T(8,128)(2,1)S(1)}, bf16[168,8,128]{2,1,0:T(8,128)(2,1)S(1)}, u32[]{:S(2)}, u32[]{:S(2)}) %collective-permute-start.8) | collective-permute-done | bytes 344096 | tf_op jit(solution)/shard_map/ppermute | solution.py:32
  27.4 3.0 %collective-permute-done.9 = bf16[168,8,128]{2,1,0:T(8,128)(2,1)S(1)} collective-permute-done((bf16[168,8,128]{2,1,0:T(8,128)(2,1)S(1)}, bf16[168,8,128]{2,1,0:T(8,128)(2,1)S(1)}, u32[]{:S(2)}, u32[]{:S(2)}) %collective-permute-start.9) | collective-permute-done | bytes 344096 | tf_op jit(solution)/shard_map/ppermute | solution.py:32
  30.4 1.7 %collective-permute-done.7 = bf16[344,8,128]{2,1,0:T(8,128)(2,1)S(1)} collective-permute-done((bf16[344,8,128]{2,1,0:T(8,128)(2,1)S(1)}, bf16[344,8,128]{2,1,0:T(8,128)(2,1)S(1)}, u32[]{:S(2)}, u32[]{:S(2)}) %collective-permute-start.7) | collective-permute-done | bytes 704544 | tf_op jit(solution)/shard_map/ppermute | solution.py:32
  32.1 1.4 collective-permute-start.10
  33.5 0.2 collective-permute-start.11
  33.8 2.1 %collective-permute-start.12 = (bf16[84,8,128]{2,1,0:T(8,128)(2,1)S(1)}, bf16[84,8,128]{2,1,0:T(8,128)(2,1)S(1)}, u32[]{:S(2)}, u32[]{:S(2)}) collective-permute-start(bf16[84,8,128]{2,1,0:T(8,128)(2,1)S(1)} %slice.30), channel_id=1, source_target_pairs={{0,6},{1,7},{2,0},{3,1},{4,2},{5,3},{6,4},{7,5},{8,14},{9,15},{10,... | collective-permute-start | bytes 516104 | tf_op jit(solution)/shard_map/ppermute | solution.py:32
  35.9 0.1 collective-permute-start.13
  36.1 0.1 constant_dynamic-update-slice_fusion.4
  36.2 0.0 copy-start.3
  36.2 2.1 %collective-permute-done.12 = bf16[84,8,128]{2,1,0:T(8,128)(2,1)S(1)} collective-permute-done((bf16[84,8,128]{2,1,0:T(8,128)(2,1)S(1)}, bf16[84,8,128]{2,1,0:T(8,128)(2,1)S(1)}, u32[]{:S(2)}, u32[]{:S(2)}) %collective-permute-start.12) | collective-permute-done | bytes 172064 | tf_op jit(solution)/shard_map/ppermute | solution.py:32
  38.3 3.2 %collective-permute-done.13 = bf16[84,8,128]{2,1,0:T(8,128)(2,1)S(1)} collective-permute-done((bf16[84,8,128]{2,1,0:T(8,128)(2,1)S(1)}, bf16[84,8,128]{2,1,0:T(8,128)(2,1)S(1)}, u32[]{:S(2)}, u32[]{:S(2)}) %collective-permute-start.13) | collective-permute-done | bytes 172064 | tf_op jit(solution)/shard_map/ppermute | solution.py:32
  41.5 0.1 pad_maximum_fusion.1
  41.6 0.0 copy-start
  41.6 0.2 pad_maximum_fusion
  41.8 1.8 %collective-permute-start.14 = (bf16[688,8,128]{2,1,0:T(8,128)(2,1)S(1)}, bf16[688,8,128]{2,1,0:T(8,128)(2,1)}, u32[]{:S(2)}, u32[]{:S(2)}) collective-permute-start(bf16[688,8,128]{2,1,0:T(8,128)(2,1)S(1)} %constant_dynamic-update-slice_fusion.4), channel_id=1, source_target_pairs={{0,6},{1,97},{2,0},{3,99},{4,2},{5,101},{6,4},{7,103},{8,14},{9,10... | collective-permute-start | bytes 4227080 | tf_op jit(solution)/shard_map/ppermute | solution.py:32
  43.6 1.7 %collective-permute-start.16 = (bf16[336,8,128]{2,1,0:T(8,128)(2,1)S(1)}, bf16[336,8,128]{2,1,0:T(8,128)(2,1)}, u32[]{:S(2)}, u32[]{:S(2)}) collective-permute-start(bf16[336,8,128]{2,1,0:T(8,128)(2,1)S(1)} %constant_dynamic-update-slice_fusion.9), channel_id=1, source_target_pairs={{0,24},{1,25},{2,26},{3,27},{4,28},{5,29},{6,30},{7,31},{8,0},{9,1... | collective-permute-start | bytes 2064392 | tf_op jit(solution)/shard_map/ppermute | solution.py:32
  45.3 2.5 %collective-permute-start.22 = (bf16[688,8,128]{2,1,0:T(8,128)(2,1)S(1)}, bf16[688,8,128]{2,1,0:T(8,128)(2,1)S(1)}, u32[]{:S(2)}, u32[]{:S(2)}) collective-permute-start(bf16[688,8,128]{2,1,0:T(8,128)(2,1)S(1)} %pad_maximum_fusion), channel_id=1, source_target_pairs={{0,6},{1,97},{2,0},{3,99},{4,2},{5,101},{6,4},{7,103},{8,14},{9,10... | collective-permute-start | bytes 4227080 | tf_op jit(solution)/shard_map/ppermute | solution.py:32
  47.8 6.4 %collective-permute-done.16 = bf16[336,8,128]{2,1,0:T(8,128)(2,1)} collective-permute-done((bf16[336,8,128]{2,1,0:T(8,128)(2,1)S(1)}, bf16[336,8,128]{2,1,0:T(8,128)(2,1)}, u32[]{:S(2)}, u32[]{:S(2)}) %collective-permute-start.16) | collective-permute-done | bytes 688160 | tf_op jit(solution)/shard_map/ppermute | solution.py:32
  54.2 2.5 %collective-permute-done.17 = bf16[336,8,128]{2,1,0:T(8,128)(2,1)} collective-permute-done((bf16[336,8,128]{2,1,0:T(8,128)(2,1)S(1)}, bf16[336,8,128]{2,1,0:T(8,128)(2,1)}, u32[]{:S(2)}, u32[]{:S(2)}) %collective-permute-start.17) | collective-permute-done | bytes 688160 | tf_op jit(solution)/shard_map/ppermute | solution.py:32
  56.7 0.5 collective-permute-start.24
  57.2 2.5 %collective-permute-done.14 = bf16[688,8,128]{2,1,0:T(8,128)(2,1)} collective-permute-done((bf16[688,8,128]{2,1,0:T(8,128)(2,1)S(1)}, bf16[688,8,128]{2,1,0:T(8,128)(2,1)}, u32[]{:S(2)}, u32[]{:S(2)}) %collective-permute-start.14) | collective-permute-done | bytes 1409056 | tf_op jit(solution)/shard_map/ppermute | solution.py:32
  59.8 0.0 collective-permute-start.25
  59.8 2.9 %collective-permute-done.15 = bf16[688,8,128]{2,1,0:T(8,128)(2,1)} collective-permute-done((bf16[688,8,128]{2,1,0:T(8,128)(2,1)S(1)}, bf16[688,8,128]{2,1,0:T(8,128)(2,1)}, u32[]{:S(2)}, u32[]{:S(2)}) %collective-permute-start.15) | collective-permute-done | bytes 1409056 | tf_op jit(solution)/shard_map/ppermute | solution.py:32
  62.7 0.1 collective-permute-start.18
  62.8 5.9 %collective-permute-done.24 = bf16[336,8,128]{2,1,0:T(8,128)(2,1)S(1)} collective-permute-done((bf16[336,8,128]{2,1,0:T(8,128)(2,1)S(1)}, bf16[336,8,128]{2,1,0:T(8,128)(2,1)S(1)}, u32[]{:S(2)}, u32[]{:S(2)}) %collective-permute-start.24) | collective-permute-done | bytes 688160 | tf_op jit(solution)/shard_map/ppermute | solution.py:32
  68.7 2.7 %collective-permute-done.25 = bf16[336,8,128]{2,1,0:T(8,128)(2,1)S(1)} collective-permute-done((bf16[336,8,128]{2,1,0:T(8,128)(2,1)S(1)}, bf16[336,8,128]{2,1,0:T(8,128)(2,1)S(1)}, u32[]{:S(2)}, u32[]{:S(2)}) %collective-permute-start.25) | collective-permute-done | bytes 688160 | tf_op jit(solution)/shard_map/ppermute | solution.py:32
  71.5 9.3 %collective-permute-start.26 = (bf16[512,1024]{1,0:T(8,128)(2,1)S(1)}, bf16[512,1024]{1,0:T(8,128)(2,1)S(1)}, u32[]{:S(2)}, u32[]{:S(2)}) collective-permute-start(bf16[512,1024]{1,0:T(8,128)(2,1)S(1)} %copy-done), channel_id=1, source_target_pairs={{0,1},{1,0},{2,3},{3,2},{4,5},{5,4},{6,7},{7,6},{8,9},{9,8},{10,11... | collective-permute-start | bytes 3145736 | tf_op jit(solution)/shard_map/ppermute | solution.py:37
  80.7 1.5 collective-permute-start.20
  82.2 0.3 collective-permute-start.21
  82.5 0.8 copy-done.5
  83.3 0.8 dynamic_slice.7
  84.0 0.1 reshape.74
  84.2 0.8 subtract_shift-right-arithmetic_fusion.starts
  85.0 0.2 shift-right-arithmetic_reduce_fusion
  85.2 0.0 slice-start
  85.2 0.0 slice-start.1
  85.2 7.1 %fetch_near.1 = (bf16[8192,128]{1,0:T(8,128)(2,1)S(1)}, bf16[8192,128]{1,0:T(8,128)(2,1)S(1)}) custom-call(s32[64]{0:T(128)S(1)} %fusion.3.codes, bf16[5504,128]{1,0:T(8,128)(2,1)} %bitcast.28, bf16[5504,128]{1,0:T(8,128)(2,1)} %bitcast.26, bf16[5504,128]{1,0:T(8,128)(2,1)} %bitcast.9.refs_2_, bf16[5504,128]{1,0:T(8,128)(2,1)} %bitcast.29, ...), custom_call_target="tpu_custom_call" | custom-call | tf_op jit(solution)/shard_map/fetch_near/pallas_call | solution.py:243
  92.3 4.6 %collective-permute-done.20 = bf16[336,8,128]{2,1,0:T(8,128)(2,1)} collective-permute-done((bf16[336,8,128]{2,1,0:T(8,128)(2,1)}, bf16[336,8,128]{2,1,0:T(8,128)(2,1)}, u32[]{:S(2)}, u32[]{:S(2)}) %collective-permute-start.20) | collective-permute-done | bytes 688160 | tf_op jit(solution)/shard_map/ppermute | solution.py:32
  96.9 2.2 %collective-permute-done.21 = bf16[336,8,128]{2,1,0:T(8,128)(2,1)} collective-permute-done((bf16[336,8,128]{2,1,0:T(8,128)(2,1)}, bf16[336,8,128]{2,1,0:T(8,128)(2,1)}, u32[]{:S(2)}, u32[]{:S(2)}) %collective-permute-start.21) | collective-permute-done | bytes 688160 | tf_op jit(solution)/shard_map/ppermute | solution.py:32
  99.1 5.7 %fetch_far.1 = (bf16[8192,128]{1,0:T(8,128)(2,1)S(1)}, bf16[8192,128]{1,0:T(8,128)(2,1)S(1)}) custom-call(s32[64]{0:T(128)S(1)} %fusion.3.codes, bf16[5504,128]{1,0:T(8,128)(2,1)} %bitcast.3.refs_0_, bf16[5504,128]{1,0:T(8,128)(2,1)} %bitcast.4.refs_1_, bf16[2688,128]{1,0:T(8,128)(2,1)} %bitcast.5.refs_2_, ...), custom_call_target="tpu_custom_call", output_to_operand_aliasing={{0}: (5, {}), {1}: (6, {})} | custom-call | tf_op jit(solution)/shard_map/fetch_far/pallas_call | solution.py:246
  104.8 0.0 slice-start.3
  104.9 7.3 %attend.3 = (bf16[512,1024]{1,0:T(8,128)(2,1)S(1)}, f32[512,256]{1,0:T(8,128)S(1)}) custom-call(s32[1]{0:T(128)} %bitcast.19.place, s32[9]{0:T(128)S(1)} %subtract_shift-right-arithmetic_fusion.starts, bf16[512,1024]{1,0:T(8,128)(2,1)S(1)} %collective-permute-done.26.q_ref, bf16[8192,128]{1,0:T(8,128)(2,1)S(1)} %get-tuple-element.61.kbuf, ...), custom_call_target="tpu_custom_call" | custom-call | tf_op jit(solution)/shard_map/attend/pallas_call | solution.py:346
  112.2 8.8 %collective-permute-start.27 = (bf16[512,1024]{1,0:T(8,128)(2,1)S(1)}, bf16[512,1024]{1,0:T(8,128)(2,1)S(1)}, u32[]{:S(2)}, u32[]{:S(2)}) collective-permute-start(bf16[512,1024]{1,0:T(8,128)(2,1)S(1)} %get-tuple-element.65), channel_id=1, source_target_pairs={{0,1},{1,0},{2,3},{3,2},{4,5},{5,4},{6,7},{7,6},{8,9},{9,8},{10,11... | collective-permute-start | bytes 3145736 | tf_op jit(solution)/shard_map/ppermute | solution.py:37
  121.0 0.1 collective-permute-start.28
  121.1 12.7 %attend.2 = (bf16[512,1024]{1,0:T(8,128)(2,1)S(1)}, f32[512,256]{1,0:T(8,128)S(1)}) custom-call(s32[1]{0:T(128)} %bitcast.place, s32[9]{0:T(128)S(1)} %subtract_shift-right-arithmetic_fusion.starts, bf16[512,1024]{1,0:T(8,128)(2,1)S(1)} %copy-done, bf16[8192,128]{1,0:T(8,128)(2,1)S(1)} %get-tuple-element.61.kbuf, bf16[8192,128]{1,0:T(8,128)(2,1)S(1)} %get-tuple-element.62.vbuf), custom_call_target="tpu_custom_call" | custom-call | tf_op jit(solution)/shard_map/attend/pallas_call | solution.py:346
  133.9 12.4 %project.1 = bf16[512,8192]{1,0:T(8,128)(2,1)} custom-call(bf16[512,1024]{1,0:T(8,128)(2,1)S(1)} %get-tuple-element.63.o_a, f32[512,256]{1,0:T(8,128)S(1)} %get-tuple-element.64.stat_a, bf16[512,1024]{1,0:T(8,128)(2,1)S(1)} %collective-permute-done.27.o_b, f32[512,256]{1,0:T(8,128)S(1)} %collective-permute-done.28.stat_b, bf16[1024,8192]{1,0:T(8,128)(2,1)S(1)} %bitcast.25), custom_call_target="tpu_custom_call" | custom-call | tf_op jit(solution)/shard_map/project/pallas_call | solution.py:396
  (52 shorter events, 0.4 us)
Async XLA Ops:
  0.9 16.7 %collective-permute-start = (bf16[86,8,128]{2,1,0:T(8,128)(2,1)S(1)}, bf16[86,8,128]{2,1,0:T(8,128)(2,1)S(1)}, u32[]{:S(2)}, u32[]{:S(2)}) collective-permute-start(bf16[86,8,128]{2,1,0:T(8,128)(2,1)S(1)} %fusion), channel_id=1, source_target_pairs={{0,16},{1,5},{2,18},{3,7},{4,20},{5,1},{6,22},{7,3},{8,24},{9,13},... | collective-permute-start | bytes 528392 | tf_op jit(solution)/shard_map/ppermute | solution.py:32
  4.6 13.0 %collective-permute-start.2 = (bf16[86,8,128]{2,1,0:T(8,128)(2,1)S(1)}, bf16[86,8,128]{2,1,0:T(8,128)(2,1)S(1)}, u32[]{:S(2)}, u32[]{:S(2)}) collective-permute-start(bf16[86,8,128]{2,1,0:T(8,128)(2,1)S(1)} %fusion), channel_id=1, source_target_pairs={{0,24},{1,7},{2,26},{3,1},{4,28},{5,3},{6,30},{7,5},{8,0},{9,15},{... | collective-permute-start | bytes 528392 | tf_op jit(solution)/shard_map/ppermute | solution.py:32
  5.4 12.2 %collective-permute-start.4 = (bf16[86,8,128]{2,1,0:T(8,128)(2,1)S(1)}, bf16[86,8,128]{2,1,0:T(8,128)(2,1)S(1)}, u32[]{:S(2)}, u32[]{:S(2)}) collective-permute-start(bf16[86,8,128]{2,1,0:T(8,128)(2,1)S(1)} %fusion), channel_id=1, source_target_pairs={{0,8},{1,3},{2,10},{3,5},{4,12},{5,7},{6,14},{7,1},{8,16},{9,11},{... | collective-permute-start | bytes 528392 | tf_op jit(solution)/shard_map/ppermute | solution.py:32
  7.0 15.9 %copy-start.7 = (bf16[512,128]{1,0:T(8,128)(2,1)S(1)}, bf16[512,128]{1,0:T(8,128)(2,1)}, u32[]{:S(2)}) copy-start(bf16[512,128]{1,0:T(8,128)(2,1)} %param.8) | copy-start | bytes 393220
  7.0 5.5 %collective-permute-start.1 = (bf16[42,8,128]{2,1,0:T(8,128)(2,1)S(1)}, bf16[42,8,128]{2,1,0:T(8,128)(2,1)S(1)}, u32[]{:S(2)}, u32[]{:S(2)}) collective-permute-start(bf16[42,8,128]{2,1,0:T(8,128)(2,1)S(1)} %slice_bitcast_fusion), channel_id=1, source_target_pairs={{0,64},{1,65},{2,66},{3,67},{4,68},{5,69},{6,70},{7,71},{8,72},{9,... | collective-permute-start | bytes 258056 | tf_op jit(solution)/shard_map/ppermute | solution.py:32
  10.6 3.8 %collective-permute-start.3 = (bf16[42,8,128]{2,1,0:T(8,128)(2,1)S(1)}, bf16[42,8,128]{2,1,0:T(8,128)(2,1)S(1)}, u32[]{:S(2)}, u32[]{:S(2)}) collective-permute-start(bf16[42,8,128]{2,1,0:T(8,128)(2,1)S(1)} %slice_bitcast_fusion), channel_id=1, source_target_pairs={{0,96},{1,97},{2,98},{3,99},{4,100},{5,101},{6,102},{7,103},{8,104... | collective-permute-start | bytes 258056 | tf_op jit(solution)/shard_map/ppermute | solution.py:32
  12.5 5.1 %collective-permute-start.5 = (bf16[42,8,128]{2,1,0:T(8,128)(2,1)S(1)}, bf16[42,8,128]{2,1,0:T(8,128)(2,1)S(1)}, u32[]{:S(2)}, u32[]{:S(2)}) collective-permute-start(bf16[42,8,128]{2,1,0:T(8,128)(2,1)S(1)} %slice_bitcast_fusion), channel_id=1, source_target_pairs={{0,32},{1,33},{2,34},{3,35},{4,36},{5,37},{6,38},{7,39},{8,40},{9,... | collective-permute-start | bytes 258056 | tf_op jit(solution)/shard_map/ppermute | solution.py:32
  17.8 12.6 %collective-permute-start.6 = (bf16[344,8,128]{2,1,0:T(8,128)(2,1)S(1)}, bf16[344,8,128]{2,1,0:T(8,128)(2,1)S(1)}, u32[]{:S(2)}, u32[]{:S(2)}) collective-permute-start(bf16[344,8,128]{2,1,0:T(8,128)(2,1)S(1)} %get-tuple-element.69), channel_id=1, source_target_pairs={{0,96},{1,25},{2,98},{3,27},{4,100},{5,29},{6,102},{7,31},{8,104},... | collective-permute-start | bytes 2113544 | tf_op jit(solution)/shard_map/ppermute | solution.py:32
  20.6 11.5 %collective-permute-start.7 = (bf16[344,8,128]{2,1,0:T(8,128)(2,1)S(1)}, bf16[344,8,128]{2,1,0:T(8,128)(2,1)S(1)}, u32[]{:S(2)}, u32[]{:S(2)}) collective-permute-start(bf16[344,8,128]{2,1,0:T(8,128)(2,1)S(1)} %get-tuple-element.69), channel_id=1, source_target_pairs={{0,32},{1,9},{2,34},{3,11},{4,36},{5,13},{6,38},{7,15},{8,40},{9,1... | collective-permute-start | bytes 2113544 | tf_op jit(solution)/shard_map/ppermute | solution.py:32
  20.7 6.7 %collective-permute-start.8 = (bf16[168,8,128]{2,1,0:T(8,128)(2,1)S(1)}, bf16[168,8,128]{2,1,0:T(8,128)(2,1)S(1)}, u32[]{:S(2)}, u32[]{:S(2)}) collective-permute-start(bf16[168,8,128]{2,1,0:T(8,128)(2,1)S(1)} %pad_maximum_fusion.2), channel_id=1, source_target_pairs={{0,6},{1,7},{2,0},{3,1},{4,2},{5,3},{6,4},{7,5},{8,14},{9,15},{10,... | collective-permute-start | bytes 1032200 | tf_op jit(solution)/shard_map/ppermute | solution.py:32
  22.8 7.6 %collective-permute-start.9 = (bf16[168,8,128]{2,1,0:T(8,128)(2,1)S(1)}, bf16[168,8,128]{2,1,0:T(8,128)(2,1)S(1)}, u32[]{:S(2)}, u32[]{:S(2)}) collective-permute-start(bf16[168,8,128]{2,1,0:T(8,128)(2,1)S(1)} %pad_maximum_fusion.2), channel_id=1, source_target_pairs={{0,2},{1,3},{2,4},{3,5},{4,6},{5,7},{6,0},{7,1},{8,10},{9,11},{10,... | collective-permute-start | bytes 1032200 | tf_op jit(solution)/shard_map/ppermute | solution.py:32
  32.1 9.4 %collective-permute-start.10 = (bf16[172,8,128]{2,1,0:T(8,128)(2,1)S(1)}, bf16[172,8,128]{2,1,0:T(8,128)(2,1)S(1)}, u32[]{:S(2)}, u32[]{:S(2)}) collective-permute-start(bf16[172,8,128]{2,1,0:T(8,128)(2,1)S(1)} %slice.28), channel_id=1, source_target_pairs={{0,96},{1,25},{2,98},{3,27},{4,100},{5,29},{6,102},{7,31},{8,104},... | collective-permute-start | bytes 1056776 | tf_op jit(solution)/shard_map/ppermute | solution.py:32
  33.5 8.0 %collective-permute-start.11 = (bf16[172,8,128]{2,1,0:T(8,128)(2,1)S(1)}, bf16[172,8,128]{2,1,0:T(8,128)(2,1)S(1)}, u32[]{:S(2)}, u32[]{:S(2)}) collective-permute-start(bf16[172,8,128]{2,1,0:T(8,128)(2,1)S(1)} %slice.29), channel_id=1, source_target_pairs={{0,32},{1,9},{2,34},{3,11},{4,36},{5,13},{6,38},{7,15},{8,40},{9,1... | collective-permute-start | bytes 1056776 | tf_op jit(solution)/shard_map/ppermute | solution.py:32
  33.8 4.5 %collective-permute-start.12 = (bf16[84,8,128]{2,1,0:T(8,128)(2,1)S(1)}, bf16[84,8,128]{2,1,0:T(8,128)(2,1)S(1)}, u32[]{:S(2)}, u32[]{:S(2)}) collective-permute-start(bf16[84,8,128]{2,1,0:T(8,128)(2,1)S(1)} %slice.30), channel_id=1, source_target_pairs={{0,6},{1,7},{2,0},{3,1},{4,2},{5,3},{6,4},{7,5},{8,14},{9,15},{10,... | collective-permute-start | bytes 516104 | tf_op jit(solution)/shard_map/ppermute | solution.py:32
  35.9 5.5 %collective-permute-start.13 = (bf16[84,8,128]{2,1,0:T(8,128)(2,1)S(1)}, bf16[84,8,128]{2,1,0:T(8,128)(2,1)S(1)}, u32[]{:S(2)}, u32[]{:S(2)}) collective-permute-start(bf16[84,8,128]{2,1,0:T(8,128)(2,1)S(1)} %slice.31), channel_id=1, source_target_pairs={{0,2},{1,3},{2,4},{3,5},{4,6},{5,7},{6,0},{7,1},{8,10},{9,11},{10,... | collective-permute-start | bytes 516104 | tf_op jit(solution)/shard_map/ppermute | solution.py:32
  36.1 23.7 %copy-start.6 = (bf16[336,8,128]{2,1,0:T(8,128)(2,1)}, bf16[336,8,128]{2,1,0:T(8,128)(2,1)S(1)}, u32[]{:S(2)}) copy-start(bf16[336,8,128]{2,1,0:T(8,128)(2,1)S(1)} %constant_dynamic-update-slice_fusion.9) | copy-start | bytes 2064388
  36.2 18.0 %copy-start.3 = (bf16[688,8,128]{2,1,0:T(8,128)(2,1)}, bf16[688,8,128]{2,1,0:T(8,128)(2,1)S(1)}, u32[]{:S(2)}) copy-start(bf16[688,8,128]{2,1,0:T(8,128)(2,1)S(1)} %constant_dynamic-update-slice_fusion.4) | copy-start | bytes 4227076
  41.6 15.2 %copy-start.2 = (bf16[336,8,128]{2,1,0:T(8,128)(2,1)}, bf16[336,8,128]{2,1,0:T(8,128)(2,1)S(1)}, u32[]{:S(2)}) copy-start(bf16[336,8,128]{2,1,0:T(8,128)(2,1)S(1)} %pad_maximum_fusion.1) | copy-start | bytes 2064388
  41.6 29.9 %copy-start = (bf16[512,1024]{1,0:T(8,128)(2,1)S(1)}, bf16[512,1024]{1,0:T(8,128)(2,1)}, u32[]{:S(2)}) copy-start(bf16[512,1024]{1,0:T(8,128)(2,1)} %q_ref.1) | copy-start | bytes 3145732
  41.8 43.4 %copy-start.1 = (bf16[688,8,128]{2,1,0:T(8,128)(2,1)}, bf16[688,8,128]{2,1,0:T(8,128)(2,1)S(1)}, u32[]{:S(2)}) copy-start(bf16[688,8,128]{2,1,0:T(8,128)(2,1)S(1)} %pad_maximum_fusion) | copy-start | bytes 4227076
  41.8 18.0 %collective-permute-start.14 = (bf16[688,8,128]{2,1,0:T(8,128)(2,1)S(1)}, bf16[688,8,128]{2,1,0:T(8,128)(2,1)}, u32[]{:S(2)}, u32[]{:S(2)}) collective-permute-start(bf16[688,8,128]{2,1,0:T(8,128)(2,1)S(1)} %constant_dynamic-update-slice_fusion.4), channel_id=1, source_target_pairs={{0,6},{1,97},{2,0},{3,99},{4,2},{5,101},{6,4},{7,103},{8,14},{9,10... | collective-permute-start | bytes 4227080 | tf_op jit(solution)/shard_map/ppermute | solution.py:32
  43.6 19.1 %collective-permute-start.15 = (bf16[688,8,128]{2,1,0:T(8,128)(2,1)S(1)}, bf16[688,8,128]{2,1,0:T(8,128)(2,1)}, u32[]{:S(2)}, u32[]{:S(2)}) collective-permute-start(bf16[688,8,128]{2,1,0:T(8,128)(2,1)S(1)} %pad_maximum_fusion), channel_id=1, source_target_pairs={{0,2},{1,33},{2,4},{3,35},{4,6},{5,37},{6,0},{7,39},{8,10},{9,41},... | collective-permute-start | bytes 4227080 | tf_op jit(solution)/shard_map/ppermute | solution.py:32
  43.6 10.6 %collective-permute-start.16 = (bf16[336,8,128]{2,1,0:T(8,128)(2,1)S(1)}, bf16[336,8,128]{2,1,0:T(8,128)(2,1)}, u32[]{:S(2)}, u32[]{:S(2)}) collective-permute-start(bf16[336,8,128]{2,1,0:T(8,128)(2,1)S(1)} %constant_dynamic-update-slice_fusion.9), channel_id=1, source_target_pairs={{0,24},{1,25},{2,26},{3,27},{4,28},{5,29},{6,30},{7,31},{8,0},{9,1... | collective-permute-start | bytes 2064392 | tf_op jit(solution)/shard_map/ppermute | solution.py:32
  45.3 11.4 %collective-permute-start.17 = (bf16[336,8,128]{2,1,0:T(8,128)(2,1)S(1)}, bf16[336,8,128]{2,1,0:T(8,128)(2,1)}, u32[]{:S(2)}, u32[]{:S(2)}) collective-permute-start(bf16[336,8,128]{2,1,0:T(8,128)(2,1)S(1)} %pad_maximum_fusion.1), channel_id=1, source_target_pairs={{0,8},{1,9},{2,10},{3,11},{4,12},{5,13},{6,14},{7,15},{8,16},{9,17... | collective-permute-start | bytes 2064392 | tf_op jit(solution)/shard_map/ppermute | solution.py:32
  45.3 35.4 %collective-permute-start.22 = (bf16[688,8,128]{2,1,0:T(8,128)(2,1)S(1)}, bf16[688,8,128]{2,1,0:T(8,128)(2,1)S(1)}, u32[]{:S(2)}, u32[]{:S(2)}) collective-permute-start(bf16[688,8,128]{2,1,0:T(8,128)(2,1)S(1)} %pad_maximum_fusion), channel_id=1, source_target_pairs={{0,6},{1,97},{2,0},{3,99},{4,2},{5,101},{6,4},{7,103},{8,14},{9,10... | collective-permute-start | bytes 4227080 | tf_op jit(solution)/shard_map/ppermute | solution.py:32
  54.2 28.0 %collective-permute-start.23 = (bf16[688,8,128]{2,1,0:T(8,128)(2,1)S(1)}, bf16[688,8,128]{2,1,0:T(8,128)(2,1)S(1)}, u32[]{:S(2)}, u32[]{:S(2)}) collective-permute-start(bf16[688,8,128]{2,1,0:T(8,128)(2,1)S(1)} %constant_dynamic-update-slice_fusion.4), channel_id=1, source_target_pairs={{0,2},{1,33},{2,4},{3,35},{4,6},{5,37},{6,0},{7,39},{8,10},{9,41},... | collective-permute-start | bytes 4227080 | tf_op jit(solution)/shard_map/ppermute | solution.py:32
  56.7 12.0 %collective-permute-start.24 = (bf16[336,8,128]{2,1,0:T(8,128)(2,1)S(1)}, bf16[336,8,128]{2,1,0:T(8,128)(2,1)S(1)}, u32[]{:S(2)}, u32[]{:S(2)}) collective-permute-start(bf16[336,8,128]{2,1,0:T(8,128)(2,1)S(1)} %pad_maximum_fusion.1), channel_id=1, source_target_pairs={{0,24},{1,25},{2,26},{3,27},{4,28},{5,29},{6,30},{7,31},{8,0},{9,1... | collective-permute-start | bytes 2064392 | tf_op jit(solution)/shard_map/ppermute | solution.py:32
  59.8 11.7 %collective-permute-start.25 = (bf16[336,8,128]{2,1,0:T(8,128)(2,1)S(1)}, bf16[336,8,128]{2,1,0:T(8,128)(2,1)S(1)}, u32[]{:S(2)}, u32[]{:S(2)}) collective-permute-start(bf16[336,8,128]{2,1,0:T(8,128)(2,1)S(1)} %constant_dynamic-update-slice_fusion.9), channel_id=1, source_target_pairs={{0,8},{1,9},{2,10},{3,11},{4,12},{5,13},{6,14},{7,15},{8,16},{9,17... | collective-permute-start | bytes 2064392 | tf_op jit(solution)/shard_map/ppermute | solution.py:32
  62.7 36.4 %collective-permute-start.18 = (bf16[688,8,128]{2,1,0:T(8,128)(2,1)}, bf16[688,8,128]{2,1,0:T(8,128)(2,1)}, u32[]{:S(2)}, u32[]{:S(2)}) collective-permute-start(bf16[688,8,128]{2,1,0:T(8,128)(2,1)} %collective-permute-done.14), channel_id=1, source_target_pairs={{0,6},{1,97},{2,0},{3,99},{4,2},{5,101},{6,4},{7,103},{8,14},{9,10... | collective-permute-start | bytes 4227080 | tf_op jit(solution)/shard_map/ppermute | solution.py:32
  68.7 13.7 %copy-start.8 = (bf16[336,8,128]{2,1,0:T(8,128)(2,1)}, bf16[336,8,128]{2,1,0:T(8,128)(2,1)S(1)}, u32[]{:S(2)}) copy-start(bf16[336,8,128]{2,1,0:T(8,128)(2,1)S(1)} %collective-permute-done.24) | copy-start | bytes 2064388
  68.7 30.4 %collective-permute-start.19 = (bf16[688,8,128]{2,1,0:T(8,128)(2,1)}, bf16[688,8,128]{2,1,0:T(8,128)(2,1)}, u32[]{:S(2)}, u32[]{:S(2)}) collective-permute-start(bf16[688,8,128]{2,1,0:T(8,128)(2,1)} %collective-permute-done.15), channel_id=1, source_target_pairs={{0,2},{1,33},{2,4},{3,35},{4,6},{5,37},{6,0},{7,39},{8,10},{9,41},... | collective-permute-start | bytes 4227080 | tf_op jit(solution)/shard_map/ppermute | solution.py:32
  71.4 11.0 %copy-start.9 = (bf16[336,8,128]{2,1,0:T(8,128)(2,1)}, bf16[336,8,128]{2,1,0:T(8,128)(2,1)S(1)}, u32[]{:S(2)}) copy-start(bf16[336,8,128]{2,1,0:T(8,128)(2,1)S(1)} %collective-permute-done.25) | copy-start | bytes 2064388
  71.5 33.4 %collective-permute-start.26 = (bf16[512,1024]{1,0:T(8,128)(2,1)S(1)}, bf16[512,1024]{1,0:T(8,128)(2,1)S(1)}, u32[]{:S(2)}, u32[]{:S(2)}) collective-permute-start(bf16[512,1024]{1,0:T(8,128)(2,1)S(1)} %copy-done), channel_id=1, source_target_pairs={{0,1},{1,0},{2,3},{3,2},{4,5},{5,4},{6,7},{7,6},{8,9},{9,8},{10,11... | collective-permute-start | bytes 3145736 | tf_op jit(solution)/shard_map/ppermute | solution.py:37
  80.7 1.5 %copy-start.4 = (bf16[688,8,128]{2,1,0:T(8,128)(2,1)}, bf16[688,8,128]{2,1,0:T(8,128)(2,1)S(1)}, u32[]{:S(2)}) copy-start(bf16[688,8,128]{2,1,0:T(8,128)(2,1)S(1)} %collective-permute-done.22) | copy-start | bytes 4227076
  80.7 16.2 %collective-permute-start.20 = (bf16[336,8,128]{2,1,0:T(8,128)(2,1)}, bf16[336,8,128]{2,1,0:T(8,128)(2,1)}, u32[]{:S(2)}, u32[]{:S(2)}) collective-permute-start(bf16[336,8,128]{2,1,0:T(8,128)(2,1)} %collective-permute-done.16), channel_id=1, source_target_pairs={{0,24},{1,25},{2,26},{3,27},{4,28},{5,29},{6,30},{7,31},{8,0},{9,1... | collective-permute-start | bytes 2064392 | tf_op jit(solution)/shard_map/ppermute | solution.py:32
  82.2 1.1 copy-start.5
  82.2 16.9 %collective-permute-start.21 = (bf16[336,8,128]{2,1,0:T(8,128)(2,1)}, bf16[336,8,128]{2,1,0:T(8,128)(2,1)}, u32[]{:S(2)}, u32[]{:S(2)}) collective-permute-start(bf16[336,8,128]{2,1,0:T(8,128)(2,1)} %collective-permute-done.17), channel_id=1, source_target_pairs={{0,8},{1,9},{2,10},{3,11},{4,12},{5,13},{6,14},{7,15},{8,16},{9,17... | collective-permute-start | bytes 2064392 | tf_op jit(solution)/shard_map/ppermute | solution.py:32
  85.2 48.7 %slice-start = ((s8[16777216]{0:T(1024)(128)(4,1)}), s8[4194304]{0:T(1024)(128)(4,1)S(1)}, s32[]{:S(2)}) async-start(s8[16777216]{0:T(1024)(128)(4,1)} %bitcast.24), calls=%async_computation | async-start | bytes 8388608
  85.2 48.7 %slice-start.1 = ((s8[16777216]{0:T(1024)(128)(4,1)}), s8[4194304]{0:T(1024)(128)(4,1)S(1)}, s32[]{:S(2)}) async-start(s8[16777216]{0:T(1024)(128)(4,1)} %bitcast.24), calls=%async_computation.1 | async-start | bytes 8388608
  99.1 34.8 %slice-start.2 = ((s8[16777216]{0:T(1024)(128)(4,1)}), s8[4194304]{0:T(1024)(128)(4,1)S(1)}, s32[]{:S(2)}) async-start(s8[16777216]{0:T(1024)(128)(4,1)} %bitcast.24), calls=%async_computation.2 | async-start | bytes 8388608
  104.8 29.0 %slice-start.3 = ((s8[16777216]{0:T(1024)(128)(4,1)}), s8[4194304]{0:T(1024)(128)(4,1)S(1)}, s32[]{:S(2)}) async-start(s8[16777216]{0:T(1024)(128)(4,1)} %bitcast.24), calls=%async_computation.3 | async-start | bytes 8388608
  112.2 21.6 %collective-permute-start.27 = (bf16[512,1024]{1,0:T(8,128)(2,1)S(1)}, bf16[512,1024]{1,0:T(8,128)(2,1)S(1)}, u32[]{:S(2)}, u32[]{:S(2)}) collective-permute-start(bf16[512,1024]{1,0:T(8,128)(2,1)S(1)} %get-tuple-element.65), channel_id=1, source_target_pairs={{0,1},{1,0},{2,3},{3,2},{4,5},{5,4},{6,7},{7,6},{8,9},{9,8},{10,11... | collective-permute-start | bytes 3145736 | tf_op jit(solution)/shard_map/ppermute | solution.py:37
  121.0 12.8 %collective-permute-start.28 = (f32[512,256]{1,0:T(8,128)S(1)}, f32[512,256]{1,0:T(8,128)S(1)}, u32[]{:S(2)}, u32[]{:S(2)}) collective-permute-start(f32[512,256]{1,0:T(8,128)S(1)} %get-tuple-element.66), channel_id=1, source_target_pairs={{0,1},{1,0},{2,3},{3,2},{4,5},{5,4},{6,7},{7,6},{8,9},{9,8},{10,11... | collective-permute-start | bytes 1572872 | tf_op jit(solution)/shard_map/ppermute | solution.py:37
where the time goes:
time: 146 us
  waiting for transfers between devices  49.5 us (34%)
  starting transfers between devices  45.8 us (31%)
  Pallas kernels  45.3 us (31%)
  local copies, waits for them, and re-layouts  3.11 us (2%)
  other arithmetic  2.21 us (2%)
    ppermute x26, waiting for transfers between devices, send(): return lax.ppermute(array, ('row', 'col'), pairs)  49.5 us
    ppermute x26, starting transfers between devices, send(): return lax.ppermute(array, ('row', 'col'), pairs)  27.6 us
    pallas_call x2, Pallas kernels, attention_call(): pl.pallas_call(attend, name='attend', out_shape=(jax.ShapeDtypeStruct((ro...  20.1 us
    ppermute x3, starting transfers between devices, swap(): return lax.ppermute(array, ('row', 'col'), pairs)  18.2 us
    pallas_call x1, Pallas kernels, projection_call(): pl.pallas_call(project, name='project', grid=(width // tile,), out_shape=...  12.4 us
    pallas_call x1, Pallas kernels, fetched(): pl.pallas_call(fetch_near, name='fetch_near', in_specs=[smem, *[hbm] * 12...  7.12 us
    pallas_call x1, Pallas kernels, fetched(): pl.pallas_call(fetch_far, name='fetch_far', in_specs=[smem, *[hbm] * 4, v...  5.73 us
  transfers between devices with their start and end apart: 29, of which 16 were waited for; matrix products, arithmetic and copies ran while one was open for 2% of the time, Pallas kernels for 17%

commit v1 on v0

--- a/solution.py
+++ b/solution.py
@@ -15,6 +15,8 @@
 SMALL = 2 * SHARD - BIG
 SPLIT = BIG - SHARD - BLOCK
 QUADS = 4
+NEAR = 7
+MERGE = 64
 SLOTS = 64
 SCALE = 1.4426950408889634 * HEAD_DIM ** (-0.5)
 STRIDE = {"x": 1, "y": 4, "z": 16}
@@ -68,41 +70,62 @@
         forth(big, b),
         forth(small, s),
     )
-    big = jnp.concatenate([big, others[2], others[4], others[0]], axis=0)
-    small = jnp.concatenate([small, others[3], others[5], others[1]], axis=0)
-    half = big.shape[0] // 2, small.shape[0] // 2
-    b, s = big_axes[1], small_axes[1]
-    big_after, big_before, small_after, small_before = together(
-        back(big, b), forth(big, b), back(small, s), forth(small, s)
-    )
-    big_low, big_high, small_low, small_high = together(
-        back(big_after[: half[0]], b),
-        forth(big_before[half[0] :], b),
-        back(small_after[: half[1]], s),
-        forth(small_before[half[1] :], s),
-    )
-    b, s = big_axes[2], small_axes[2]
-    big_first, big_second, small_first, small_second = together(
-        jnp.concatenate([big, big_after], axis=0),
-        jnp.concatenate([big_before, big_low, big_high], axis=0),
-        jnp.concatenate([small, small_after], axis=0),
-        jnp.concatenate([small_before, small_low, small_high], axis=0),
-    )
-    big_a, big_d, small_a, small_d = together(
-        back(big_first, b), forth(big_second, b), back(small_first, s), forth(small_second, s)
-    )
-    big_b, big_c = back(big_second, b), forth(big_first, b)
-    small_b, small_c = back(small_second, s), forth(small_first, s)
-    big_low, big_high = back(big_a, b), forth(big_d, b)
-    small_low, small_high = back(small_a, s), forth(small_d, s)
-    flat = lambda *parts: [
-        pltpu.with_memory_space_constraint(part.reshape(-1, HEAD_DIM), pltpu.HBM) for part in parts
-    ]
-    return (
-        flat(big_first, big_second, big_a, big_b, big_c, big_d, big_low, big_high),
-        flat(
-            small_first, small_second, small_a, small_b, small_c, small_d, small_low, small_high
-        ),
+    big, small = together(
+        jnp.concatenate([big, others[2], others[4], others[0]], axis=0),
+        jnp.concatenate([small, others[3], others[5], others[1]], axis=0),
+    )
+    parts = {"big": (big, big_axes), "small": (small, small_axes)}
+
+    def each(act):
+        return {part: act(part, parts[part][1][1], parts[part][1][2]) for part in parts}
+
+    def ready(*dicts):
+        flat = together(*(array for one in dicts for array in one.values()))
+        return [dict(zip(parts, flat[2 * k : 2 * k + 2])) for k in range(len(dicts))]
+
+    joined = lambda *dicts: {
+        part: jnp.concatenate([one[part] for one in dicts], axis=0) for part in parts
+    }
+    own = {part: array for part, (array, _) in parts.items()}
+    after = each(lambda part, ring, last: back(own[part], ring))
+    before = each(lambda part, ring, last: forth(own[part], ring))
+    after, before = ready(after, before)
+    half = {part: array.shape[0] // 2 for part, array in own.items()}
+    first, before, low, high = ready(
+        joined(own, after),
+        before,
+        {part: after[part][: half[part]] for part in parts},
+        {part: before[part][half[part] :] for part in parts},
+    )
+    low = each(lambda part, ring, last: back(low[part], ring))
+    high = each(lambda part, ring, last: forth(high[part], ring))
+    first_after = each(lambda part, ring, last: back(first[part], last))
+    before_before = each(lambda part, ring, last: forth(before[part], last))
+    first_before = each(lambda part, ring, last: forth(first[part], last))
+    low, high = ready(low, high)
+    rest, second = joined(low, high), joined(before, low, high)
+    rest_before = each(lambda part, ring, last: forth(rest[part], last))
+    second_after = each(lambda part, ring, last: back(second[part], last))
+    before_far = each(lambda part, ring, last: forth(before_before[part], last))
+    first_far = each(lambda part, ring, last: back(first_after[part], last))
+    rest_far = each(lambda part, ring, last: forth(rest_before[part], last))
+    return tuple(
+        [
+            pltpu.with_memory_space_constraint(piece[part].reshape(-1, HEAD_DIM), pltpu.HBM)
+            for piece in (
+                first,
+                second,
+                first_after,
+                second_after,
+                first_before,
+                before_before,
+                rest_before,
+                first_far,
+                before_far,
+                rest_far,
+            )
+        ]
+        for part in parts
     )
 
 
@@ -134,28 +157,28 @@
     return pl.multiple_of(row, 16)
 
 
-def fetch(first_piece, codes, big, small, kbuf, vbuf, sems):
+def fetch(first_piece, codes, big, small, kbuf, vbuf, sems, entries, left=None):
     count = len(big)
 
     def parts(index):
         code = codes[index]
-        in_big, in_small, within = code & 63, (code >> 6) & 63, code >> 12
-        return in_big, in_small, within, index * BLOCK
-
-    def has(place):
-        piece = (place >> 3) - first_piece
-        return (piece >= 0) & (piece < count)
+        big_piece, big_chunk = code & 15, (code >> 4) & 7
+        small_piece, small_chunk = (code >> 7) & 15, (code >> 11) & 7
+        return big_piece, big_chunk, small_piece, small_chunk, code >> 14, index * BLOCK
+
+    def has(piece):
+        return (piece >= first_piece) & (piece < first_piece + count)
 
     def copy(source, row, rows, target, to, sem):
         return pltpu.make_async_copy(
             source.at[pl.ds(aligned(row), rows), :], target.at[pl.ds(aligned(to), rows), :], sem
         )
 
-    def issue(index, _):
-        in_big, in_small, within, at = parts(index)
+    def issue(index):
+        big_piece, big_chunk, small_piece, small_chunk, within, at = parts(index)
 
         def from_big(piece):
-            row = (in_big & 7) * BIG
+            row = big_chunk * BIG
             copy(big[piece], row + within * BLOCK, BLOCK, kbuf, at, sems.at[0, index]).start()
 
             @pl.when(within == 0)
@@ -167,7 +190,7 @@
                 copy(big[piece], row + SHARD + BLOCK, SPLIT, vbuf, at, sems.at[1, index]).start()
 
         def from_small(piece):
-            row = (in_small & 7) * SMALL
+            row = small_chunk * SMALL
 
             @pl.when(within == 1)
             def _():
@@ -184,49 +207,67 @@
                     sems.at[2, index],
                 ).start()
 
-        pl.when(has(in_big))(lambda: choose((in_big >> 3) - first_piece, count, from_big))
-        pl.when(has(in_small) & (within >= 1))(
-            lambda: choose((in_small >> 3) - first_piece, count, from_small)
+        pl.when(has(big_piece))(lambda: choose(big_piece - first_piece, count, from_big))
+        pl.when(has(small_piece) & (within >= 1))(
+            lambda: choose(small_piece - first_piece, count, from_small)
         )
-        return 0
-
-    def finish(index, _):
-        in_big, in_small, within, at = parts(index)
-
-        @pl.when(has(in_big))
+
+    def finish(index):
+        big_piece, _, small_piece, _, within, at = parts(index)
+
+        @pl.when(has(big_piece))
         def _():
-            copy(big[0], 0, BLOCK, kbuf, at, sems.at[0, index]).wait()
+            copy(big[1], 0, BLOCK, kbuf, at, sems.at[0, index]).wait()
 
             @pl.when(within == 0)
             def _():
-                copy(big[0], 0, BLOCK, vbuf, at, sems.at[1, index]).wait()
+                copy(big[1], 0, BLOCK, vbuf, at, sems.at[1, index]).wait()
 
             @pl.when(within == 1)
             def _():
-                copy(big[0], 0, SPLIT, vbuf, at, sems.at[1, index]).wait()
-
-        @pl.when(has(in_small))
+                copy(big[1], 0, SPLIT, vbuf, at, sems.at[1, index]).wait()
+
+        @pl.when(has(small_piece))
         def _():
             @pl.when(within == 1)
             def _():
-                copy(small[0], 0, BLOCK - SPLIT, vbuf, at + SPLIT, sems.at[2, index]).wait()
+                copy(small[1], 0, BLOCK - SPLIT, vbuf, at + SPLIT, sems.at[2, index]).wait()
 
             @pl.when(within >= 2)
             def _():
-                copy(small[0], 0, BLOCK, vbuf, at, sems.at[2, index]).wait()
-
+                copy(small[1], 0, BLOCK, vbuf, at, sems.at[2, index]).wait()
+
+    number, entry_of = entries
+
+    def begin(k, missing):
+        index = entry_of(k)
+        issue(index)
+        if left is None:
+            return missing
+        big_piece, _, small_piece, _, within, _ = parts(index)
+        left[missing] = index
+        whole = has(big_piece) & (has(small_piece) | (within == 0))
+        return missing + jnp.where(whole, jnp.int32(0), jnp.int32(1))
+
+    missing = lax.fori_loop(0, number, begin, jnp.int32(0))
+    if left is not None:
+        left[SLOTS] = missing
+
+    def end(k, _):
+        finish(entry_of(k))
         return 0
 
-    lax.fori_loop(0, SLOTS, issue, 0)
-    lax.fori_loop(0, SLOTS, finish, 0)
+    lax.fori_loop(0, number, end, 0)
 
 
 def fetch_near(codes, *refs):
-    fetch(0, codes, refs[:6], refs[6:12], *refs[12:])
-
-
-def fetch_far(codes, *refs):
-    fetch(6, codes, refs[:2], refs[2:4], *refs[6:])
+    kbuf, vbuf, left, sems = refs[2 * NEAR :]
+    fetch(0, codes, refs[:NEAR], refs[NEAR : 2 * NEAR], kbuf, vbuf, sems, (SLOTS, lambda k: k), left)
+
+
+def fetch_far(codes, left, *refs):
+    kbuf, vbuf, sems = refs[8:]
+    fetch(NEAR, codes, refs[:3], refs[3:6], kbuf, vbuf, sems, (left[SLOTS], lambda k: left[k]))
 
 
 def fetched(codes, big, small):
@@ -235,21 +276,26 @@
     hbm = pl.BlockSpec(memory_space=pltpu.HBM)
     blocks = jax.ShapeDtypeStruct((SLOTS * BLOCK, HEAD_DIM), jnp.bfloat16)
     common = dict(
-        out_shape=(blocks, blocks),
-        out_specs=(vmem, vmem),
         scratch_shapes=[pltpu.SemaphoreType.DMA((3, SLOTS))],
         compiler_params=pltpu.CompilerParams(vmem_limit_bytes=10 * 2**20),
     )
-    near = pl.pallas_call(
-        fetch_near, name="fetch_near", in_specs=[smem, *[hbm] * 12], **common
-    )(codes, *big[:6], *small[:6])
+    *near, left = pl.pallas_call(
+        fetch_near,
+        name="fetch_near",
+        in_specs=[smem, *[hbm] * (2 * NEAR)],
+        out_shape=(blocks, blocks, jax.ShapeDtypeStruct((2 * SLOTS,), jnp.int32)),
+        out_specs=(vmem, vmem, smem),
+        **common,
+    )(codes, *big[:NEAR], *small[:NEAR])
     return pl.pallas_call(
         fetch_far,
         name="fetch_far",
-        in_specs=[smem, *[hbm] * 4, vmem, vmem],
-        input_output_aliases={5: 0, 6: 1},
+        in_specs=[smem, smem, *[hbm] * 6, vmem, vmem],
+        out_shape=(blocks, blocks),
+        out_specs=(vmem, vmem),
+        input_output_aliases={8: 0, 9: 1},
         **common,
-    )(codes, *big[6:], *small[6:], *near)
+    )(codes, left, *big[NEAR:], *small[NEAR:], *near)
 
 
 def attend(place, starts, q_ref, kbuf, vbuf, o_ref, stat_ref, s_ref, m_ref, acc):
@@ -282,7 +328,7 @@
                 ],
                 axis=0,
             )
-            scores = lax.dot_general(
+            scores = SCALE * lax.dot_general(
                 heads, keys, (((1,), (1,)), ((), ())), preferred_element_type=jnp.float32
             )
             columns = [scores[:, k * BLOCK : (k + 1) * BLOCK] for k in range(count)]
@@ -300,7 +346,7 @@
             top = m_ref[...]
             weights = jnp.concatenate(
                 [
-                    jnp.exp2(s_ref[into, :, k * BLOCK : (k + 1) * BLOCK] * SCALE - top).astype(
+                    jnp.exp2(s_ref[into, :, k * BLOCK : (k + 1) * BLOCK] - top).astype(
                         jnp.bfloat16
                     )
                     for k in range(count)
@@ -319,7 +365,7 @@
 
         each_quad(score)
         m_ref[...] = jnp.broadcast_to(
-            jnp.max(m_ref[...], axis=1, keepdims=True) * SCALE, m_ref.shape
+            jnp.max(m_ref[...], axis=1, keepdims=True), m_ref.shape
         )
         each_quad(weigh)
 
@@ -364,23 +410,28 @@
 def project(o_a, stat_a, o_b, stat_b, w_ref, out_ref, att):
     step, tile = pl.program_id(0), out_ref.shape[1]
 
-    @pl.when(step == 0)
-    def _():
-        top_a, top_b = stat_a[:, :HEAD_DIM], stat_b[:, :HEAD_DIM]
+    def merge(chunk, _):
+        rows = pl.ds(aligned(chunk * MERGE), MERGE)
+        top_a, top_b = stat_a[rows, :HEAD_DIM], stat_b[rows, :HEAD_DIM]
         top = jnp.maximum(top_a, top_b)
         by_a, by_b = jnp.exp2(top_a - top), jnp.exp2(top_b - top)
-        total = stat_a[:, HEAD_DIM:] * by_a + stat_b[:, HEAD_DIM:] * by_b
+        total = stat_a[rows, HEAD_DIM:] * by_a + stat_b[rows, HEAD_DIM:] * by_b
         by_a, by_b = by_a / total, by_b / total
         for head in range(HEADS):
             columns = slice(head * HEAD_DIM, (head + 1) * HEAD_DIM)
-            shape = (att.shape[0], HEAD_DIM)
-            part_a = o_a[:, columns].astype(jnp.float32) * jnp.broadcast_to(
+            shape = (MERGE, HEAD_DIM)
+            part_a = o_a[rows, columns].astype(jnp.float32) * jnp.broadcast_to(
                 by_a[:, head : head + 1], shape
             )
-            part_b = o_b[:, columns].astype(jnp.float32) * jnp.broadcast_to(
+            part_b = o_b[rows, columns].astype(jnp.float32) * jnp.broadcast_to(
                 by_b[:, head : head + 1], shape
             )
-            att[:, columns] = (part_a + part_b).astype(jnp.bfloat16)
+            att[rows, columns] = (part_a + part_b).astype(jnp.bfloat16)
+        return 0
+
+    @pl.when(step == 0)
+    def _():
+        lax.fori_loop(0, att.shape[0] // MERGE, merge, 0)
 
     out_ref[...] = jnp.dot(
         att[...],
@@ -418,7 +469,17 @@
         core == 0, slot_of(theirs, mine, BIG_AXES[0]), slot_of(theirs, mine, BIG_AXES[1])
     )
     in_small = slot_of(theirs, mine, SMALL_AXES[0])
-    return starts.astype(jnp.int32), (in_big | in_small << 6 | within << 12).astype(jnp.int32)
+
+    def piece_and_chunk(place):
+        plane, inner = place >> 4, place & 15
+        halves = 2 * plane + (inner >> 3)
+        thirds = 3 * plane - 2 + ((inner - 4) >> 2) * (inner >> 3)
+        whole = (plane < 2) | (inner < 8)
+        piece = jnp.where(plane < 2, halves, thirds)
+        return piece | jnp.where(whole, inner & 7, inner & 3) << 4
+
+    codes = piece_and_chunk(in_big) | piece_and_chunk(in_small) << 7 | within << 14
+    return starts.astype(jnp.int32), codes.astype(jnp.int32)
 
 
 def local(queries, keys, values, row_ptr, col_blocks, w_out):

time: 146 us -> 178 us (1.22)
  waiting for transfers between devices: 49.5 us -> 76.5 us
  starting transfers between devices: 45.8 us -> 47.9 us
  local copies, waits for them, and re-layouts: 3.11 us -> 5.05 us
    ppermute x26 -> x30, waiting for transfers between devices: 49.5 us -> 76.5 us  [send(): return lax.ppermute(array, ('row', 'col'), pairs)]
    ppermute x26 -> x30, starting transfers between devices: 27.6 us -> 32.1 us  [send(): return lax.ppermute(array, ('row', 'col'), pairs)]
    ppermute x3, starting transfers between devices: 18.2 us -> 15.8 us  [swap(): return lax.ppermute(array, ('row', 'col'), pairs)]
    unnamed x35 -> x38, local copies, waits for them, and re-layouts: 1.06 us -> 3.12 us
  transfers between devices with their start and end apart: 29 -> 33, of which waited for: 16 -> 14; matrix products, arithmetic and copies ran while one was open for 2% -> 2% of each run, Pallas kernels for 17% -> 14%
where the time goes in v1:
time: 178 us
  waiting for transfers between devices  76.5 us (43%)
  starting transfers between devices  47.9 us (27%)
  Pallas kernels  45.3 us (25%)
  local copies, waits for them, and re-layouts  5.05 us (3%)
  other arithmetic  2.36 us (1%)
    ppermute x30, waiting for transfers between devices, send(): return lax.ppermute(array, ('row', 'col'), pairs)  76.5 us
    ppermute x30, starting transfers between devices, send(): return lax.ppermute(array, ('row', 'col'), pairs)  32.1 us
    pallas_call x2, Pallas kernels, attention_call(): pl.pallas_call(attend, name='attend', out_shape=(jax.ShapeDtypeStruct((ro...  20 us
    ppermute x3, starting transfers between devices, swap(): return lax.ppermute(array, ('row', 'col'), pairs)  15.8 us
    pallas_call x1, Pallas kernels, projection_call(): pl.pallas_call(project, name='project', grid=(width // tile,), out_shape=...  13 us
    pallas_call x1, Pallas kernels, fetched(): pl.pallas_call(fetch_near, name='fetch_near', in_specs=[smem, *[hbm] * (2...  8.7 us
    pallas_call x1, Pallas kernels, fetched(): pl.pallas_call(fetch_far, name='fetch_far', in_specs=[smem, smem, *[hbm]...  3.61 us
  transfers between devices with their start and end apart: 33, of which 14 were waited for; matrix products, arithmetic and copies ran while one was open for 2% of the time, Pallas kernels for 14%

profile of v1, /device:TPU:1, one launch (start us, length us, event | category | flops | bytes accessed | tf_op | source)
XLA Modules:
  0.0 177.6 jit_solution(1194929909446200956)
XLA Ops:
  0.0 0.9 fusion
  0.9 3.6 %collective-permute-start = (bf16[86,8,128]{2,1,0:T(8,128)(2,1)S(1)}, bf16[86,8,128]{2,1,0:T(8,128)(2,1)S(1)}, u32[]{:S(2)}, u32[]{:S(2)}) collective-permute-start(bf16[86,8,128]{2,1,0:T(8,128)(2,1)S(1)} %fusion), channel_id=1, source_target_pairs={{0,16},{1,5},{2,18},{3,7},{4,20},{5,1},{6,22},{7,3},{8,24},{9,13},... | collective-permute-start | bytes 528392 | tf_op jit(solution)/shard_map/ppermute | solution.py:34
  4.6 0.9 collective-permute-start.2
  5.4 0.6 collective-permute-start.4
  6.1 0.9 slice_bitcast_fusion
  7.0 3.6 %collective-permute-start.1 = (bf16[42,8,128]{2,1,0:T(8,128)(2,1)S(1)}, bf16[42,8,128]{2,1,0:T(8,128)(2,1)S(1)}, u32[]{:S(2)}, u32[]{:S(2)}) collective-permute-start(bf16[42,8,128]{2,1,0:T(8,128)(2,1)S(1)} %slice_bitcast_fusion), channel_id=1, source_target_pairs={{0,64},{1,65},{2,66},{3,67},{4,68},{5,69},{6,70},{7,71},{8,72},{9,... | collective-permute-start | bytes 258056 | tf_op jit(solution)/shard_map/ppermute | solution.py:34
  10.5 0.4 collective-permute-start.3
  11.0 1.4 collective-permute-done.1
  12.4 1.3 collective-permute-start.5
  13.7 0.6 collective-permute-done.3
  14.4 3.1 %collective-permute-done.5 = bf16[42,8,128]{2,1,0:T(8,128)(2,1)S(1)} collective-permute-done((bf16[42,8,128]{2,1,0:T(8,128)(2,1)S(1)}, bf16[42,8,128]{2,1,0:T(8,128)(2,1)S(1)}, u32[]{:S(2)}, u32[]{:S(2)}) %collective-permute-start.5) | collective-permute-done | bytes 86048 | tf_op jit(solution)/shard_map/ppermute | solution.py:34
  17.6 0.1 pad_maximum_fusion.1
  17.7 2.8 %collective-permute-start.6 = (bf16[344,8,128]{2,1,0:T(8,128)(2,1)S(1)}, bf16[344,8,128]{2,1,0:T(8,128)(2,1)S(1)}, u32[]{:S(2)}, u32[]{:S(2)}) collective-permute-start(bf16[344,8,128]{2,1,0:T(8,128)(2,1)S(1)} %pad_maximum_fusion.1), channel_id=1, source_target_pairs={{0,96},{1,25},{2,98},{3,27},{4,100},{5,29},{6,102},{7,31},{8,104},... | collective-permute-start | bytes 2113544 | tf_op jit(solution)/shard_map/ppermute | solution.py:34
  20.5 2.1 %collective-permute-start.7 = (bf16[168,8,128]{2,1,0:T(8,128)(2,1)S(1)}, bf16[168,8,128]{2,1,0:T(8,128)(2,1)S(1)}, u32[]{:S(2)}, u32[]{:S(2)}) collective-permute-start(bf16[168,8,128]{2,1,0:T(8,128)(2,1)S(1)} %pad_maximum_fusion.4), channel_id=1, source_target_pairs={{0,6},{1,7},{2,0},{3,1},{4,2},{5,3},{6,4},{7,5},{8,14},{9,15},{10,... | collective-permute-start | bytes 1032200 | tf_op jit(solution)/shard_map/ppermute | solution.py:34
  22.6 0.0 collective-permute-start.9
  22.6 4.6 %collective-permute-done.7 = bf16[168,8,128]{2,1,0:T(8,128)(2,1)S(1)} collective-permute-done((bf16[168,8,128]{2,1,0:T(8,128)(2,1)S(1)}, bf16[168,8,128]{2,1,0:T(8,128)(2,1)S(1)}, u32[]{:S(2)}, u32[]{:S(2)}) %collective-permute-start.7) | collective-permute-done | bytes 344096 | tf_op jit(solution)/shard_map/ppermute | solution.py:34
  27.2 3.0 %collective-permute-done.9 = bf16[168,8,128]{2,1,0:T(8,128)(2,1)S(1)} collective-permute-done((bf16[168,8,128]{2,1,0:T(8,128)(2,1)S(1)}, bf16[168,8,128]{2,1,0:T(8,128)(2,1)S(1)}, u32[]{:S(2)}, u32[]{:S(2)}) %collective-permute-start.9) | collective-permute-done | bytes 344096 | tf_op jit(solution)/shard_map/ppermute | solution.py:34
  30.2 0.0 collective-permute-done.6
  30.2 1.8 %collective-permute-done.8 = bf16[344,8,128]{2,1,0:T(8,128)(2,1)S(1)} collective-permute-done((bf16[344,8,128]{2,1,0:T(8,128)(2,1)S(1)}, bf16[344,8,128]{2,1,0:T(8,128)(2,1)S(1)}, u32[]{:S(2)}, u32[]{:S(2)}) %collective-permute-start.8) | collective-permute-done | bytes 704544 | tf_op jit(solution)/shard_map/ppermute | solution.py:34
  32.0 0.1 pad_maximum_fusion
  32.1 0.0 copy-start.1
  32.1 0.1 pad_maximum_fusion.3
  32.3 0.3 collective-permute-start.22
  32.6 1.9 %collective-permute-start.11 = (bf16[84,8,128]{2,1,0:T(8,128)(2,1)S(1)}, bf16[84,8,128]{2,1,0:T(8,128)(2,1)S(1)}, u32[]{:S(2)}, u32[]{:S(2)}) collective-permute-start(bf16[84,8,128]{2,1,0:T(8,128)(2,1)S(1)} %slice.29), channel_id=1, source_target_pairs={{0,6},{1,7},{2,0},{3,1},{4,2},{5,3},{6,4},{7,5},{8,14},{9,15},{10,... | collective-permute-start | bytes 516104 | tf_op jit(solution)/shard_map/ppermute | solution.py:34
  34.5 2.6 %collective-permute-start.10 = (bf16[172,8,128]{2,1,0:T(8,128)(2,1)S(1)}, bf16[172,8,128]{2,1,0:T(8,128)(2,1)S(1)}, u32[]{:S(2)}, u32[]{:S(2)}) collective-permute-start(bf16[172,8,128]{2,1,0:T(8,128)(2,1)S(1)} %slice.28), channel_id=1, source_target_pairs={{0,96},{1,25},{2,98},{3,27},{4,100},{5,29},{6,102},{7,31},{8,104},... | collective-permute-start | bytes 1056776 | tf_op jit(solution)/shard_map/ppermute | solution.py:34
  37.1 2.7 %collective-permute-start.19 = (bf16[336,8,128]{2,1,0:T(8,128)(2,1)S(1)}, bf16[336,8,128]{2,1,0:T(8,128)(2,1)}, u32[]{:S(2)}, u32[]{:S(2)}) collective-permute-start(bf16[336,8,128]{2,1,0:T(8,128)(2,1)S(1)} %pad_maximum_fusion.3), channel_id=1, source_target_pairs={{0,24},{1,25},{2,26},{3,27},{4,28},{5,29},{6,30},{7,31},{8,0},{9,1... | collective-permute-start | bytes 2064392 | tf_op jit(solution)/shard_map/ppermute | solution.py:34
  39.8 0.2 collective-permute-done.13
  40.0 0.5 collective-permute-start.21
  40.5 1.0 collective-permute-start.14
  41.6 1.1 collective-permute-start.28
  42.7 5.3 %collective-permute-done.12 = bf16[172,8,128]{2,1,0:T(8,128)(2,1)S(1)} collective-permute-done((bf16[172,8,128]{2,1,0:T(8,128)(2,1)S(1)}, bf16[172,8,128]{2,1,0:T(8,128)(2,1)S(1)}, u32[]{:S(2)}, u32[]{:S(2)}) %collective-permute-start.12) | collective-permute-done | bytes 352288 | tf_op jit(solution)/shard_map/ppermute | solution.py:34
  48.1 0.1 collective-permute-start.23
  48.2 0.0 copy-start
  48.3 19.1 %collective-permute-done.28 = bf16[168,8,128]{2,1,0:T(8,128)(2,1)S(1)} collective-permute-done((bf16[168,8,128]{2,1,0:T(8,128)(2,1)S(1)}, bf16[168,8,128]{2,1,0:T(8,128)(2,1)S(1)}, u32[]{:S(2)}, u32[]{:S(2)}) %collective-permute-start.28) | collective-permute-done | bytes 344096 | tf_op jit(solution)/shard_map/ppermute | solution.py:34
  67.4 1.9 %collective-permute-start.17 = (bf16[344,8,128]{2,1,0:T(8,128)(2,1)S(1)}, bf16[344,8,128]{2,1,0:T(8,128)(2,1)}, u32[]{:S(2)}, u32[]{:S(2)}) collective-permute-start(bf16[344,8,128]{2,1,0:T(8,128)(2,1)S(1)} %collective-permute-done.8), channel_id=1, source_target_pairs={{0,2},{1,33},{2,4},{3,35},{4,6},{5,37},{6,0},{7,39},{8,10},{9,41},... | collective-permute-start | bytes 2113544 | tf_op jit(solution)/shard_map/ppermute | solution.py:34
  69.4 1.6 collective-permute-start.15
  71.0 3.8 %collective-permute-done.23 = bf16[168,8,128]{2,1,0:T(8,128)(2,1)S(1)} collective-permute-done((bf16[168,8,128]{2,1,0:T(8,128)(2,1)S(1)}, bf16[168,8,128]{2,1,0:T(8,128)(2,1)S(1)}, u32[]{:S(2)}, u32[]{:S(2)}) %collective-permute-start.23) | collective-permute-done | bytes 344096 | tf_op jit(solution)/shard_map/ppermute | solution.py:34
  74.8 0.1 pad_maximum_fusion.2
  74.9 19.9 %collective-permute-done.17 = bf16[344,8,128]{2,1,0:T(8,128)(2,1)} collective-permute-done((bf16[344,8,128]{2,1,0:T(8,128)(2,1)S(1)}, bf16[344,8,128]{2,1,0:T(8,128)(2,1)}, u32[]{:S(2)}, u32[]{:S(2)}) %collective-permute-start.17) | collective-permute-done | bytes 704544 | tf_op jit(solution)/shard_map/ppermute | solution.py:34
  94.8 2.7 %collective-permute-start.24 = (bf16[688,8,128]{2,1,0:T(8,128)(2,1)}, bf16[688,8,128]{2,1,0:T(8,128)(2,1)}, u32[]{:S(2)}, u32[]{:S(2)}) collective-permute-start(bf16[688,8,128]{2,1,0:T(8,128)(2,1)} %collective-permute-done.14), channel_id=1, source_target_pairs={{0,6},{1,97},{2,0},{3,99},{4,2},{5,101},{6,4},{7,103},{8,14},{9,10... | collective-permute-start | bytes 4227080 | tf_op jit(solution)/shard_map/ppermute | solution.py:34
  97.5 0.9 copy-done.8
  98.4 6.5 %collective-permute-done.29 = bf16[168,8,128]{2,1,0:T(8,128)(2,1)} collective-permute-done((bf16[168,8,128]{2,1,0:T(8,128)(2,1)S(1)}, bf16[168,8,128]{2,1,0:T(8,128)(2,1)}, u32[]{:S(2)}, u32[]{:S(2)}) %collective-permute-start.29) | collective-permute-done | bytes 344096 | tf_op jit(solution)/shard_map/ppermute | solution.py:34
  104.9 7.7 %collective-permute-start.30 = (bf16[512,1024]{1,0:T(8,128)(2,1)S(1)}, bf16[512,1024]{1,0:T(8,128)(2,1)S(1)}, u32[]{:S(2)}, u32[]{:S(2)}) collective-permute-start(bf16[512,1024]{1,0:T(8,128)(2,1)S(1)} %copy-done), channel_id=1, source_target_pairs={{0,1},{1,0},{2,3},{3,2},{4,5},{5,4},{6,7},{7,6},{8,9},{9,8},{10,11... | collective-permute-start | bytes 3145736 | tf_op jit(solution)/shard_map/ppermute | solution.py:39
  112.6 0.3 collective-permute-start.26
  112.9 0.1 collective-permute-start.27
  113.0 0.7 copy-done.5
  113.7 0.5 copy-done.6
  114.2 0.8 dynamic_slice.7
  114.9 0.1 reshape.86
  115.1 0.8 subtract_shift-right-arithmetic_fusion.starts
  115.9 0.2 shift-right-arithmetic_reduce_fusion
  116.1 0.0 slice-start
  116.1 0.0 slice-start.1
  116.1 8.7 %fetch_near.1 = (bf16[8192,128]{1,0:T(8,128)(2,1)S(1)}, bf16[8192,128]{1,0:T(8,128)(2,1)S(1)}, s32[128]{0:T(128)S(1)}) custom-call(s32[64]{0:T(128)S(1)} %fusion.5.codes, bf16[5504,128]{1,0:T(8,128)(2,1)} %bitcast.28, bf16[5504,128]{1,0:T(8,128)(2,1)} %bitcast.29, bf16[5504,128]{1,0:T(8,128)(2,1)} %bitcast.5.refs_2_, bf16[5504,128]{1,0:T(8,128)(2,1)} %bitcast.33, ...), custom_call_target="tpu_custom_call" | custom-call | tf_op jit(solution)/shard_map/fetch_near/pallas_call | solution.py:282
  124.8 4.8 %collective-permute-done.27 = bf16[336,8,128]{2,1,0:T(8,128)(2,1)S(1)} collective-permute-done((bf16[336,8,128]{2,1,0:T(8,128)(2,1)}, bf16[336,8,128]{2,1,0:T(8,128)(2,1)S(1)}, u32[]{:S(2)}, u32[]{:S(2)}) %collective-permute-start.27) | collective-permute-done | bytes 688160 | tf_op jit(solution)/shard_map/ppermute | solution.py:34
  129.6 2.2 %collective-permute-done.26 = bf16[344,8,128]{2,1,0:T(8,128)(2,1)S(1)} collective-permute-done((bf16[344,8,128]{2,1,0:T(8,128)(2,1)}, bf16[344,8,128]{2,1,0:T(8,128)(2,1)S(1)}, u32[]{:S(2)}, u32[]{:S(2)}) %collective-permute-start.26) | collective-permute-done | bytes 704544 | tf_op jit(solution)/shard_map/ppermute | solution.py:34
  131.8 0.8 copy-done.7
  132.7 3.6 %fetch_far.1 = (bf16[8192,128]{1,0:T(8,128)(2,1)S(1)}, bf16[8192,128]{1,0:T(8,128)(2,1)S(1)}) custom-call(s32[64]{0:T(128)S(1)} %fusion.5.codes, s32[128]{0:T(128)S(1)} %get-tuple-element.64.left, bf16[5504,128]{1,0:T(8,128)(2,1)} %bitcast.17.refs_0_, bf16[2752,128]{1,0:T(8,128)(2,1)} %bitcast.18.refs_1_, ...), custom_call_target="tpu_custom_call", output_to_operand_aliasing={{0}: (8, {}), {1}: (9, {})} | custom-call | tf_op jit(solution)/shard_map/fetch_far/pallas_call | solution.py:290
  136.3 0.0 slice-start.3
  136.3 7.3 %attend.3 = (bf16[512,1024]{1,0:T(8,128)(2,1)S(1)}, f32[512,256]{1,0:T(8,128)S(1)}) custom-call(s32[1]{0:T(128)} %bitcast.23.place, s32[9]{0:T(128)S(1)} %subtract_shift-right-arithmetic_fusion.starts, bf16[512,1024]{1,0:T(8,128)(2,1)S(1)} %collective-permute-done.30.q_ref, bf16[8192,128]{1,0:T(8,128)(2,1)S(1)} %get-tuple-element.67.kbuf, ...), custom_call_target="tpu_custom_call" | custom-call | tf_op jit(solution)/shard_map/attend/pallas_call | solution.py:392
  143.7 8.1 %collective-permute-start.31 = (bf16[512,1024]{1,0:T(8,128)(2,1)S(1)}, bf16[512,1024]{1,0:T(8,128)(2,1)S(1)}, u32[]{:S(2)}, u32[]{:S(2)}) collective-permute-start(bf16[512,1024]{1,0:T(8,128)(2,1)S(1)} %get-tuple-element.71), channel_id=1, source_target_pairs={{0,1},{1,0},{2,3},{3,2},{4,5},{5,4},{6,7},{7,6},{8,9},{9,8},{10,11... | collective-permute-start | bytes 3145736 | tf_op jit(solution)/shard_map/ppermute | solution.py:39
  151.7 0.1 collective-permute-start.32
  151.8 12.7 %attend.2 = (bf16[512,1024]{1,0:T(8,128)(2,1)S(1)}, f32[512,256]{1,0:T(8,128)S(1)}) custom-call(s32[1]{0:T(128)} %bitcast.place, s32[9]{0:T(128)S(1)} %subtract_shift-right-arithmetic_fusion.starts, bf16[512,1024]{1,0:T(8,128)(2,1)S(1)} %copy-done, bf16[8192,128]{1,0:T(8,128)(2,1)S(1)} %get-tuple-element.67.kbuf, bf16[8192,128]{1,0:T(8,128)(2,1)S(1)} %get-tuple-element.68.vbuf), custom_call_target="tpu_custom_call" | custom-call | tf_op jit(solution)/shard_map/attend/pallas_call | solution.py:392
  164.6 13.0 %project.1 = bf16[512,8192]{1,0:T(8,128)(2,1)} custom-call(bf16[512,1024]{1,0:T(8,128)(2,1)S(1)} %get-tuple-element.69.o_a, f32[512,256]{1,0:T(8,128)S(1)} %get-tuple-element.70.stat_a, bf16[512,1024]{1,0:T(8,128)(2,1)S(1)} %collective-permute-done.31.o_b, f32[512,256]{1,0:T(8,128)S(1)} %collective-permute-done.32.stat_b, bf16[1024,8192]{1,0:T(8,128)(2,1)S(1)} %bitcast.27), custom_call_target="tpu_custom_call" | custom-call | tf_op jit(solution)/shard_map/project/pallas_call | solution.py:447
  (65 shorter events, 0.5 us)
Async XLA Ops:
  0.9 16.6 %collective-permute-start = (bf16[86,8,128]{2,1,0:T(8,128)(2,1)S(1)}, bf16[86,8,128]{2,1,0:T(8,128)(2,1)S(1)}, u32[]{:S(2)}, u32[]{:S(2)}) collective-permute-start(bf16[86,8,128]{2,1,0:T(8,128)(2,1)S(1)} %fusion), channel_id=1, source_target_pairs={{0,16},{1,5},{2,18},{3,7},{4,20},{5,1},{6,22},{7,3},{8,24},{9,13},... | collective-permute-start | bytes 528392 | tf_op jit(solution)/shard_map/ppermute | solution.py:34
  4.6 12.9 %collective-permute-start.2 = (bf16[86,8,128]{2,1,0:T(8,128)(2,1)S(1)}, bf16[86,8,128]{2,1,0:T(8,128)(2,1)S(1)}, u32[]{:S(2)}, u32[]{:S(2)}) collective-permute-start(bf16[86,8,128]{2,1,0:T(8,128)(2,1)S(1)} %fusion), channel_id=1, source_target_pairs={{0,24},{1,7},{2,26},{3,1},{4,28},{5,3},{6,30},{7,5},{8,0},{9,15},{... | collective-permute-start | bytes 528392 | tf_op jit(solution)/shard_map/ppermute | solution.py:34
  5.4 12.1 %collective-permute-start.4 = (bf16[86,8,128]{2,1,0:T(8,128)(2,1)S(1)}, bf16[86,8,128]{2,1,0:T(8,128)(2,1)S(1)}, u32[]{:S(2)}, u32[]{:S(2)}) collective-permute-start(bf16[86,8,128]{2,1,0:T(8,128)(2,1)S(1)} %fusion), channel_id=1, source_target_pairs={{0,8},{1,3},{2,10},{3,5},{4,12},{5,7},{6,14},{7,1},{8,16},{9,11},{... | collective-permute-start | bytes 528392 | tf_op jit(solution)/shard_map/ppermute | solution.py:34
  7.0 5.5 %collective-permute-start.1 = (bf16[42,8,128]{2,1,0:T(8,128)(2,1)S(1)}, bf16[42,8,128]{2,1,0:T(8,128)(2,1)S(1)}, u32[]{:S(2)}, u32[]{:S(2)}) collective-permute-start(bf16[42,8,128]{2,1,0:T(8,128)(2,1)S(1)} %slice_bitcast_fusion), channel_id=1, source_target_pairs={{0,64},{1,65},{2,66},{3,67},{4,68},{5,69},{6,70},{7,71},{8,72},{9,... | collective-permute-start | bytes 258056 | tf_op jit(solution)/shard_map/ppermute | solution.py:34
  10.5 3.8 %collective-permute-start.3 = (bf16[42,8,128]{2,1,0:T(8,128)(2,1)S(1)}, bf16[42,8,128]{2,1,0:T(8,128)(2,1)S(1)}, u32[]{:S(2)}, u32[]{:S(2)}) collective-permute-start(bf16[42,8,128]{2,1,0:T(8,128)(2,1)S(1)} %slice_bitcast_fusion), channel_id=1, source_target_pairs={{0,96},{1,97},{2,98},{3,99},{4,100},{5,101},{6,102},{7,103},{8,104... | collective-permute-start | bytes 258056 | tf_op jit(solution)/shard_map/ppermute | solution.py:34
  12.4 5.1 %collective-permute-start.5 = (bf16[42,8,128]{2,1,0:T(8,128)(2,1)S(1)}, bf16[42,8,128]{2,1,0:T(8,128)(2,1)S(1)}, u32[]{:S(2)}, u32[]{:S(2)}) collective-permute-start(bf16[42,8,128]{2,1,0:T(8,128)(2,1)S(1)} %slice_bitcast_fusion), channel_id=1, source_target_pairs={{0,32},{1,33},{2,34},{3,35},{4,36},{5,37},{6,38},{7,39},{8,40},{9,... | collective-permute-start | bytes 258056 | tf_op jit(solution)/shard_map/ppermute | solution.py:34
  17.7 12.5 %collective-permute-start.6 = (bf16[344,8,128]{2,1,0:T(8,128)(2,1)S(1)}, bf16[344,8,128]{2,1,0:T(8,128)(2,1)S(1)}, u32[]{:S(2)}, u32[]{:S(2)}) collective-permute-start(bf16[344,8,128]{2,1,0:T(8,128)(2,1)S(1)} %pad_maximum_fusion.1), channel_id=1, source_target_pairs={{0,96},{1,25},{2,98},{3,27},{4,100},{5,29},{6,102},{7,31},{8,104},... | collective-permute-start | bytes 2113544 | tf_op jit(solution)/shard_map/ppermute | solution.py:34
  20.5 11.5 %collective-permute-start.8 = (bf16[344,8,128]{2,1,0:T(8,128)(2,1)S(1)}, bf16[344,8,128]{2,1,0:T(8,128)(2,1)S(1)}, u32[]{:S(2)}, u32[]{:S(2)}) collective-permute-start(bf16[344,8,128]{2,1,0:T(8,128)(2,1)S(1)} %pad_maximum_fusion.1), channel_id=1, source_target_pairs={{0,32},{1,9},{2,34},{3,11},{4,36},{5,13},{6,38},{7,15},{8,40},{9,1... | collective-permute-start | bytes 2113544 | tf_op jit(solution)/shard_map/ppermute | solution.py:34
  20.5 6.7 %collective-permute-start.7 = (bf16[168,8,128]{2,1,0:T(8,128)(2,1)S(1)}, bf16[168,8,128]{2,1,0:T(8,128)(2,1)S(1)}, u32[]{:S(2)}, u32[]{:S(2)}) collective-permute-start(bf16[168,8,128]{2,1,0:T(8,128)(2,1)S(1)} %pad_maximum_fusion.4), channel_id=1, source_target_pairs={{0,6},{1,7},{2,0},{3,1},{4,2},{5,3},{6,4},{7,5},{8,14},{9,15},{10,... | collective-permute-start | bytes 1032200 | tf_op jit(solution)/shard_map/ppermute | solution.py:34
  22.6 7.6 %collective-permute-start.9 = (bf16[168,8,128]{2,1,0:T(8,128)(2,1)S(1)}, bf16[168,8,128]{2,1,0:T(8,128)(2,1)S(1)}, u32[]{:S(2)}, u32[]{:S(2)}) collective-permute-start(bf16[168,8,128]{2,1,0:T(8,128)(2,1)S(1)} %pad_maximum_fusion.4), channel_id=1, source_target_pairs={{0,2},{1,3},{2,4},{3,5},{4,6},{5,7},{6,0},{7,1},{8,10},{9,11},{10,... | collective-permute-start | bytes 1032200 | tf_op jit(solution)/shard_map/ppermute | solution.py:34
  32.1 35.3 %copy-start.1 = (bf16[688,8,128]{2,1,0:T(8,128)(2,1)}, bf16[688,8,128]{2,1,0:T(8,128)(2,1)S(1)}, u32[]{:S(2)}) copy-start(bf16[688,8,128]{2,1,0:T(8,128)(2,1)S(1)} %pad_maximum_fusion) | copy-start | bytes 4227076
  32.2 9.4 %copy-start.3 = (bf16[336,8,128]{2,1,0:T(8,128)(2,1)}, bf16[336,8,128]{2,1,0:T(8,128)(2,1)S(1)}, u32[]{:S(2)}) copy-start(bf16[336,8,128]{2,1,0:T(8,128)(2,1)S(1)} %pad_maximum_fusion.3) | copy-start | bytes 2064388
  32.3 8.2 %collective-permute-start.22 = (bf16[168,8,128]{2,1,0:T(8,128)(2,1)S(1)}, bf16[168,8,128]{2,1,0:T(8,128)(2,1)S(1)}, u32[]{:S(2)}, u32[]{:S(2)}) collective-permute-start(bf16[168,8,128]{2,1,0:T(8,128)(2,1)S(1)} %collective-permute-done.9), channel_id=1, source_target_pairs={{0,8},{1,9},{2,10},{3,11},{4,12},{5,13},{6,14},{7,15},{8,16},{9,17... | collective-permute-start | bytes 1032200 | tf_op jit(solution)/shard_map/ppermute | solution.py:34
  32.6 4.5 %collective-permute-start.11 = (bf16[84,8,128]{2,1,0:T(8,128)(2,1)S(1)}, bf16[84,8,128]{2,1,0:T(8,128)(2,1)S(1)}, u32[]{:S(2)}, u32[]{:S(2)}) collective-permute-start(bf16[84,8,128]{2,1,0:T(8,128)(2,1)S(1)} %slice.29), channel_id=1, source_target_pairs={{0,6},{1,7},{2,0},{3,1},{4,2},{5,3},{6,4},{7,5},{8,14},{9,15},{10,... | collective-permute-start | bytes 516104 | tf_op jit(solution)/shard_map/ppermute | solution.py:34
  34.5 5.5 %collective-permute-start.13 = (bf16[84,8,128]{2,1,0:T(8,128)(2,1)S(1)}, bf16[84,8,128]{2,1,0:T(8,128)(2,1)S(1)}, u32[]{:S(2)}, u32[]{:S(2)}) collective-permute-start(bf16[84,8,128]{2,1,0:T(8,128)(2,1)S(1)} %slice.31), channel_id=1, source_target_pairs={{0,2},{1,3},{2,4},{3,5},{4,6},{5,7},{6,0},{7,1},{8,10},{9,11},{10,... | collective-permute-start | bytes 516104 | tf_op jit(solution)/shard_map/ppermute | solution.py:34
  34.5 7.1 %collective-permute-start.10 = (bf16[172,8,128]{2,1,0:T(8,128)(2,1)S(1)}, bf16[172,8,128]{2,1,0:T(8,128)(2,1)S(1)}, u32[]{:S(2)}, u32[]{:S(2)}) collective-permute-start(bf16[172,8,128]{2,1,0:T(8,128)(2,1)S(1)} %slice.28), channel_id=1, source_target_pairs={{0,96},{1,25},{2,98},{3,27},{4,100},{5,29},{6,102},{7,31},{8,104},... | collective-permute-start | bytes 1056776 | tf_op jit(solution)/shard_map/ppermute | solution.py:34
  37.1 10.9 %collective-permute-start.12 = (bf16[172,8,128]{2,1,0:T(8,128)(2,1)S(1)}, bf16[172,8,128]{2,1,0:T(8,128)(2,1)S(1)}, u32[]{:S(2)}, u32[]{:S(2)}) collective-permute-start(bf16[172,8,128]{2,1,0:T(8,128)(2,1)S(1)} %slice.30), channel_id=1, source_target_pairs={{0,32},{1,9},{2,34},{3,11},{4,36},{5,13},{6,38},{7,15},{8,40},{9,1... | collective-permute-start | bytes 1056776 | tf_op jit(solution)/shard_map/ppermute | solution.py:34
  37.1 30.3 %collective-permute-start.19 = (bf16[336,8,128]{2,1,0:T(8,128)(2,1)S(1)}, bf16[336,8,128]{2,1,0:T(8,128)(2,1)}, u32[]{:S(2)}, u32[]{:S(2)}) collective-permute-start(bf16[336,8,128]{2,1,0:T(8,128)(2,1)S(1)} %pad_maximum_fusion.3), channel_id=1, source_target_pairs={{0,24},{1,25},{2,26},{3,27},{4,28},{5,29},{6,30},{7,31},{8,0},{9,1... | collective-permute-start | bytes 2064392 | tf_op jit(solution)/shard_map/ppermute | solution.py:34
  40.0 29.4 %collective-permute-start.21 = (bf16[336,8,128]{2,1,0:T(8,128)(2,1)S(1)}, bf16[336,8,128]{2,1,0:T(8,128)(2,1)}, u32[]{:S(2)}, u32[]{:S(2)}) collective-permute-start(bf16[336,8,128]{2,1,0:T(8,128)(2,1)S(1)} %pad_maximum_fusion.3), channel_id=1, source_target_pairs={{0,8},{1,9},{2,10},{3,11},{4,12},{5,13},{6,14},{7,15},{8,16},{9,17... | collective-permute-start | bytes 2064392 | tf_op jit(solution)/shard_map/ppermute | solution.py:34
  40.5 7.7 %copy-start.10 = (bf16[168,8,128]{2,1,0:T(8,128)(2,1)}, bf16[168,8,128]{2,1,0:T(8,128)(2,1)S(1)}, u32[]{:S(2)}) copy-start(bf16[168,8,128]{2,1,0:T(8,128)(2,1)S(1)} %collective-permute-done.22) | copy-start | bytes 1032196
  40.5 54.3 %collective-permute-start.14 = (bf16[688,8,128]{2,1,0:T(8,128)(2,1)S(1)}, bf16[688,8,128]{2,1,0:T(8,128)(2,1)}, u32[]{:S(2)}, u32[]{:S(2)}) collective-permute-start(bf16[688,8,128]{2,1,0:T(8,128)(2,1)S(1)} %pad_maximum_fusion), channel_id=1, source_target_pairs={{0,6},{1,97},{2,0},{3,99},{4,2},{5,101},{6,4},{7,103},{8,14},{9,10... | collective-permute-start | bytes 4227080 | tf_op jit(solution)/shard_map/ppermute | solution.py:34
  41.6 25.8 %collective-permute-start.28 = (bf16[168,8,128]{2,1,0:T(8,128)(2,1)S(1)}, bf16[168,8,128]{2,1,0:T(8,128)(2,1)S(1)}, u32[]{:S(2)}, u32[]{:S(2)}) collective-permute-start(bf16[168,8,128]{2,1,0:T(8,128)(2,1)S(1)} %collective-permute-done.22), channel_id=1, source_target_pairs={{0,8},{1,9},{2,10},{3,11},{4,12},{5,13},{6,14},{7,15},{8,16},{9,17... | collective-permute-start | bytes 1032200 | tf_op jit(solution)/shard_map/ppermute | solution.py:34
  48.1 26.7 %collective-permute-start.23 = (bf16[168,8,128]{2,1,0:T(8,128)(2,1)S(1)}, bf16[168,8,128]{2,1,0:T(8,128)(2,1)S(1)}, u32[]{:S(2)}, u32[]{:S(2)}) collective-permute-start(bf16[168,8,128]{2,1,0:T(8,128)(2,1)S(1)} %pad_maximum_fusion.5), channel_id=1, source_target_pairs={{0,8},{1,9},{2,10},{3,11},{4,12},{5,13},{6,14},{7,15},{8,16},{9,17... | collective-permute-start | bytes 1032200 | tf_op jit(solution)/shard_map/ppermute | solution.py:34
  48.2 56.7 %copy-start = (bf16[512,1024]{1,0:T(8,128)(2,1)S(1)}, bf16[512,1024]{1,0:T(8,128)(2,1)}, u32[]{:S(2)}) copy-start(bf16[512,1024]{1,0:T(8,128)(2,1)} %q_ref.1) | copy-start | bytes 3145732
  48.3 64.3 %copy-start.2 = (bf16[688,8,128]{2,1,0:T(8,128)(2,1)}, bf16[688,8,128]{2,1,0:T(8,128)(2,1)S(1)}, u32[]{:S(2)}) copy-start(bf16[688,8,128]{2,1,0:T(8,128)(2,1)S(1)} %constant_dynamic-update-slice_fusion) | copy-start | bytes 4227076
  67.4 7.4 %copy-start.11 = (bf16[168,8,128]{2,1,0:T(8,128)(2,1)}, bf16[168,8,128]{2,1,0:T(8,128)(2,1)S(1)}, u32[]{:S(2)}) copy-start(bf16[168,8,128]{2,1,0:T(8,128)(2,1)S(1)} %collective-permute-done.28) | copy-start | bytes 1032196
  67.4 45.2 %collective-permute-start.16 = (bf16[688,8,128]{2,1,0:T(8,128)(2,1)S(1)}, bf16[688,8,128]{2,1,0:T(8,128)(2,1)S(1)}, u32[]{:S(2)}, u32[]{:S(2)}) collective-permute-start(bf16[688,8,128]{2,1,0:T(8,128)(2,1)S(1)} %pad_maximum_fusion), channel_id=1, source_target_pairs={{0,2},{1,33},{2,4},{3,35},{4,6},{5,37},{6,0},{7,39},{8,10},{9,41},... | collective-permute-start | bytes 4227080 | tf_op jit(solution)/shard_map/ppermute | solution.py:34
  67.4 27.4 %collective-permute-start.17 = (bf16[344,8,128]{2,1,0:T(8,128)(2,1)S(1)}, bf16[344,8,128]{2,1,0:T(8,128)(2,1)}, u32[]{:S(2)}, u32[]{:S(2)}) collective-permute-start(bf16[344,8,128]{2,1,0:T(8,128)(2,1)S(1)} %collective-permute-done.8), channel_id=1, source_target_pairs={{0,2},{1,33},{2,4},{3,35},{4,6},{5,37},{6,0},{7,39},{8,10},{9,41},... | collective-permute-start | bytes 2113544 | tf_op jit(solution)/shard_map/ppermute | solution.py:34
  69.4 43.5 %collective-permute-start.15 = (bf16[688,8,128]{2,1,0:T(8,128)(2,1)S(1)}, bf16[688,8,128]{2,1,0:T(8,128)(2,1)S(1)}, u32[]{:S(2)}, u32[]{:S(2)}) collective-permute-start(bf16[688,8,128]{2,1,0:T(8,128)(2,1)S(1)} %constant_dynamic-update-slice_fusion), channel_id=1, source_target_pairs={{0,6},{1,97},{2,0},{3,99},{4,2},{5,101},{6,4},{7,103},{8,14},{9,10... | collective-permute-start | bytes 4227080 | tf_op jit(solution)/shard_map/ppermute | solution.py:34
  71.0 41.9 %copy-start.4 = (bf16[336,8,128]{2,1,0:T(8,128)(2,1)}, bf16[336,8,128]{2,1,0:T(8,128)(2,1)S(1)}, u32[]{:S(2)}) copy-start(bf16[336,8,128]{2,1,0:T(8,128)(2,1)S(1)} %constant_dynamic-update-slice_fusion.3) | copy-start | bytes 2064388
  74.8 38.2 %copy-start.12 = (bf16[168,8,128]{2,1,0:T(8,128)(2,1)}, bf16[168,8,128]{2,1,0:T(8,128)(2,1)S(1)}, u32[]{:S(2)}) copy-start(bf16[168,8,128]{2,1,0:T(8,128)(2,1)S(1)} %collective-permute-done.23) | copy-start | bytes 1032196
  74.8 22.7 %collective-permute-start.20 = (bf16[336,8,128]{2,1,0:T(8,128)(2,1)S(1)}, bf16[336,8,128]{2,1,0:T(8,128)(2,1)S(1)}, u32[]{:S(2)}, u32[]{:S(2)}) collective-permute-start(bf16[336,8,128]{2,1,0:T(8,128)(2,1)S(1)} %constant_dynamic-update-slice_fusion.3), channel_id=1, source_target_pairs={{0,24},{1,25},{2,26},{3,27},{4,28},{5,29},{6,30},{7,31},{8,0},{9,1... | collective-permute-start | bytes 2064392 | tf_op jit(solution)/shard_map/ppermute | solution.py:34
  94.8 17.8 %collective-permute-start.18 = (bf16[344,8,128]{2,1,0:T(8,128)(2,1)S(1)}, bf16[344,8,128]{2,1,0:T(8,128)(2,1)}, u32[]{:S(2)}, u32[]{:S(2)}) collective-permute-start(bf16[344,8,128]{2,1,0:T(8,128)(2,1)S(1)} %pad_maximum_fusion.2), channel_id=1, source_target_pairs={{0,2},{1,33},{2,4},{3,35},{4,6},{5,37},{6,0},{7,39},{8,10},{9,41},... | collective-permute-start | bytes 2113544 | tf_op jit(solution)/shard_map/ppermute | solution.py:34
  94.8 37.0 %collective-permute-start.24 = (bf16[688,8,128]{2,1,0:T(8,128)(2,1)}, bf16[688,8,128]{2,1,0:T(8,128)(2,1)}, u32[]{:S(2)}, u32[]{:S(2)}) collective-permute-start(bf16[688,8,128]{2,1,0:T(8,128)(2,1)} %collective-permute-done.14), channel_id=1, source_target_pairs={{0,6},{1,97},{2,0},{3,99},{4,2},{5,101},{6,4},{7,103},{8,14},{9,10... | collective-permute-start | bytes 4227080 | tf_op jit(solution)/shard_map/ppermute | solution.py:34
  97.5 0.9 copy-start.8
  97.5 7.4 %collective-permute-start.29 = (bf16[168,8,128]{2,1,0:T(8,128)(2,1)S(1)}, bf16[168,8,128]{2,1,0:T(8,128)(2,1)}, u32[]{:S(2)}, u32[]{:S(2)}) collective-permute-start(bf16[168,8,128]{2,1,0:T(8,128)(2,1)S(1)} %collective-permute-done.23), channel_id=1, source_target_pairs={{0,8},{1,9},{2,10},{3,11},{4,12},{5,13},{6,14},{7,15},{8,16},{9,17... | collective-permute-start | bytes 1032200 | tf_op jit(solution)/shard_map/ppermute | solution.py:34
  104.9 31.4 %collective-permute-start.30 = (bf16[512,1024]{1,0:T(8,128)(2,1)S(1)}, bf16[512,1024]{1,0:T(8,128)(2,1)S(1)}, u32[]{:S(2)}, u32[]{:S(2)}) collective-permute-start(bf16[512,1024]{1,0:T(8,128)(2,1)S(1)} %copy-done), channel_id=1, source_target_pairs={{0,1},{1,0},{2,3},{3,2},{4,5},{5,4},{6,7},{7,6},{8,9},{9,8},{10,11... | collective-permute-start | bytes 3145736 | tf_op jit(solution)/shard_map/ppermute | solution.py:39
  112.6 17.0 %collective-permute-start.25 = (bf16[344,8,128]{2,1,0:T(8,128)(2,1)}, bf16[344,8,128]{2,1,0:T(8,128)(2,1)}, u32[]{:S(2)}, u32[]{:S(2)}) collective-permute-start(bf16[344,8,128]{2,1,0:T(8,128)(2,1)} %collective-permute-done.17), channel_id=1, source_target_pairs={{0,2},{1,33},{2,4},{3,35},{4,6},{5,37},{6,0},{7,39},{8,10},{9,41},... | collective-permute-start | bytes 2113544 | tf_op jit(solution)/shard_map/ppermute | solution.py:34
  112.6 1.1 copy-start.5
  112.6 19.2 %collective-permute-start.26 = (bf16[344,8,128]{2,1,0:T(8,128)(2,1)}, bf16[344,8,128]{2,1,0:T(8,128)(2,1)S(1)}, u32[]{:S(2)}, u32[]{:S(2)}) collective-permute-start(bf16[344,8,128]{2,1,0:T(8,128)(2,1)} %collective-permute-done.18), channel_id=1, source_target_pairs={{0,2},{1,33},{2,4},{3,35},{4,6},{5,37},{6,0},{7,39},{8,10},{9,41},... | collective-permute-start | bytes 2113544 | tf_op jit(solution)/shard_map/ppermute | solution.py:34
  112.9 1.3 copy-start.6
  112.9 16.7 %collective-permute-start.27 = (bf16[336,8,128]{2,1,0:T(8,128)(2,1)}, bf16[336,8,128]{2,1,0:T(8,128)(2,1)S(1)}, u32[]{:S(2)}, u32[]{:S(2)}) collective-permute-start(bf16[336,8,128]{2,1,0:T(8,128)(2,1)} %collective-permute-done.19), channel_id=1, source_target_pairs={{0,24},{1,25},{2,26},{3,27},{4,28},{5,29},{6,30},{7,31},{8,0},{9,1... | collective-permute-start | bytes 2064392 | tf_op jit(solution)/shard_map/ppermute | solution.py:34
  116.1 48.5 %slice-start = ((s8[16777216]{0:T(1024)(128)(4,1)}), s8[4194304]{0:T(1024)(128)(4,1)S(1)}, s32[]{:S(2)}) async-start(s8[16777216]{0:T(1024)(128)(4,1)} %bitcast.26), calls=%async_computation | async-start | bytes 8388608
  116.1 48.5 %slice-start.1 = ((s8[16777216]{0:T(1024)(128)(4,1)}), s8[4194304]{0:T(1024)(128)(4,1)S(1)}, s32[]{:S(2)}) async-start(s8[16777216]{0:T(1024)(128)(4,1)} %bitcast.26), calls=%async_computation.1 | async-start | bytes 8388608
  129.6 2.2 %copy-start.9 = (bf16[336,8,128]{2,1,0:T(8,128)(2,1)}, bf16[336,8,128]{2,1,0:T(8,128)(2,1)S(1)}, u32[]{:S(2)}) copy-start(bf16[336,8,128]{2,1,0:T(8,128)(2,1)S(1)} %collective-permute-done.27) | copy-start | bytes 2064388
  131.8 0.9 copy-start.7
  132.7 31.9 %slice-start.2 = ((s8[16777216]{0:T(1024)(128)(4,1)}), s8[4194304]{0:T(1024)(128)(4,1)S(1)}, s32[]{:S(2)}) async-start(s8[16777216]{0:T(1024)(128)(4,1)} %bitcast.26), calls=%async_computation.2 | async-start | bytes 8388608
  136.3 28.3 %slice-start.3 = ((s8[16777216]{0:T(1024)(128)(4,1)}), s8[4194304]{0:T(1024)(128)(4,1)S(1)}, s32[]{:S(2)}) async-start(s8[16777216]{0:T(1024)(128)(4,1)} %bitcast.26), calls=%async_computation.3 | async-start | bytes 8388608
  143.7 20.9 %collective-permute-start.31 = (bf16[512,1024]{1,0:T(8,128)(2,1)S(1)}, bf16[512,1024]{1,0:T(8,128)(2,1)S(1)}, u32[]{:S(2)}, u32[]{:S(2)}) collective-permute-start(bf16[512,1024]{1,0:T(8,128)(2,1)S(1)} %get-tuple-element.71), channel_id=1, source_target_pairs={{0,1},{1,0},{2,3},{3,2},{4,5},{5,4},{6,7},{7,6},{8,9},{9,8},{10,11... | collective-permute-start | bytes 3145736 | tf_op jit(solution)/shard_map/ppermute | solution.py:39
  151.7 12.8 %collective-permute-start.32 = (f32[512,256]{1,0:T(8,128)S(1)}, f32[512,256]{1,0:T(8,128)S(1)}, u32[]{:S(2)}, u32[]{:S(2)}) collective-permute-start(f32[512,256]{1,0:T(8,128)S(1)} %get-tuple-element.72), channel_id=1, source_target_pairs={{0,1},{1,0},{2,3},{3,2},{4,5},{5,4},{6,7},{7,6},{8,9},{9,8},{10,11... | collective-permute-start | bytes 1572872 | tf_op jit(solution)/shard_map/ppermute | solution.py:39

commit v2 on v1

--- a/solution.py
+++ b/solution.py
@@ -56,76 +56,45 @@
 
 
 def gathered(both):
-    big = both[:BIG].reshape(-1, 8, HEAD_DIM)
-    small = both[BIG:].reshape(-1, 8, HEAD_DIM)
-    big_axes = [[axes[phase] for axes in BIG_AXES] for phase in range(3)]
-    small_axes = [[axes[phase] for axes in SMALL_AXES] for phase in range(3)]
-    b, s = big_axes[0], small_axes[0]
-    big, *others = together(
-        big,
-        across(big, b),
-        across(small, s),
-        back(big, b),
-        back(small, s),
-        forth(big, b),
-        forth(small, s),
-    )
-    big, small = together(
-        jnp.concatenate([big, others[2], others[4], others[0]], axis=0),
-        jnp.concatenate([small, others[3], others[5], others[1]], axis=0),
-    )
-    parts = {"big": (big, big_axes), "small": (small, small_axes)}
-
-    def each(act):
-        return {part: act(part, parts[part][1][1], parts[part][1][2]) for part in parts}
-
-    def ready(*dicts):
-        flat = together(*(array for one in dicts for array in one.values()))
-        return [dict(zip(parts, flat[2 * k : 2 * k + 2])) for k in range(len(dicts))]
-
-    joined = lambda *dicts: {
-        part: jnp.concatenate([one[part] for one in dicts], axis=0) for part in parts
-    }
-    own = {part: array for part, (array, _) in parts.items()}
-    after = each(lambda part, ring, last: back(own[part], ring))
-    before = each(lambda part, ring, last: forth(own[part], ring))
-    after, before = ready(after, before)
-    half = {part: array.shape[0] // 2 for part, array in own.items()}
-    first, before, low, high = ready(
-        joined(own, after),
-        before,
-        {part: after[part][: half[part]] for part in parts},
-        {part: before[part][half[part] :] for part in parts},
-    )
-    low = each(lambda part, ring, last: back(low[part], ring))
-    high = each(lambda part, ring, last: forth(high[part], ring))
-    first_after = each(lambda part, ring, last: back(first[part], last))
-    before_before = each(lambda part, ring, last: forth(before[part], last))
-    first_before = each(lambda part, ring, last: forth(first[part], last))
-    low, high = ready(low, high)
-    rest, second = joined(low, high), joined(before, low, high)
-    rest_before = each(lambda part, ring, last: forth(rest[part], last))
-    second_after = each(lambda part, ring, last: back(second[part], last))
-    before_far = each(lambda part, ring, last: forth(before_before[part], last))
-    first_far = each(lambda part, ring, last: back(first_after[part], last))
-    rest_far = each(lambda part, ring, last: forth(rest_before[part], last))
-    return tuple(
-        [
-            pltpu.with_memory_space_constraint(piece[part].reshape(-1, HEAD_DIM), pltpu.HBM)
-            for piece in (
-                first,
-                second,
-                first_after,
-                second_after,
-                first_before,
-                before_before,
-                rest_before,
-                first_far,
-                before_far,
-                rest_far,
-            )
+    def steps(part, axes):
+        first, ring, last = ([axes[core][phase] for core in range(2)] for phase in range(3))
+        join = lambda *arrays: jnp.concatenate(arrays, axis=0)
+        far, after, before = together(across(part, first), back(part, first), forth(part, first))
+        (own,) = together(join(part, after, before, far))
+        half = own.shape[0] // 2
+        after, before = together(back(own, ring), forth(own, ring))
+        first_half, before, low, high = together(
+            join(own, after), before, after[:half], before[half:]
+        )
+        low, high = back(low, ring), forth(high, ring)
+        first_after, before_before = back(first_half, last), forth(before, last)
+        first_before = forth(first_half, last)
+        low, high = together(low, high)
+        rest, second = join(low, high), join(before, low, high)
+        rest_before = forth(rest, last)
+        second_after = back(second, last)
+        first_far, before_far = back(first_after, last), forth(before_before, last)
+        rest_far = forth(rest_before, last)
+        pieces = (
+            first_half,
+            second,
+            first_after,
+            second_after,
+            first_before,
+            before_before,
+            rest_before,
+            first_far,
+            before_far,
+            rest_far,
+        )
+        return [
+            pltpu.with_memory_space_constraint(piece.reshape(-1, HEAD_DIM), pltpu.HBM)
+            for piece in pieces
         ]
-        for part in parts
+
+    return (
+        steps(both[:BIG].reshape(-1, 8, HEAD_DIM), BIG_AXES),
+        steps(both[BIG:].reshape(-1, 8, HEAD_DIM), SMALL_AXES),
     )
 
 
@@ -157,7 +126,7 @@
     return pl.multiple_of(row, 16)
 
 
-def fetch(first_piece, codes, big, small, kbuf, vbuf, sems, entries, left=None):
+def fetch(first_piece, codes, big, small, kbuf, vbuf, sems):
     count = len(big)
 
     def parts(index):
@@ -237,69 +206,66 @@
             def _():
                 copy(small[1], 0, BLOCK, vbuf, at, sems.at[2, index]).wait()
 
-    number, entry_of = entries
-
-    def begin(k, missing):
-        index = entry_of(k)
+    return parts, has, issue, finish
+
+
+def fetch_near(codes, starts, *refs):
+    big, small = refs[:NEAR], refs[NEAR : 2 * NEAR]
+    kbuf, vbuf, left, sems = refs[2 * NEAR :]
+    parts, has, issue, finish = fetch(0, codes, big, small, kbuf, vbuf, sems)
+
+    def begin(index, missing):
         issue(index)
-        if left is None:
-            return missing
         big_piece, _, small_piece, _, within, _ = parts(index)
         left[missing] = index
         whole = has(big_piece) & (has(small_piece) | (within == 0))
         return missing + jnp.where(whole, jnp.int32(0), jnp.int32(1))
 
-    missing = lax.fori_loop(0, number, begin, jnp.int32(0))
-    if left is not None:
-        left[SLOTS] = missing
-
-    def end(k, _):
-        finish(entry_of(k))
+    def block_row(row, missing):
+        missing = lax.fori_loop(starts[row], starts[row + 1], begin, missing)
+        left[SLOTS + row] = missing
+        return missing
+
+    def end(index, _):
+        finish(index)
         return 0
 
-    lax.fori_loop(0, number, end, 0)
-
-
-def fetch_near(codes, *refs):
-    kbuf, vbuf, left, sems = refs[2 * NEAR :]
-    fetch(0, codes, refs[:NEAR], refs[NEAR : 2 * NEAR], kbuf, vbuf, sems, (SLOTS, lambda k: k), left)
-
-
-def fetch_far(codes, left, *refs):
-    kbuf, vbuf, sems = refs[8:]
-    fetch(NEAR, codes, refs[:3], refs[3:6], kbuf, vbuf, sems, (left[SLOTS], lambda k: left[k]))
-
-
-def fetched(codes, big, small):
+    lax.fori_loop(0, RPD, block_row, jnp.int32(0))
+    lax.fori_loop(0, SLOTS, end, 0)
+
+
+def fetched(codes, starts, big, small):
     vmem = pl.BlockSpec(memory_space=pltpu.VMEM)
     smem = pl.BlockSpec(memory_space=pltpu.SMEM)
     hbm = pl.BlockSpec(memory_space=pltpu.HBM)
     blocks = jax.ShapeDtypeStruct((SLOTS * BLOCK, HEAD_DIM), jnp.bfloat16)
-    common = dict(
+    return pl.pallas_call(
+        fetch_near,
+        name="fetch_near",
+        in_specs=[smem, smem, *[hbm] * (2 * NEAR)],
+        out_shape=(blocks, blocks, jax.ShapeDtypeStruct((2 * SLOTS,), jnp.int32)),
+        out_specs=(vmem, vmem, smem),
         scratch_shapes=[pltpu.SemaphoreType.DMA((3, SLOTS))],
         compiler_params=pltpu.CompilerParams(vmem_limit_bytes=10 * 2**20),
-    )
-    *near, left = pl.pallas_call(
-        fetch_near,
-        name="fetch_near",
-        in_specs=[smem, *[hbm] * (2 * NEAR)],
-        out_shape=(blocks, blocks, jax.ShapeDtypeStruct((2 * SLOTS,), jnp.int32)),
-        out_specs=(vmem, vmem, smem),
-        **common,
-    )(codes, *big[:NEAR], *small[:NEAR])
-    return pl.pallas_call(
-        fetch_far,
-        name="fetch_far",
-        in_specs=[smem, smem, *[hbm] * 6, vmem, vmem],
-        out_shape=(blocks, blocks),
-        out_specs=(vmem, vmem),
-        input_output_aliases={8: 0, 9: 1},
-        **common,
-    )(codes, left, *big[NEAR:], *small[NEAR:], *near)
-
-
-def attend(place, starts, q_ref, kbuf, vbuf, o_ref, stat_ref, s_ref, m_ref, acc):
-    first_row = place[0]
+    )(codes, starts, *big[:NEAR], *small[:NEAR])
+
+
+def attend(place, starts, codes, left, own_queries, their_queries, *refs):
+    big, small = refs[:3], refs[3:6]
+    own_out, own_stat, their_out, their_stat, kbuf, vbuf = refs[8:14]
+    qs, s_ref, m_ref, acc, sems = refs[14:]
+    core = place[0]
+    _, _, issue, finish = fetch(NEAR, codes, big, small, kbuf, vbuf, sems)
+
+    def begin(k, _):
+        issue(left[k])
+        return 0
+
+    def end(k, _):
+        finish(left[k])
+        return 0
+
+    lax.fori_loop(0, left[SLOTS + RPD - 1], begin, 0)
 
     def blocks_of(buf, slot, end, count):
         return [
@@ -307,41 +273,41 @@
             for k in range(count)
         ]
 
-    def block_row(local, _):
-        row = first_row + local
-        begin, end = starts[row], starts[row + 1]
-        number = end - begin
+    def block_row(row, waited):
+        lax.fori_loop(waited, left[SLOTS + row], end, 0)
+        begin, stop = starts[row], starts[row + 1]
+        number = stop - begin
         quads = (number + 1) >> 2
         rest = begin + 4 * quads
+        mine = (row >> 2) == core
+        local = pl.ds(aligned((row & 3) * BLOCK), BLOCK)
+        columns_of = lambda head: slice(head * HEAD_DIM, (head + 1) * HEAD_DIM)
+        rows_of = lambda head: slice(head * BLOCK, (head + 1) * BLOCK)
+
+        def take(queries):
+            for head in range(HEADS):
+                qs[rows_of(head), :] = queries[local, columns_of(head)]
+
+        lax.cond(mine, lambda: take(own_queries), lambda: take(their_queries))
         m_ref[...] = jnp.full(m_ref.shape, -1e30, jnp.float32)
         acc[...] = jnp.zeros(acc.shape, jnp.float32)
 
         def score(slot, into, count):
-            keys = jnp.concatenate(blocks_of(kbuf, slot, end, count), axis=0)
-            heads = jnp.concatenate(
-                [
-                    q_ref[
-                        pl.ds(aligned(local * BLOCK), BLOCK),
-                        head * HEAD_DIM : (head + 1) * HEAD_DIM,
-                    ]
-                    for head in range(HEADS)
-                ],
-                axis=0,
-            )
+            keys = jnp.concatenate(blocks_of(kbuf, slot, stop, count), axis=0)
             scores = SCALE * lax.dot_general(
-                heads, keys, (((1,), (1,)), ((), ())), preferred_element_type=jnp.float32
+                qs[...], keys, (((1,), (1,)), ((), ())), preferred_element_type=jnp.float32
             )
             columns = [scores[:, k * BLOCK : (k + 1) * BLOCK] for k in range(count)]
             top = m_ref[...]
             for column in columns:
                 top = jnp.maximum(top, column)
             m_ref[...] = top
-            columns[-1] = jnp.where(slot + count - 1 < end, columns[-1], -1e30)
+            columns[-1] = jnp.where(slot + count - 1 < stop, columns[-1], -1e30)
             for k in range(count):
                 s_ref[into, :, k * BLOCK : (k + 1) * BLOCK] = columns[k]
 
         def weigh(slot, into, count):
-            values = jnp.concatenate(blocks_of(vbuf, slot, end, count), axis=0)
+            values = jnp.concatenate(blocks_of(vbuf, slot, stop, count), axis=0)
             values = jnp.concatenate([values, jnp.ones(values.shape, values.dtype)], axis=1)
             top = m_ref[...]
             weights = jnp.concatenate(
@@ -361,7 +327,7 @@
                 return 0
 
             lax.fori_loop(0, quads, body, 0)
-            pl.when(rest < end)(lambda: step(rest, quads, 2))
+            pl.when(rest < stop)(lambda: step(rest, quads, 2))
 
         each_quad(score)
         m_ref[...] = jnp.broadcast_to(
@@ -370,41 +336,62 @@
         each_quad(weigh)
 
         lane = lax.broadcasted_iota(jnp.int32, (BLOCK, HEAD_DIM), 1)
-        tops = sums = jnp.zeros((BLOCK, HEAD_DIM), jnp.float32)
-        for head in range(HEADS):
-            rows = slice(head * BLOCK, (head + 1) * BLOCK)
-            o_ref[pl.ds(aligned(local * BLOCK), BLOCK), head * HEAD_DIM : (head + 1) * HEAD_DIM] = (
-                acc[rows, :HEAD_DIM].astype(jnp.bfloat16)
-            )
-            tops = jnp.where(lane == head, m_ref[rows, :], tops)
-            sums = jnp.where(lane == head, acc[rows, HEAD_DIM:], sums)
-        stat_ref[pl.ds(aligned(local * BLOCK), BLOCK), :HEAD_DIM] = tops
-        stat_ref[pl.ds(aligned(local * BLOCK), BLOCK), HEAD_DIM:] = sums
-        return 0
-
-    lax.fori_loop(0, 4, block_row, 0)
-
-
-def attention_call(place, starts, queries, keys, values):
-    rows = queries.shape[0]
+
+        def put(out, stat):
+            tile = jnp.zeros((BLOCK, HEAD_DIM), jnp.float32)
+            for head in range(HEADS):
+                out[local, columns_of(head)] = acc[rows_of(head), :HEAD_DIM].astype(jnp.bfloat16)
+                tile = jnp.where(lane == head, m_ref[rows_of(head), :], tile)
+                tile = jnp.where(lane == HEADS + head, acc[rows_of(head), HEAD_DIM:], tile)
+            stat[local, :] = tile
+
+        lax.cond(mine, lambda: put(own_out, own_stat), lambda: put(their_out, their_stat))
+        return left[SLOTS + row]
+
+    lax.fori_loop(0, RPD, block_row, jnp.int32(0))
+
+
+def attention_call(place, starts, codes, own_queries, their_queries, big, small, listed):
+    rows = own_queries.shape[0]
     smem = pl.BlockSpec(memory_space=pltpu.SMEM)
     vmem = pl.BlockSpec(memory_space=pltpu.VMEM)
+    hbm = pl.BlockSpec(memory_space=pltpu.HBM)
+    keys, values, left = listed
+    out = jax.ShapeDtypeStruct((rows, HEADS * HEAD_DIM), jnp.bfloat16)
+    stat = jax.ShapeDtypeStruct((rows, HEAD_DIM), jnp.float32)
+    blocks = jax.ShapeDtypeStruct(keys.shape, keys.dtype)
     return pl.pallas_call(
         attend,
         name="attend",
-        out_shape=(
-            jax.ShapeDtypeStruct((rows, HEADS * HEAD_DIM), jnp.bfloat16),
-            jax.ShapeDtypeStruct((rows, 2 * HEAD_DIM), jnp.float32),
-        ),
-        in_specs=[smem, smem, vmem, vmem, vmem],
-        out_specs=(vmem, vmem),
+        out_shape=(out, stat, out, stat, blocks, blocks),
+        in_specs=[*[smem] * 4, vmem, vmem, *[hbm] * 6, vmem, vmem],
+        out_specs=(vmem,) * 6,
+        input_output_aliases={12: 4, 13: 5},
         scratch_shapes=[
+            pltpu.VMEM((HEADS * BLOCK, HEAD_DIM), jnp.bfloat16),
             pltpu.VMEM((QUADS, HEADS * BLOCK, 4 * BLOCK), jnp.float32),
             pltpu.VMEM((HEADS * BLOCK, BLOCK), jnp.float32),
             pltpu.VMEM((HEADS * BLOCK, 2 * HEAD_DIM), jnp.float32),
+            pltpu.SemaphoreType.DMA((3, SLOTS)),
         ],
-        compiler_params=pltpu.CompilerParams(vmem_limit_bytes=24 * 2**20),
-    )(place, starts, queries, keys, values)
+        cost_estimate=pl.CostEstimate(
+            flops=8 * SLOTS * HEADS * BLOCK * BLOCK * HEAD_DIM,
+            transcendentals=SLOTS * HEADS * BLOCK * BLOCK,
+            bytes_accessed=4 * SLOTS * BLOCK * HEAD_DIM + 8 * rows * HEADS * HEAD_DIM,
+        ),
+        compiler_params=pltpu.CompilerParams(vmem_limit_bytes=20 * 2**20),
+    )(
+        place,
+        starts,
+        codes,
+        left,
+        own_queries,
+        their_queries,
+        *big[NEAR:],
+        *small[NEAR:],
+        keys,
+        values,
+    )[:4]
 
 
 def project(o_a, stat_a, o_b, stat_b, w_ref, out_ref, att):
@@ -412,10 +399,11 @@
 
     def merge(chunk, _):
         rows = pl.ds(aligned(chunk * MERGE), MERGE)
-        top_a, top_b = stat_a[rows, :HEAD_DIM], stat_b[rows, :HEAD_DIM]
+        top_a, top_b = stat_a[rows, :], stat_b[rows, :]
         top = jnp.maximum(top_a, top_b)
         by_a, by_b = jnp.exp2(top_a - top), jnp.exp2(top_b - top)
-        total = stat_a[rows, HEAD_DIM:] * by_a + stat_b[rows, HEAD_DIM:] * by_b
+        sums = lambda stat: pltpu.roll(stat, HEAD_DIM - HEADS, 1)
+        total = sums(top_a) * by_a + sums(top_b) * by_b
         by_a, by_b = by_a / total, by_b / total
         for head in range(HEADS):
             columns = slice(head * HEAD_DIM, (head + 1) * HEAD_DIM)
@@ -488,14 +476,18 @@
     big, small = gathered(jnp.concatenate([keys, values], axis=0))
     other_queries = swap(queries)
     starts, codes = tables(row_pos, core, row_ptr, col_blocks)
-    listed = fetched(codes, big, small)
-    place = lambda first: first.reshape(1).astype(jnp.int32)
-    o_theirs, stat_theirs = attention_call(
-        place(4 - 4 * core), starts, other_queries, *listed
+    listed = fetched(codes, starts, big, small)
+    own_out, own_stat, their_out, their_stat = attention_call(
+        core.reshape(1).astype(jnp.int32),
+        starts,
+        codes,
+        queries,
+        other_queries,
+        big,
+        small,
+        listed,
     )
-    o_got, stat_got = swap(o_theirs), swap(stat_theirs)
-    o_own, stat_own = attention_call(place(4 * core), starts, queries, *listed)
-    return projection_call(o_own, stat_own, o_got, stat_got, w_out)
+    return projection_call(own_out, own_stat, swap(their_out), swap(their_stat), w_out)
 
 
 def solution(mesh):

time: 178 us -> 160 us (0.90)
  waiting for transfers between devices: 76.5 us -> 47.4 us
  starting transfers between devices: 47.9 us -> 58.4 us
    ppermute x30, waiting for transfers between devices: 76.5 us -> 44.9 us  [send(): return lax.ppermute(array, ('row', 'col'), pairs)]
    ppermute x30, starting transfers between devices: 32.1 us -> 46.1 us  [send(): return lax.ppermute(array, ('row', 'col'), pairs)]
    ppermute x3, starting transfers between devices: 15.8 us -> 12.3 us  [swap(): return lax.ppermute(array, ('row', 'col'), pairs)]
    ppermute x3, waiting for transfers between devices: 0.01 us -> 2.57 us  [swap(): return lax.ppermute(array, ('row', 'col'), pairs)]
    pallas_call x4 -> x2, Pallas kernels: 32.3 us -> 31.5 us  [the longest x1 22.7 us: attention_call(): pl.pallas_call(attend, name='attend', out_shape=(out, stat, out, stat, bl...]
  transfers between devices with their start and end apart: 33 -> 33, of which waited for: 14 -> 10; matrix products, arithmetic and copies ran while one was open for 2% -> 4% of each run, Pallas kernels for 14% -> 6%
where the time goes in v2:
time: 160 us; the launch traced here: 159 us
  starting transfers between devices  58.4 us (36%)
  waiting for transfers between devices  47.4 us (30%)
  Pallas kernels  45 us (28%)
  local copies, waits for them, and re-layouts  5.72 us (4%)
  other arithmetic  2.44 us (2%)
    ppermute x30, starting transfers between devices, send(): return lax.ppermute(array, ('row', 'col'), pairs)  46.1 us
    ppermute x30, waiting for transfers between devices, send(): return lax.ppermute(array, ('row', 'col'), pairs)  44.9 us
    pallas_call x1, Pallas kernels, attention_call(): pl.pallas_call(attend, name='attend', out_shape=(out, stat, out, stat, bl...  22.7 us
    pallas_call x1, Pallas kernels, projection_call(): pl.pallas_call(project, name='project', grid=(width // tile,), out_shape=...  13.5 us
    ppermute x3, starting transfers between devices, swap(): return lax.ppermute(array, ('row', 'col'), pairs)  12.3 us
    pallas_call x1, Pallas kernels, fetched(): pl.pallas_call(fetch_near, name='fetch_near', in_specs=[smem, smem, *[hbm...  8.79 us
  transfers between devices with their start and end apart: 33, of which 10 were waited for; matrix products, arithmetic and copies ran while one was open for 4% of the time, Pallas kernels for 6%

profile of v2, /device:TPU:1, one launch (start us, length us, event | category | flops | bytes accessed | tf_op | source)
XLA Modules:
  0.0 159.3 jit_solution(577137410814948836)
XLA Ops:
  0.0 1.0 fusion
  1.0 3.6 %collective-permute-start = (bf16[86,8,128]{2,1,0:T(8,128)(2,1)S(1)}, bf16[86,8,128]{2,1,0:T(8,128)(2,1)S(1)}, u32[]{:S(2)}, u32[]{:S(2)}) collective-permute-start(bf16[86,8,128]{2,1,0:T(8,128)(2,1)S(1)} %fusion), channel_id=1, source_target_pairs={{0,16},{1,5},{2,18},{3,7},{4,20},{5,1},{6,22},{7,3},{8,24},{9,13},... | collective-permute-start | bytes 528392 | tf_op jit(solution)/shard_map/ppermute | solution.py:34
  4.7 0.9 collective-permute-start.1
  5.5 0.6 collective-permute-start.2
  6.1 0.9 slice_bitcast_fusion
  7.0 3.6 %collective-permute-start.12 = (bf16[42,8,128]{2,1,0:T(8,128)(2,1)S(1)}, bf16[42,8,128]{2,1,0:T(8,128)(2,1)S(1)}, u32[]{:S(2)}, u32[]{:S(2)}) collective-permute-start(bf16[42,8,128]{2,1,0:T(8,128)(2,1)S(1)} %slice_bitcast_fusion), channel_id=1, source_target_pairs={{0,64},{1,65},{2,66},{3,67},{4,68},{5,69},{6,70},{7,71},{8,72},{9,... | collective-permute-start | bytes 258056 | tf_op jit(solution)/shard_map/ppermute | solution.py:34
  10.6 0.4 collective-permute-start.13
  11.1 0.0 collective-permute-done
  11.1 1.0 collective-permute-start.14
  12.1 0.0 collective-permute-done.1
  12.1 0.0 collective-permute-done.2
  12.1 0.1 pad_maximum_fusion.1
  12.2 2.8 %collective-permute-start.3 = (bf16[344,8,128]{2,1,0:T(8,128)(2,1)S(1)}, bf16[344,8,128]{2,1,0:T(8,128)(2,1)S(1)}, u32[]{:S(2)}, u32[]{:S(2)}) collective-permute-start(bf16[344,8,128]{2,1,0:T(8,128)(2,1)S(1)} %pad_maximum_fusion.1), channel_id=1, source_target_pairs={{0,96},{1,25},{2,98},{3,27},{4,100},{5,29},{6,102},{7,31},{8,104},... | collective-permute-start | bytes 2113544 | tf_op jit(solution)/shard_map/ppermute | solution.py:34
  15.0 0.6 collective-permute-done.14
  15.7 2.4 %collective-permute-start.15 = (bf16[168,8,128]{2,1,0:T(8,128)(2,1)S(1)}, bf16[168,8,128]{2,1,0:T(8,128)(2,1)S(1)}, u32[]{:S(2)}, u32[]{:S(2)}) collective-permute-start(bf16[168,8,128]{2,1,0:T(8,128)(2,1)S(1)} %pad_maximum_fusion.4), channel_id=1, source_target_pairs={{0,6},{1,7},{2,0},{3,1},{4,2},{5,3},{6,4},{7,5},{8,14},{9,15},{10,... | collective-permute-start | bytes 1032200 | tf_op jit(solution)/shard_map/ppermute | solution.py:34
  18.1 3.8 %collective-permute-start.24 = (bf16[512,1024]{1,0:T(8,128)(2,1)S(1)}, bf16[512,1024]{1,0:T(8,128)(2,1)S(1)}, u32[]{:S(2)}, u32[]{:S(2)}) collective-permute-start(bf16[512,1024]{1,0:T(8,128)(2,1)S(1)} %copy-done), channel_id=1, source_target_pairs={{0,1},{1,0},{2,3},{3,2},{4,5},{5,4},{6,7},{7,6},{8,9},{9,8},{10,11... | collective-permute-start | bytes 3145736 | tf_op jit(solution)/shard_map/ppermute | solution.py:39
  21.9 0.4 collective-permute-done.15
  22.3 3.4 %collective-permute-done.16 = bf16[168,8,128]{2,1,0:T(8,128)(2,1)S(1)} collective-permute-done((bf16[168,8,128]{2,1,0:T(8,128)(2,1)S(1)}, bf16[168,8,128]{2,1,0:T(8,128)(2,1)S(1)}, u32[]{:S(2)}, u32[]{:S(2)}) %collective-permute-start.16) | collective-permute-done | bytes 344096 | tf_op jit(solution)/shard_map/ppermute | solution.py:34
  25.7 0.1 pad_maximum_fusion.3
  25.8 0.1 collective-permute-start.17
  25.9 1.5 collective-permute-start.18
  27.3 1.1 collective-permute-start.22
  28.5 0.1 pad_maximum_fusion
  28.6 0.0 copy-start.1
  28.6 1.7 %collective-permute-start.5 = (bf16[172,8,128]{2,1,0:T(8,128)(2,1)S(1)}, bf16[172,8,128]{2,1,0:T(8,128)(2,1)S(1)}, u32[]{:S(2)}, u32[]{:S(2)}) collective-permute-start(bf16[172,8,128]{2,1,0:T(8,128)(2,1)S(1)} %slice.27), channel_id=1, source_target_pairs={{0,96},{1,25},{2,98},{3,27},{4,100},{5,29},{6,102},{7,31},{8,104},... | collective-permute-start | bytes 1056776 | tf_op jit(solution)/shard_map/ppermute | solution.py:34
  30.3 2.4 %collective-permute-start.6 = (bf16[172,8,128]{2,1,0:T(8,128)(2,1)S(1)}, bf16[172,8,128]{2,1,0:T(8,128)(2,1)S(1)}, u32[]{:S(2)}, u32[]{:S(2)}) collective-permute-start(bf16[172,8,128]{2,1,0:T(8,128)(2,1)S(1)} %slice.28), channel_id=1, source_target_pairs={{0,32},{1,9},{2,34},{3,11},{4,36},{5,13},{6,38},{7,15},{8,40},{9,1... | collective-permute-start | bytes 1056776 | tf_op jit(solution)/shard_map/ppermute | solution.py:34
  32.7 2.7 %collective-permute-start.7 = (bf16[688,8,128]{2,1,0:T(8,128)(2,1)S(1)}, bf16[688,8,128]{2,1,0:T(8,128)(2,1)}, u32[]{:S(2)}, u32[]{:S(2)}) collective-permute-start(bf16[688,8,128]{2,1,0:T(8,128)(2,1)S(1)} %pad_maximum_fusion), channel_id=1, source_target_pairs={{0,6},{1,97},{2,0},{3,99},{4,2},{5,101},{6,4},{7,103},{8,14},{9,10... | collective-permute-start | bytes 4227080 | tf_op jit(solution)/shard_map/ppermute | solution.py:34
  35.5 2.5 %collective-permute-start.19 = (bf16[336,8,128]{2,1,0:T(8,128)(2,1)S(1)}, bf16[336,8,128]{2,1,0:T(8,128)(2,1)}, u32[]{:S(2)}, u32[]{:S(2)}) collective-permute-start(bf16[336,8,128]{2,1,0:T(8,128)(2,1)S(1)} %pad_maximum_fusion.3), channel_id=1, source_target_pairs={{0,24},{1,25},{2,26},{3,27},{4,28},{5,29},{6,30},{7,31},{8,0},{9,1... | collective-permute-start | bytes 2064392 | tf_op jit(solution)/shard_map/ppermute | solution.py:34
  38.0 1.1 collective-permute-start.21
  39.1 1.3 collective-permute-done.6
  40.4 3.5 %collective-permute-start.23 = (bf16[168,8,128]{2,1,0:T(8,128)(2,1)S(1)}, bf16[168,8,128]{2,1,0:T(8,128)(2,1)S(1)}, u32[]{:S(2)}, u32[]{:S(2)}) collective-permute-start(bf16[168,8,128]{2,1,0:T(8,128)(2,1)S(1)} %pad_maximum_fusion.5), channel_id=1, source_target_pairs={{0,8},{1,9},{2,10},{3,11},{4,12},{5,13},{6,14},{7,15},{8,16},{9,17... | collective-permute-start | bytes 1032200 | tf_op jit(solution)/shard_map/ppermute | solution.py:34
  44.0 1.0 constant_dynamic-update-slice_fusion.2
  45.0 11.7 %collective-permute-done.23 = bf16[168,8,128]{2,1,0:T(8,128)(2,1)S(1)} collective-permute-done((bf16[168,8,128]{2,1,0:T(8,128)(2,1)S(1)}, bf16[168,8,128]{2,1,0:T(8,128)(2,1)S(1)}, u32[]{:S(2)}, u32[]{:S(2)}) %collective-permute-start.23) | collective-permute-done | bytes 344096 | tf_op jit(solution)/shard_map/ppermute | solution.py:34
  56.7 5.8 %collective-permute-start.20 = (bf16[336,8,128]{2,1,0:T(8,128)(2,1)S(1)}, bf16[336,8,128]{2,1,0:T(8,128)(2,1)S(1)}, u32[]{:S(2)}, u32[]{:S(2)}) collective-permute-start(bf16[336,8,128]{2,1,0:T(8,128)(2,1)S(1)} %constant_dynamic-update-slice_fusion.3), channel_id=1, source_target_pairs={{0,24},{1,25},{2,26},{3,27},{4,28},{5,29},{6,30},{7,31},{8,0},{9,1... | collective-permute-start | bytes 2064392 | tf_op jit(solution)/shard_map/ppermute | solution.py:34
  62.5 1.2 collective-permute-start.9
  63.7 0.8 constant_dynamic-update-slice_fusion.1
  64.5 0.8 constant_dynamic-update-slice_fusion
  65.3 1.5 collective-permute-start.8
  66.7 0.1 collective-permute-start.29
  66.8 0.1 pad_maximum_fusion.2
  66.9 7.5 %collective-permute-done.29 = bf16[168,8,128]{2,1,0:T(8,128)(2,1)S(1)} collective-permute-done((bf16[168,8,128]{2,1,0:T(8,128)(2,1)S(1)}, bf16[168,8,128]{2,1,0:T(8,128)(2,1)S(1)}, u32[]{:S(2)}, u32[]{:S(2)}) %collective-permute-start.29) | collective-permute-done | bytes 344096 | tf_op jit(solution)/shard_map/ppermute | solution.py:34
  74.4 0.4 collective-permute-start.10
  74.8 1.4 collective-permute-start.11
  76.3 1.2 collective-permute-start.25
  77.5 11.7 %collective-permute-done.10 = bf16[344,8,128]{2,1,0:T(8,128)(2,1)} collective-permute-done((bf16[344,8,128]{2,1,0:T(8,128)(2,1)S(1)}, bf16[344,8,128]{2,1,0:T(8,128)(2,1)}, u32[]{:S(2)}, u32[]{:S(2)}) %collective-permute-start.10) | collective-permute-done | bytes 704544 | tf_op jit(solution)/shard_map/ppermute | solution.py:34
  89.2 0.0 collective-permute-start.26
  89.2 7.5 %collective-permute-done.11 = bf16[344,8,128]{2,1,0:T(8,128)(2,1)} collective-permute-done((bf16[344,8,128]{2,1,0:T(8,128)(2,1)S(1)}, bf16[344,8,128]{2,1,0:T(8,128)(2,1)}, u32[]{:S(2)}, u32[]{:S(2)}) %collective-permute-start.11) | collective-permute-done | bytes 704544 | tf_op jit(solution)/shard_map/ppermute | solution.py:34
  96.7 0.0 collective-permute-start.27
  96.8 1.1 copy-done.4
  97.9 2.4 %collective-permute-start.28 = (bf16[336,8,128]{2,1,0:T(8,128)(2,1)}, bf16[336,8,128]{2,1,0:T(8,128)(2,1)}, u32[]{:S(2)}, u32[]{:S(2)}) collective-permute-start(bf16[336,8,128]{2,1,0:T(8,128)(2,1)} %collective-permute-done.19), channel_id=1, source_target_pairs={{0,24},{1,25},{2,26},{3,27},{4,28},{5,29},{6,30},{7,31},{8,0},{9,1... | collective-permute-start | bytes 2064392 | tf_op jit(solution)/shard_map/ppermute | solution.py:34
  100.3 0.1 collective-permute-start.30
  100.4 0.8 subtract_shift-right-arithmetic_fusion.starts
  101.1 0.8 dynamic_slice.7
  101.9 0.1 reshape.83
  102.0 0.2 shift-right-arithmetic_reduce_fusion
  102.3 8.8 %fetch_near.1 = (bf16[8192,128]{1,0:T(8,128)(2,1)S(1)}, bf16[8192,128]{1,0:T(8,128)(2,1)S(1)}, s32[128]{0:T(128)S(1)}) custom-call(s32[64]{0:T(128)S(1)} %fusion.5.codes, s32[9]{0:T(128)S(1)} %subtract_shift-right-arithmetic_fusion.starts, bf16[5504,128]{1,0:T(8,128)(2,1)} %bitcast.27, bf16[5504,128]{1,0:T(8,128)(2,1)} %bitcast.3.refs_1_, ...), custom_call_target="tpu_custom_call" | custom-call | tf_op jit(solution)/shard_map/fetch_near/pallas_call | solution.py:242
  111.1 0.0 copy-start.9
  111.1 0.7 collective-permute-done.27
  111.8 0.1 copy-done.9
  112.0 22.7 %attend.1 = (bf16[512,1024]{1,0:T(8,128)(2,1)S(1)}, f32[512,128]{1,0:T(8,128)S(1)}, bf16[512,1024]{1,0:T(8,128)(2,1)S(1)}, f32[512,128]{1,0:T(8,128)S(1)}, bf16[...) custom-call(s32[1]{0:T(128)} %bitcast.place, ...), custom_call_target="tpu_custom_call", output_to_operand_aliasing={{4}: (12, {}), {5}: (13, {})} | custom-call | flops 8589934592 | bytes 8388608 | tf_op jit(solution)/shard_map/attend/pallas_call | solution.py:363
  134.7 8.4 %collective-permute-start.31 = (bf16[512,1024]{1,0:T(8,128)(2,1)S(1)}, bf16[512,1024]{1,0:T(8,128)(2,1)S(1)}, u32[]{:S(2)}, u32[]{:S(2)}) collective-permute-start(bf16[512,1024]{1,0:T(8,128)(2,1)S(1)} %get-tuple-element.61), channel_id=1, source_target_pairs={{0,1},{1,0},{2,3},{3,2},{4,5},{5,4},{6,7},{7,6},{8,9},{9,8},{10,11... | collective-permute-start | bytes 3145736 | tf_op jit(solution)/shard_map/ppermute | solution.py:39
  143.1 0.1 collective-permute-start.32
  143.2 2.6 %collective-permute-done.32.stat_b = f32[512,128]{1,0:T(8,128)S(1)} collective-permute-done((f32[512,128]{1,0:T(8,128)S(1)}, f32[512,128]{1,0:T(8,128)S(1)}, u32[]{:S(2)}, u32[]{:S(2)}) %collective-permute-start.32) | collective-permute-done | bytes 262176 | tf_op jit(solution)/shard_map/ppermute | solution.py:39
  145.8 13.5 %project.1 = bf16[512,8192]{1,0:T(8,128)(2,1)} custom-call(bf16[512,1024]{1,0:T(8,128)(2,1)S(1)} %get-tuple-element.59.o_a, f32[512,128]{1,0:T(8,128)S(1)} %get-tuple-element.60.stat_a, bf16[512,1024]{1,0:T(8,128)(2,1)S(1)} %collective-permute-done.31.o_b, f32[512,128]{1,0:T(8,128)S(1)} %collective-permute-done.32.stat_b, bf16[1024,8192]{1,0:T(8,128)(2,1)S(1)} %bitcast.26), custom_call_target="tpu_custom_call" | custom-call | tf_op jit(solution)/shard_map/project/pallas_call | solution.py:435
  (59 shorter events, 0.4 us)
Async XLA Ops:
  0.0 18.1 %copy-start = (bf16[512,1024]{1,0:T(8,128)(2,1)S(1)}, bf16[512,1024]{1,0:T(8,128)(2,1)}, u32[]{:S(2)}) copy-start(bf16[512,1024]{1,0:T(8,128)(2,1)} %own_queries.1) | copy-start | bytes 3145732
  1.0 10.0 %collective-permute-start = (bf16[86,8,128]{2,1,0:T(8,128)(2,1)S(1)}, bf16[86,8,128]{2,1,0:T(8,128)(2,1)S(1)}, u32[]{:S(2)}, u32[]{:S(2)}) collective-permute-start(bf16[86,8,128]{2,1,0:T(8,128)(2,1)S(1)} %fusion), channel_id=1, source_target_pairs={{0,16},{1,5},{2,18},{3,7},{4,20},{5,1},{6,22},{7,3},{8,24},{9,13},... | collective-permute-start | bytes 528392 | tf_op jit(solution)/shard_map/ppermute | solution.py:34
  4.7 7.4 %collective-permute-start.1 = (bf16[86,8,128]{2,1,0:T(8,128)(2,1)S(1)}, bf16[86,8,128]{2,1,0:T(8,128)(2,1)S(1)}, u32[]{:S(2)}, u32[]{:S(2)}) collective-permute-start(bf16[86,8,128]{2,1,0:T(8,128)(2,1)S(1)} %fusion), channel_id=1, source_target_pairs={{0,24},{1,7},{2,26},{3,1},{4,28},{5,3},{6,30},{7,5},{8,0},{9,15},{... | collective-permute-start | bytes 528392 | tf_op jit(solution)/shard_map/ppermute | solution.py:34
  5.5 6.6 %collective-permute-start.2 = (bf16[86,8,128]{2,1,0:T(8,128)(2,1)S(1)}, bf16[86,8,128]{2,1,0:T(8,128)(2,1)S(1)}, u32[]{:S(2)}, u32[]{:S(2)}) collective-permute-start(bf16[86,8,128]{2,1,0:T(8,128)(2,1)S(1)} %fusion), channel_id=1, source_target_pairs={{0,8},{1,3},{2,10},{3,5},{4,12},{5,7},{6,14},{7,1},{8,16},{9,11},{... | collective-permute-start | bytes 528392 | tf_op jit(solution)/shard_map/ppermute | solution.py:34
  7.0 8.0 %collective-permute-start.12 = (bf16[42,8,128]{2,1,0:T(8,128)(2,1)S(1)}, bf16[42,8,128]{2,1,0:T(8,128)(2,1)S(1)}, u32[]{:S(2)}, u32[]{:S(2)}) collective-permute-start(bf16[42,8,128]{2,1,0:T(8,128)(2,1)S(1)} %slice_bitcast_fusion), channel_id=1, source_target_pairs={{0,64},{1,65},{2,66},{3,67},{4,68},{5,69},{6,70},{7,71},{8,72},{9,... | collective-permute-start | bytes 258056 | tf_op jit(solution)/shard_map/ppermute | solution.py:34
  10.6 4.4 %collective-permute-start.13 = (bf16[42,8,128]{2,1,0:T(8,128)(2,1)S(1)}, bf16[42,8,128]{2,1,0:T(8,128)(2,1)S(1)}, u32[]{:S(2)}, u32[]{:S(2)}) collective-permute-start(bf16[42,8,128]{2,1,0:T(8,128)(2,1)S(1)} %slice_bitcast_fusion), channel_id=1, source_target_pairs={{0,96},{1,97},{2,98},{3,99},{4,100},{5,101},{6,102},{7,103},{8,104... | collective-permute-start | bytes 258056 | tf_op jit(solution)/shard_map/ppermute | solution.py:34
  11.1 4.5 %collective-permute-start.14 = (bf16[42,8,128]{2,1,0:T(8,128)(2,1)S(1)}, bf16[42,8,128]{2,1,0:T(8,128)(2,1)S(1)}, u32[]{:S(2)}, u32[]{:S(2)}) collective-permute-start(bf16[42,8,128]{2,1,0:T(8,128)(2,1)S(1)} %slice_bitcast_fusion), channel_id=1, source_target_pairs={{0,32},{1,33},{2,34},{3,35},{4,36},{5,37},{6,38},{7,39},{8,40},{9,... | collective-permute-start | bytes 258056 | tf_op jit(solution)/shard_map/ppermute | solution.py:34
  12.2 15.1 %collective-permute-start.3 = (bf16[344,8,128]{2,1,0:T(8,128)(2,1)S(1)}, bf16[344,8,128]{2,1,0:T(8,128)(2,1)S(1)}, u32[]{:S(2)}, u32[]{:S(2)}) collective-permute-start(bf16[344,8,128]{2,1,0:T(8,128)(2,1)S(1)} %pad_maximum_fusion.1), channel_id=1, source_target_pairs={{0,96},{1,25},{2,98},{3,27},{4,100},{5,29},{6,102},{7,31},{8,104},... | collective-permute-start | bytes 2113544 | tf_op jit(solution)/shard_map/ppermute | solution.py:34
  15.0 13.4 %collective-permute-start.4 = (bf16[344,8,128]{2,1,0:T(8,128)(2,1)S(1)}, bf16[344,8,128]{2,1,0:T(8,128)(2,1)S(1)}, u32[]{:S(2)}, u32[]{:S(2)}) collective-permute-start(bf16[344,8,128]{2,1,0:T(8,128)(2,1)S(1)} %pad_maximum_fusion.1), channel_id=1, source_target_pairs={{0,32},{1,9},{2,34},{3,11},{4,36},{5,13},{6,38},{7,15},{8,40},{9,1... | collective-permute-start | bytes 2113544 | tf_op jit(solution)/shard_map/ppermute | solution.py:34
  15.7 6.6 %collective-permute-start.15 = (bf16[168,8,128]{2,1,0:T(8,128)(2,1)S(1)}, bf16[168,8,128]{2,1,0:T(8,128)(2,1)S(1)}, u32[]{:S(2)}, u32[]{:S(2)}) collective-permute-start(bf16[168,8,128]{2,1,0:T(8,128)(2,1)S(1)} %pad_maximum_fusion.4), channel_id=1, source_target_pairs={{0,6},{1,7},{2,0},{3,1},{4,2},{5,3},{6,4},{7,5},{8,14},{9,15},{10,... | collective-permute-start | bytes 1032200 | tf_op jit(solution)/shard_map/ppermute | solution.py:34
  18.1 7.6 %collective-permute-start.16 = (bf16[168,8,128]{2,1,0:T(8,128)(2,1)S(1)}, bf16[168,8,128]{2,1,0:T(8,128)(2,1)S(1)}, u32[]{:S(2)}, u32[]{:S(2)}) collective-permute-start(bf16[168,8,128]{2,1,0:T(8,128)(2,1)S(1)} %pad_maximum_fusion.4), channel_id=1, source_target_pairs={{0,2},{1,3},{2,4},{3,5},{4,6},{5,7},{6,0},{7,1},{8,10},{9,11},{10,... | collective-permute-start | bytes 1032200 | tf_op jit(solution)/shard_map/ppermute | solution.py:34
  18.1 44.4 %collective-permute-start.24 = (bf16[512,1024]{1,0:T(8,128)(2,1)S(1)}, bf16[512,1024]{1,0:T(8,128)(2,1)S(1)}, u32[]{:S(2)}, u32[]{:S(2)}) collective-permute-start(bf16[512,1024]{1,0:T(8,128)(2,1)S(1)} %copy-done), channel_id=1, source_target_pairs={{0,1},{1,0},{2,3},{3,2},{4,5},{5,4},{6,7},{7,6},{8,9},{9,8},{10,11... | collective-permute-start | bytes 3145736 | tf_op jit(solution)/shard_map/ppermute | solution.py:39
  25.8 12.2 %copy-start.2 = (bf16[336,8,128]{2,1,0:T(8,128)(2,1)}, bf16[336,8,128]{2,1,0:T(8,128)(2,1)S(1)}, u32[]{:S(2)}) copy-start(bf16[336,8,128]{2,1,0:T(8,128)(2,1)S(1)} %pad_maximum_fusion.3) | copy-start | bytes 2064388
  25.8 4.5 %collective-permute-start.17 = (bf16[84,8,128]{2,1,0:T(8,128)(2,1)S(1)}, bf16[84,8,128]{2,1,0:T(8,128)(2,1)S(1)}, u32[]{:S(2)}, u32[]{:S(2)}) collective-permute-start(bf16[84,8,128]{2,1,0:T(8,128)(2,1)S(1)} %slice.30), channel_id=1, source_target_pairs={{0,6},{1,7},{2,0},{3,1},{4,2},{5,3},{6,4},{7,5},{8,14},{9,15},{10,... | collective-permute-start | bytes 516104 | tf_op jit(solution)/shard_map/ppermute | solution.py:34
  25.9 6.8 %collective-permute-start.18 = (bf16[84,8,128]{2,1,0:T(8,128)(2,1)S(1)}, bf16[84,8,128]{2,1,0:T(8,128)(2,1)S(1)}, u32[]{:S(2)}, u32[]{:S(2)}) collective-permute-start(bf16[84,8,128]{2,1,0:T(8,128)(2,1)S(1)} %slice.31), channel_id=1, source_target_pairs={{0,2},{1,3},{2,4},{3,5},{4,6},{5,7},{6,0},{7,1},{8,10},{9,11},{10,... | collective-permute-start | bytes 516104 | tf_op jit(solution)/shard_map/ppermute | solution.py:34
  27.3 8.1 %collective-permute-start.22 = (bf16[168,8,128]{2,1,0:T(8,128)(2,1)S(1)}, bf16[168,8,128]{2,1,0:T(8,128)(2,1)S(1)}, u32[]{:S(2)}, u32[]{:S(2)}) collective-permute-start(bf16[168,8,128]{2,1,0:T(8,128)(2,1)S(1)} %collective-permute-done.16), channel_id=1, source_target_pairs={{0,8},{1,9},{2,10},{3,11},{4,12},{5,13},{6,14},{7,15},{8,16},{9,17... | collective-permute-start | bytes 1032200 | tf_op jit(solution)/shard_map/ppermute | solution.py:34
  28.6 33.9 %copy-start.1 = (bf16[688,8,128]{2,1,0:T(8,128)(2,1)}, bf16[688,8,128]{2,1,0:T(8,128)(2,1)S(1)}, u32[]{:S(2)}) copy-start(bf16[688,8,128]{2,1,0:T(8,128)(2,1)S(1)} %pad_maximum_fusion) | copy-start | bytes 4227076
  28.6 9.4 %collective-permute-start.5 = (bf16[172,8,128]{2,1,0:T(8,128)(2,1)S(1)}, bf16[172,8,128]{2,1,0:T(8,128)(2,1)S(1)}, u32[]{:S(2)}, u32[]{:S(2)}) collective-permute-start(bf16[172,8,128]{2,1,0:T(8,128)(2,1)S(1)} %slice.27), channel_id=1, source_target_pairs={{0,96},{1,25},{2,98},{3,27},{4,100},{5,29},{6,102},{7,31},{8,104},... | collective-permute-start | bytes 1056776 | tf_op jit(solution)/shard_map/ppermute | solution.py:34
  30.3 10.1 %collective-permute-start.6 = (bf16[172,8,128]{2,1,0:T(8,128)(2,1)S(1)}, bf16[172,8,128]{2,1,0:T(8,128)(2,1)S(1)}, u32[]{:S(2)}, u32[]{:S(2)}) collective-permute-start(bf16[172,8,128]{2,1,0:T(8,128)(2,1)S(1)} %slice.28), channel_id=1, source_target_pairs={{0,32},{1,9},{2,34},{3,11},{4,36},{5,13},{6,38},{7,15},{8,40},{9,1... | collective-permute-start | bytes 1056776 | tf_op jit(solution)/shard_map/ppermute | solution.py:34
  32.7 43.6 %collective-permute-start.7 = (bf16[688,8,128]{2,1,0:T(8,128)(2,1)S(1)}, bf16[688,8,128]{2,1,0:T(8,128)(2,1)}, u32[]{:S(2)}, u32[]{:S(2)}) collective-permute-start(bf16[688,8,128]{2,1,0:T(8,128)(2,1)S(1)} %pad_maximum_fusion), channel_id=1, source_target_pairs={{0,6},{1,97},{2,0},{3,99},{4,2},{5,101},{6,4},{7,103},{8,14},{9,10... | collective-permute-start | bytes 4227080 | tf_op jit(solution)/shard_map/ppermute | solution.py:34
  35.4 31.3 %copy-start.7 = (bf16[168,8,128]{2,1,0:T(8,128)(2,1)}, bf16[168,8,128]{2,1,0:T(8,128)(2,1)S(1)}, u32[]{:S(2)}) copy-start(bf16[168,8,128]{2,1,0:T(8,128)(2,1)S(1)} %collective-permute-done.22) | copy-start | bytes 1032196
  35.5 29.8 %collective-permute-start.19 = (bf16[336,8,128]{2,1,0:T(8,128)(2,1)S(1)}, bf16[336,8,128]{2,1,0:T(8,128)(2,1)}, u32[]{:S(2)}, u32[]{:S(2)}) collective-permute-start(bf16[336,8,128]{2,1,0:T(8,128)(2,1)S(1)} %pad_maximum_fusion.3), channel_id=1, source_target_pairs={{0,24},{1,25},{2,26},{3,27},{4,28},{5,29},{6,30},{7,31},{8,0},{9,1... | collective-permute-start | bytes 2064392 | tf_op jit(solution)/shard_map/ppermute | solution.py:34
  38.0 28.7 %collective-permute-start.21 = (bf16[336,8,128]{2,1,0:T(8,128)(2,1)S(1)}, bf16[336,8,128]{2,1,0:T(8,128)(2,1)S(1)}, u32[]{:S(2)}, u32[]{:S(2)}) collective-permute-start(bf16[336,8,128]{2,1,0:T(8,128)(2,1)S(1)} %pad_maximum_fusion.3), channel_id=1, source_target_pairs={{0,8},{1,9},{2,10},{3,11},{4,12},{5,13},{6,14},{7,15},{8,16},{9,17... | collective-permute-start | bytes 2064392 | tf_op jit(solution)/shard_map/ppermute | solution.py:34
  40.4 16.2 %collective-permute-start.23 = (bf16[168,8,128]{2,1,0:T(8,128)(2,1)S(1)}, bf16[168,8,128]{2,1,0:T(8,128)(2,1)S(1)}, u32[]{:S(2)}, u32[]{:S(2)}) collective-permute-start(bf16[168,8,128]{2,1,0:T(8,128)(2,1)S(1)} %pad_maximum_fusion.5), channel_id=1, source_target_pairs={{0,8},{1,9},{2,10},{3,11},{4,12},{5,13},{6,14},{7,15},{8,16},{9,17... | collective-permute-start | bytes 1032200 | tf_op jit(solution)/shard_map/ppermute | solution.py:34
  44.0 21.3 %copy-start.3 = (bf16[336,8,128]{2,1,0:T(8,128)(2,1)}, bf16[336,8,128]{2,1,0:T(8,128)(2,1)S(1)}, u32[]{:S(2)}) copy-start(bf16[336,8,128]{2,1,0:T(8,128)(2,1)S(1)} %constant_dynamic-update-slice_fusion.3) | copy-start | bytes 2064388
  56.7 43.6 %copy-start.8 = (bf16[168,8,128]{2,1,0:T(8,128)(2,1)}, bf16[168,8,128]{2,1,0:T(8,128)(2,1)S(1)}, u32[]{:S(2)}) copy-start(bf16[168,8,128]{2,1,0:T(8,128)(2,1)S(1)} %collective-permute-done.23) | copy-start | bytes 1032196
  56.7 18.2 %collective-permute-start.20 = (bf16[336,8,128]{2,1,0:T(8,128)(2,1)S(1)}, bf16[336,8,128]{2,1,0:T(8,128)(2,1)S(1)}, u32[]{:S(2)}, u32[]{:S(2)}) collective-permute-start(bf16[336,8,128]{2,1,0:T(8,128)(2,1)S(1)} %constant_dynamic-update-slice_fusion.3), channel_id=1, source_target_pairs={{0,24},{1,25},{2,26},{3,27},{4,28},{5,29},{6,30},{7,31},{8,0},{9,1... | collective-permute-start | bytes 2064392 | tf_op jit(solution)/shard_map/ppermute | solution.py:34
  62.5 34.2 %collective-permute-start.9 = (bf16[688,8,128]{2,1,0:T(8,128)(2,1)S(1)}, bf16[688,8,128]{2,1,0:T(8,128)(2,1)S(1)}, u32[]{:S(2)}, u32[]{:S(2)}) collective-permute-start(bf16[688,8,128]{2,1,0:T(8,128)(2,1)S(1)} %pad_maximum_fusion), channel_id=1, source_target_pairs={{0,2},{1,33},{2,4},{3,35},{4,6},{5,37},{6,0},{7,39},{8,10},{9,41},... | collective-permute-start | bytes 4227080 | tf_op jit(solution)/shard_map/ppermute | solution.py:34
  65.3 35.0 %collective-permute-start.8 = (bf16[688,8,128]{2,1,0:T(8,128)(2,1)}, bf16[688,8,128]{2,1,0:T(8,128)(2,1)}, u32[]{:S(2)}, u32[]{:S(2)}) collective-permute-start(bf16[688,8,128]{2,1,0:T(8,128)(2,1)} %constant_dynamic-update-slice_fusion), channel_id=1, source_target_pairs={{0,6},{1,97},{2,0},{3,99},{4,2},{5,101},{6,4},{7,103},{8,14},{9,10... | collective-permute-start | bytes 4227080 | tf_op jit(solution)/shard_map/ppermute | solution.py:34
  66.7 33.5 %copy-start.5 = (bf16[336,8,128]{2,1,0:T(8,128)(2,1)}, bf16[336,8,128]{2,1,0:T(8,128)(2,1)S(1)}, u32[]{:S(2)}) copy-start(bf16[336,8,128]{2,1,0:T(8,128)(2,1)S(1)} %collective-permute-done.21) | copy-start | bytes 2064388
  66.7 7.7 %collective-permute-start.29 = (bf16[168,8,128]{2,1,0:T(8,128)(2,1)S(1)}, bf16[168,8,128]{2,1,0:T(8,128)(2,1)S(1)}, u32[]{:S(2)}, u32[]{:S(2)}) collective-permute-start(bf16[168,8,128]{2,1,0:T(8,128)(2,1)S(1)} %collective-permute-done.22), channel_id=1, source_target_pairs={{0,8},{1,9},{2,10},{3,11},{4,12},{5,13},{6,14},{7,15},{8,16},{9,17... | collective-permute-start | bytes 1032200 | tf_op jit(solution)/shard_map/ppermute | solution.py:34
  74.4 36.7 %copy-start.10 = (bf16[168,8,128]{2,1,0:T(8,128)(2,1)}, bf16[168,8,128]{2,1,0:T(8,128)(2,1)S(1)}, u32[]{:S(2)}) copy-start(bf16[168,8,128]{2,1,0:T(8,128)(2,1)S(1)} %collective-permute-done.29) | copy-start | bytes 1032196
  74.4 14.8 %collective-permute-start.10 = (bf16[344,8,128]{2,1,0:T(8,128)(2,1)S(1)}, bf16[344,8,128]{2,1,0:T(8,128)(2,1)}, u32[]{:S(2)}, u32[]{:S(2)}) collective-permute-start(bf16[344,8,128]{2,1,0:T(8,128)(2,1)S(1)} %collective-permute-done.4), channel_id=1, source_target_pairs={{0,2},{1,33},{2,4},{3,35},{4,6},{5,37},{6,0},{7,39},{8,10},{9,41},... | collective-permute-start | bytes 2113544 | tf_op jit(solution)/shard_map/ppermute | solution.py:34
  74.8 25.4 %copy-start.6 = (bf16[336,8,128]{2,1,0:T(8,128)(2,1)}, bf16[336,8,128]{2,1,0:T(8,128)(2,1)S(1)}, u32[]{:S(2)}) copy-start(bf16[336,8,128]{2,1,0:T(8,128)(2,1)S(1)} %collective-permute-done.20) | copy-start | bytes 2064388
  74.8 21.9 %collective-permute-start.11 = (bf16[344,8,128]{2,1,0:T(8,128)(2,1)S(1)}, bf16[344,8,128]{2,1,0:T(8,128)(2,1)}, u32[]{:S(2)}, u32[]{:S(2)}) collective-permute-start(bf16[344,8,128]{2,1,0:T(8,128)(2,1)S(1)} %pad_maximum_fusion.2), channel_id=1, source_target_pairs={{0,2},{1,33},{2,4},{3,35},{4,6},{5,37},{6,0},{7,39},{8,10},{9,41},... | collective-permute-start | bytes 2113544 | tf_op jit(solution)/shard_map/ppermute | solution.py:34
  76.3 35.6 %collective-permute-start.25 = (bf16[688,8,128]{2,1,0:T(8,128)(2,1)}, bf16[688,8,128]{2,1,0:T(8,128)(2,1)}, u32[]{:S(2)}, u32[]{:S(2)}) collective-permute-start(bf16[688,8,128]{2,1,0:T(8,128)(2,1)} %collective-permute-done.7), channel_id=1, source_target_pairs={{0,6},{1,97},{2,0},{3,99},{4,2},{5,101},{6,4},{7,103},{8,14},{9,10... | collective-permute-start | bytes 4227080 | tf_op jit(solution)/shard_map/ppermute | solution.py:34
  89.2 21.9 %collective-permute-start.26 = (bf16[344,8,128]{2,1,0:T(8,128)(2,1)}, bf16[344,8,128]{2,1,0:T(8,128)(2,1)S(1)}, u32[]{:S(2)}, u32[]{:S(2)}) collective-permute-start(bf16[344,8,128]{2,1,0:T(8,128)(2,1)} %collective-permute-done.10), channel_id=1, source_target_pairs={{0,2},{1,33},{2,4},{3,35},{4,6},{5,37},{6,0},{7,39},{8,10},{9,41},... | collective-permute-start | bytes 2113544 | tf_op jit(solution)/shard_map/ppermute | solution.py:34
  96.7 15.1 %collective-permute-start.27 = (bf16[344,8,128]{2,1,0:T(8,128)(2,1)}, bf16[344,8,128]{2,1,0:T(8,128)(2,1)}, u32[]{:S(2)}, u32[]{:S(2)}) collective-permute-start(bf16[344,8,128]{2,1,0:T(8,128)(2,1)} %collective-permute-done.11), channel_id=1, source_target_pairs={{0,2},{1,33},{2,4},{3,35},{4,6},{5,37},{6,0},{7,39},{8,10},{9,41},... | collective-permute-start | bytes 2113544 | tf_op jit(solution)/shard_map/ppermute | solution.py:34
  96.8 1.1 copy-start.4
  97.9 13.2 %collective-permute-start.28 = (bf16[336,8,128]{2,1,0:T(8,128)(2,1)}, bf16[336,8,128]{2,1,0:T(8,128)(2,1)}, u32[]{:S(2)}, u32[]{:S(2)}) collective-permute-start(bf16[336,8,128]{2,1,0:T(8,128)(2,1)} %collective-permute-done.19), channel_id=1, source_target_pairs={{0,24},{1,25},{2,26},{3,27},{4,28},{5,29},{6,30},{7,31},{8,0},{9,1... | collective-permute-start | bytes 2064392 | tf_op jit(solution)/shard_map/ppermute | solution.py:34
  100.3 10.8 %collective-permute-start.30 = (bf16[168,8,128]{2,1,0:T(8,128)(2,1)S(1)}, bf16[168,8,128]{2,1,0:T(8,128)(2,1)}, u32[]{:S(2)}, u32[]{:S(2)}) collective-permute-start(bf16[168,8,128]{2,1,0:T(8,128)(2,1)S(1)} %collective-permute-done.23), channel_id=1, source_target_pairs={{0,8},{1,9},{2,10},{3,11},{4,12},{5,13},{6,14},{7,15},{8,16},{9,17... | collective-permute-start | bytes 1032200 | tf_op jit(solution)/shard_map/ppermute | solution.py:34
  111.1 0.9 copy-start.9
  111.8 33.9 %slice-start = ((s8[16777216]{0:T(1024)(128)(4,1)}), s8[4194304]{0:T(1024)(128)(4,1)S(1)}, s32[]{:S(2)}) async-start(s8[16777216]{0:T(1024)(128)(4,1)} %bitcast.25), calls=%async_computation | async-start | bytes 8388608
  112.0 33.8 %slice-start.1 = ((s8[16777216]{0:T(1024)(128)(4,1)}), s8[4194304]{0:T(1024)(128)(4,1)S(1)}, s32[]{:S(2)}) async-start(s8[16777216]{0:T(1024)(128)(4,1)} %bitcast.25), calls=%async_computation.1 | async-start | bytes 8388608
  112.0 33.8 %slice-start.2 = ((s8[16777216]{0:T(1024)(128)(4,1)}), s8[4194304]{0:T(1024)(128)(4,1)S(1)}, s32[]{:S(2)}) async-start(s8[16777216]{0:T(1024)(128)(4,1)} %bitcast.25), calls=%async_computation.2 | async-start | bytes 8388608
  112.0 33.8 %slice-start.3 = ((s8[16777216]{0:T(1024)(128)(4,1)}), s8[4194304]{0:T(1024)(128)(4,1)S(1)}, s32[]{:S(2)}) async-start(s8[16777216]{0:T(1024)(128)(4,1)} %bitcast.25), calls=%async_computation.3 | async-start | bytes 8388608
  134.7 11.1 %collective-permute-start.31 = (bf16[512,1024]{1,0:T(8,128)(2,1)S(1)}, bf16[512,1024]{1,0:T(8,128)(2,1)S(1)}, u32[]{:S(2)}, u32[]{:S(2)}) collective-permute-start(bf16[512,1024]{1,0:T(8,128)(2,1)S(1)} %get-tuple-element.61), channel_id=1, source_target_pairs={{0,1},{1,0},{2,3},{3,2},{4,5},{5,4},{6,7},{7,6},{8,9},{9,8},{10,11... | collective-permute-start | bytes 3145736 | tf_op jit(solution)/shard_map/ppermute | solution.py:39
  143.1 2.7 %collective-permute-start.32 = (f32[512,128]{1,0:T(8,128)S(1)}, f32[512,128]{1,0:T(8,128)S(1)}, u32[]{:S(2)}, u32[]{:S(2)}) collective-permute-start(f32[512,128]{1,0:T(8,128)S(1)} %get-tuple-element.62), channel_id=1, source_target_pairs={{0,1},{1,0},{2,3},{3,2},{4,5},{5,4},{6,7},{7,6},{8,9},{9,8},{10,11... | collective-permute-start | bytes 786440 | tf_op jit(solution)/shard_map/ppermute | solution.py:39

commit v3 on v2

--- a/solution.py
+++ b/solution.py
@@ -11,7 +11,7 @@
 RPD = 8
 AVG = 16
 SHARD = 512
-BIG = 688
+BIG = 672
 SMALL = 2 * SHARD - BIG
 SPLIT = BIG - SHARD - BLOCK
 QUADS = 4
@@ -148,22 +148,22 @@
 
         def from_big(piece):
             row = big_chunk * BIG
-            copy(big[piece], row + within * BLOCK, BLOCK, kbuf, at, sems.at[0, index]).start()
+            copy(big[piece], row + within * BLOCK, BLOCK, kbuf, at, sems.at[index]).start()
 
             @pl.when(within == 0)
             def _():
-                copy(big[piece], row + SHARD, BLOCK, vbuf, at, sems.at[1, index]).start()
+                copy(big[piece], row + SHARD, BLOCK, vbuf, at, sems.at[index]).start()
 
             @pl.when(within == 1)
             def _():
-                copy(big[piece], row + SHARD + BLOCK, SPLIT, vbuf, at, sems.at[1, index]).start()
+                copy(big[piece], row + SHARD + BLOCK, SPLIT, vbuf, at, sems.at[index]).start()
 
         def from_small(piece):
             row = small_chunk * SMALL
 
             @pl.when(within == 1)
             def _():
-                copy(small[piece], row, BLOCK - SPLIT, vbuf, at + SPLIT, sems.at[2, index]).start()
+                copy(small[piece], row, BLOCK - SPLIT, vbuf, at + SPLIT, sems.at[index]).start()
 
             @pl.when(within >= 2)
             def _():
@@ -173,7 +173,7 @@
                     BLOCK,
                     vbuf,
                     at,
-                    sems.at[2, index],
+                    sems.at[index],
                 ).start()
 
         pl.when(has(big_piece))(lambda: choose(big_piece - first_piece, count, from_big))
@@ -182,29 +182,15 @@
         )
 
     def finish(index):
-        big_piece, _, small_piece, _, within, at = parts(index)
-
-        @pl.when(has(big_piece))
-        def _():
-            copy(big[1], 0, BLOCK, kbuf, at, sems.at[0, index]).wait()
-
-            @pl.when(within == 0)
+        big_piece, _, small_piece, _, within, _ = parts(index)
+        from_big = BLOCK + jnp.where(within == 0, BLOCK, jnp.where(within == 1, SPLIT, 0))
+        from_small = jnp.where(within == 0, 0, jnp.where(within == 1, BLOCK - SPLIT, BLOCK))
+        rows = jnp.where(has(big_piece), from_big, 0) + jnp.where(has(small_piece), from_small, 0)
+        for number in sorted({BLOCK - SPLIT, BLOCK, BLOCK + SPLIT, 2 * BLOCK}):
+
+            @pl.when(rows == number)
             def _():
-                copy(big[1], 0, BLOCK, vbuf, at, sems.at[1, index]).wait()
-
-            @pl.when(within == 1)
-            def _():
-                copy(big[1], 0, SPLIT, vbuf, at, sems.at[1, index]).wait()
-
-        @pl.when(has(small_piece))
-        def _():
-            @pl.when(within == 1)
-            def _():
-                copy(small[1], 0, BLOCK - SPLIT, vbuf, at + SPLIT, sems.at[2, index]).wait()
-
-            @pl.when(within >= 2)
-            def _():
-                copy(small[1], 0, BLOCK, vbuf, at, sems.at[2, index]).wait()
+                copy(big[1], 0, number, kbuf, 0, sems.at[index]).wait()
 
     return parts, has, issue, finish
 
@@ -245,7 +231,7 @@
         in_specs=[smem, smem, *[hbm] * (2 * NEAR)],
         out_shape=(blocks, blocks, jax.ShapeDtypeStruct((2 * SLOTS,), jnp.int32)),
         out_specs=(vmem, vmem, smem),
-        scratch_shapes=[pltpu.SemaphoreType.DMA((3, SLOTS))],
+        scratch_shapes=[pltpu.SemaphoreType.DMA((SLOTS,))],
         compiler_params=pltpu.CompilerParams(vmem_limit_bytes=10 * 2**20),
     )(codes, starts, *big[:NEAR], *small[:NEAR])
 
@@ -289,8 +275,12 @@
                 qs[rows_of(head), :] = queries[local, columns_of(head)]
 
         lax.cond(mine, lambda: take(own_queries), lambda: take(their_queries))
-        m_ref[...] = jnp.full(m_ref.shape, -1e30, jnp.float32)
-        acc[...] = jnp.zeros(acc.shape, jnp.float32)
+
+        @pl.when(number == 0)
+        def _():
+            m_ref[...] = jnp.full(m_ref.shape, -1e30, jnp.float32)
+            acc[...] = jnp.zeros(acc.shape, jnp.float32)
+
 
         def score(slot, into, count):
             keys = jnp.concatenate(blocks_of(kbuf, slot, stop, count), axis=0)
@@ -298,7 +288,7 @@
                 qs[...], keys, (((1,), (1,)), ((), ())), preferred_element_type=jnp.float32
             )
             columns = [scores[:, k * BLOCK : (k + 1) * BLOCK] for k in range(count)]
-            top = m_ref[...]
+            top = jnp.where(slot == begin, -1e30, m_ref[...])
             for column in columns:
                 top = jnp.maximum(top, column)
             m_ref[...] = top
@@ -319,7 +309,8 @@
                 ],
                 axis=1,
             )
-            acc[...] += jnp.dot(weights, values, preferred_element_type=jnp.float32)
+            before = jnp.where(slot == begin, 0.0, acc[...])
+            acc[...] = before + jnp.dot(weights, values, preferred_element_type=jnp.float32)
 
         def each_quad(step):
             def body(quad, _):
@@ -372,7 +363,7 @@
             pltpu.VMEM((QUADS, HEADS * BLOCK, 4 * BLOCK), jnp.float32),
             pltpu.VMEM((HEADS * BLOCK, BLOCK), jnp.float32),
             pltpu.VMEM((HEADS * BLOCK, 2 * HEAD_DIM), jnp.float32),
-            pltpu.SemaphoreType.DMA((3, SLOTS)),
+            pltpu.SemaphoreType.DMA((SLOTS,)),
         ],
         cost_estimate=pl.CostEstimate(
             flops=8 * SLOTS * HEADS * BLOCK * BLOCK * HEAD_DIM,

time: 160 us -> 156 us (0.975)
  starting transfers between devices: 58.4 us -> 54.1 us
  waiting for transfers between devices: 47.4 us -> 50.9 us
  Pallas kernels: 45 us -> 41.8 us
    ppermute x3, starting transfers between devices: 12.3 us -> 5.87 us  [swap(): return lax.ppermute(array, ('row', 'col'), pairs)]
    ppermute x30, waiting for transfers between devices: 44.9 us -> 48.3 us  [send(): return lax.ppermute(array, ('row', 'col'), pairs)]
    ppermute x30, starting transfers between devices: 46.1 us -> 48.3 us  [send(): return lax.ppermute(array, ('row', 'col'), pairs)]
    pallas_call x1, Pallas kernels: 22.7 us -> 20.9 us  [attention_call(): pl.pallas_call(attend, name='attend', out_shape=(out, stat, out, stat, bl...]
  transfers between devices with their start and end apart: 33 -> 33, of which waited for: 10 -> 14; matrix products, arithmetic and copies ran while one was open for 4% -> 4% of each run, Pallas kernels for 6% -> 5%
where the time goes in v3:
time: 156 us; the launch traced here: 155 us
  starting transfers between devices  54.1 us (35%)
  waiting for transfers between devices  50.9 us (33%)
  Pallas kernels  41.8 us (27%)
  local copies, waits for them, and re-layouts  5.6 us (4%)
  other arithmetic  2.35 us (2%)
    ppermute x30, waiting for transfers between devices, send(): return lax.ppermute(array, ('row', 'col'), pairs)  48.3 us
    ppermute x30, starting transfers between devices, send(): return lax.ppermute(array, ('row', 'col'), pairs)  48.3 us
    pallas_call x1, Pallas kernels, attention_call(): pl.pallas_call(attend, name='attend', out_shape=(out, stat, out, stat, bl...  20.9 us
    pallas_call x1, Pallas kernels, projection_call(): pl.pallas_call(project, name='project', grid=(width // tile,), out_shape=...  13.5 us
    pallas_call x1, Pallas kernels, fetched(): pl.pallas_call(fetch_near, name='fetch_near', in_specs=[smem, smem, *[hbm...  7.37 us
    ppermute x3, starting transfers between devices, swap(): return lax.ppermute(array, ('row', 'col'), pairs)  5.87 us
  transfers between devices with their start and end apart: 33, of which 14 were waited for; matrix products, arithmetic and copies ran while one was open for 4% of the time, Pallas kernels for 5%

profile of v3, /device:TPU:1, one launch (start us, length us, event | category | flops | bytes accessed | tf_op | source)
XLA Modules:
  0.0 155.1 jit_solution(3567830096635270758)
XLA Ops:
  0.0 1.0 slice_bitcast_fusion
  1.0 4.4 %collective-permute-start.12 = (bf16[44,8,128]{2,1,0:T(8,128)(2,1)S(1)}, bf16[44,8,128]{2,1,0:T(8,128)(2,1)S(1)}, u32[]{:S(2)}, u32[]{:S(2)}) collective-permute-start(bf16[44,8,128]{2,1,0:T(8,128)(2,1)S(1)} %slice_bitcast_fusion), channel_id=1, source_target_pairs={{0,64},{1,65},{2,66},{3,67},{4,68},{5,69},{6,70},{7,71},{8,72},{9,... | collective-permute-start | bytes 270344 | tf_op jit(solution)/shard_map/ppermute | solution.py:34
  5.4 0.4 collective-permute-start.13
  5.8 1.0 collective-permute-start.14
  6.9 0.9 fusion
  7.8 2.8 %collective-permute-start = (bf16[84,8,128]{2,1,0:T(8,128)(2,1)S(1)}, bf16[84,8,128]{2,1,0:T(8,128)(2,1)S(1)}, u32[]{:S(2)}, u32[]{:S(2)}) collective-permute-start(bf16[84,8,128]{2,1,0:T(8,128)(2,1)S(1)} %fusion), channel_id=1, source_target_pairs={{0,16},{1,5},{2,18},{3,7},{4,20},{5,1},{6,22},{7,3},{8,24},{9,13},... | collective-permute-start | bytes 516104 | tf_op jit(solution)/shard_map/ppermute | solution.py:34
  10.6 0.9 collective-permute-start.1
  11.5 0.0 collective-permute-done.12
  11.5 0.6 collective-permute-start.2
  12.1 0.0 collective-permute-done.13
  12.1 0.0 collective-permute-done.14
  12.2 2.1 %collective-permute-start.15 = (bf16[176,8,128]{2,1,0:T(8,128)(2,1)S(1)}, bf16[176,8,128]{2,1,0:T(8,128)(2,1)S(1)}, u32[]{:S(2)}, u32[]{:S(2)}) collective-permute-start(bf16[176,8,128]{2,1,0:T(8,128)(2,1)S(1)} %pad_maximum_fusion.4), channel_id=1, source_target_pairs={{0,6},{1,7},{2,0},{3,1},{4,2},{5,3},{6,4},{7,5},{8,14},{9,15},{10,... | collective-permute-start | bytes 1081352 | tf_op jit(solution)/shard_map/ppermute | solution.py:34
  14.3 1.6 %collective-permute-done.1 = bf16[84,8,128]{2,1,0:T(8,128)(2,1)S(1)} collective-permute-done((bf16[84,8,128]{2,1,0:T(8,128)(2,1)S(1)}, bf16[84,8,128]{2,1,0:T(8,128)(2,1)S(1)}, u32[]{:S(2)}, u32[]{:S(2)}) %collective-permute-start.1) | collective-permute-done | bytes 172064 | tf_op jit(solution)/shard_map/ppermute | solution.py:34
  15.9 1.1 collective-permute-done.2
  17.0 0.1 pad_maximum_fusion.2
  17.1 3.1 %collective-permute-start.3 = (bf16[336,8,128]{2,1,0:T(8,128)(2,1)S(1)}, bf16[336,8,128]{2,1,0:T(8,128)(2,1)S(1)}, u32[]{:S(2)}, u32[]{:S(2)}) collective-permute-start(bf16[336,8,128]{2,1,0:T(8,128)(2,1)S(1)} %pad_maximum_fusion.2), channel_id=1, source_target_pairs={{0,96},{1,25},{2,98},{3,27},{4,100},{5,29},{6,102},{7,31},{8,104},... | collective-permute-start | bytes 2064392 | tf_op jit(solution)/shard_map/ppermute | solution.py:34
  20.2 0.0 collective-permute-start.4
  20.2 2.3 %collective-permute-start.24 = (bf16[512,1024]{1,0:T(8,128)(2,1)S(1)}, bf16[512,1024]{1,0:T(8,128)(2,1)S(1)}, u32[]{:S(2)}, u32[]{:S(2)}) collective-permute-start(bf16[512,1024]{1,0:T(8,128)(2,1)S(1)} %copy-done), channel_id=1, source_target_pairs={{0,1},{1,0},{2,3},{3,2},{4,5},{5,4},{6,7},{7,6},{8,9},{9,8},{10,11... | collective-permute-start | bytes 3145736 | tf_op jit(solution)/shard_map/ppermute | solution.py:39
  22.5 0.1 pad_maximum_fusion.1
  22.6 2.5 %collective-permute-start.17 = (bf16[88,8,128]{2,1,0:T(8,128)(2,1)S(1)}, bf16[88,8,128]{2,1,0:T(8,128)(2,1)S(1)}, u32[]{:S(2)}, u32[]{:S(2)}) collective-permute-start(bf16[88,8,128]{2,1,0:T(8,128)(2,1)S(1)} %slice.30), channel_id=1, source_target_pairs={{0,6},{1,7},{2,0},{3,1},{4,2},{5,3},{6,4},{7,5},{8,14},{9,15},{10,... | collective-permute-start | bytes 540680 | tf_op jit(solution)/shard_map/ppermute | solution.py:34
  25.2 2.4 %collective-permute-done.17 = bf16[88,8,128]{2,1,0:T(8,128)(2,1)S(1)} collective-permute-done((bf16[88,8,128]{2,1,0:T(8,128)(2,1)S(1)}, bf16[88,8,128]{2,1,0:T(8,128)(2,1)S(1)}, u32[]{:S(2)}, u32[]{:S(2)}) %collective-permute-start.17) | collective-permute-done | bytes 180256 | tf_op jit(solution)/shard_map/ppermute | solution.py:34
  27.6 1.7 %collective-permute-start.22 = (bf16[176,8,128]{2,1,0:T(8,128)(2,1)S(1)}, bf16[176,8,128]{2,1,0:T(8,128)(2,1)S(1)}, u32[]{:S(2)}, u32[]{:S(2)}) collective-permute-start(bf16[176,8,128]{2,1,0:T(8,128)(2,1)S(1)} %collective-permute-done.16), channel_id=1, source_target_pairs={{0,8},{1,9},{2,10},{3,11},{4,12},{5,13},{6,14},{7,15},{8,16},{9,17... | collective-permute-start | bytes 1081352 | tf_op jit(solution)/shard_map/ppermute | solution.py:34
  29.3 1.7 %collective-permute-done.18 = bf16[88,8,128]{2,1,0:T(8,128)(2,1)S(1)} collective-permute-done((bf16[88,8,128]{2,1,0:T(8,128)(2,1)S(1)}, bf16[88,8,128]{2,1,0:T(8,128)(2,1)S(1)}, u32[]{:S(2)}, u32[]{:S(2)}) %collective-permute-start.18) | collective-permute-done | bytes 180256 | tf_op jit(solution)/shard_map/ppermute | solution.py:34
  31.0 0.6 collective-permute-start.23
  31.7 0.1 pad_maximum_fusion
  31.8 0.0 copy-start.1
  31.8 3.4 %collective-permute-start.7 = (bf16[672,8,128]{2,1,0:T(8,128)(2,1)S(1)}, bf16[672,8,128]{2,1,0:T(8,128)(2,1)}, u32[]{:S(2)}, u32[]{:S(2)}) collective-permute-start(bf16[672,8,128]{2,1,0:T(8,128)(2,1)S(1)} %pad_maximum_fusion), channel_id=1, source_target_pairs={{0,6},{1,97},{2,0},{3,99},{4,2},{5,101},{6,4},{7,103},{8,14},{9,10... | collective-permute-start | bytes 4128776 | tf_op jit(solution)/shard_map/ppermute | solution.py:34
  35.2 2.6 %collective-permute-start.5 = (bf16[168,8,128]{2,1,0:T(8,128)(2,1)S(1)}, bf16[168,8,128]{2,1,0:T(8,128)(2,1)S(1)}, u32[]{:S(2)}, u32[]{:S(2)}) collective-permute-start(bf16[168,8,128]{2,1,0:T(8,128)(2,1)S(1)} %slice.27), channel_id=1, source_target_pairs={{0,96},{1,25},{2,98},{3,27},{4,100},{5,29},{6,102},{7,31},{8,104},... | collective-permute-start | bytes 1032200 | tf_op jit(solution)/shard_map/ppermute | solution.py:34
  37.9 0.1 collective-permute-start.19
  38.0 4.7 %collective-permute-done.23 = bf16[176,8,128]{2,1,0:T(8,128)(2,1)S(1)} collective-permute-done((bf16[176,8,128]{2,1,0:T(8,128)(2,1)S(1)}, bf16[176,8,128]{2,1,0:T(8,128)(2,1)S(1)}, u32[]{:S(2)}, u32[]{:S(2)}) %collective-permute-start.23) | collective-permute-done | bytes 360480 | tf_op jit(solution)/shard_map/ppermute | solution.py:34
  42.7 1.2 collective-permute-start.6
  44.0 2.4 %collective-permute-start.29 = (bf16[176,8,128]{2,1,0:T(8,128)(2,1)S(1)}, bf16[176,8,128]{2,1,0:T(8,128)(2,1)S(1)}, u32[]{:S(2)}, u32[]{:S(2)}) collective-permute-start(bf16[176,8,128]{2,1,0:T(8,128)(2,1)S(1)} %collective-permute-done.22), channel_id=1, source_target_pairs={{0,8},{1,9},{2,10},{3,11},{4,12},{5,13},{6,14},{7,15},{8,16},{9,17... | collective-permute-start | bytes 1081352 | tf_op jit(solution)/shard_map/ppermute | solution.py:34
  46.4 0.1 collective-permute-start.21
  46.5 4.2 %collective-permute-done.6 = bf16[168,8,128]{2,1,0:T(8,128)(2,1)S(1)} collective-permute-done((bf16[168,8,128]{2,1,0:T(8,128)(2,1)S(1)}, bf16[168,8,128]{2,1,0:T(8,128)(2,1)S(1)}, u32[]{:S(2)}, u32[]{:S(2)}) %collective-permute-start.6) | collective-permute-done | bytes 344096 | tf_op jit(solution)/shard_map/ppermute | solution.py:34
  50.7 1.9 %collective-permute-start.20 = (bf16[352,8,128]{2,1,0:T(8,128)(2,1)S(1)}, bf16[352,8,128]{2,1,0:T(8,128)(2,1)S(1)}, u32[]{:S(2)}, u32[]{:S(2)}) collective-permute-start(bf16[352,8,128]{2,1,0:T(8,128)(2,1)S(1)} %constant_dynamic-update-slice_fusion.3), channel_id=1, source_target_pairs={{0,24},{1,25},{2,26},{3,27},{4,28},{5,29},{6,30},{7,31},{8,0},{9,1... | collective-permute-start | bytes 2162696 | tf_op jit(solution)/shard_map/ppermute | solution.py:34
  52.6 0.9 constant_dynamic-update-slice_fusion.2
  53.5 2.6 %collective-permute-done.29 = bf16[176,8,128]{2,1,0:T(8,128)(2,1)S(1)} collective-permute-done((bf16[176,8,128]{2,1,0:T(8,128)(2,1)S(1)}, bf16[176,8,128]{2,1,0:T(8,128)(2,1)S(1)}, u32[]{:S(2)}, u32[]{:S(2)}) %collective-permute-start.29) | collective-permute-done | bytes 360480 | tf_op jit(solution)/shard_map/ppermute | solution.py:34
  56.1 1.2 collective-permute-start.9
  57.3 0.8 constant_dynamic-update-slice_fusion.1
  58.0 0.8 constant_dynamic-update-slice_fusion
  58.8 7.0 %collective-permute-start.8 = (bf16[672,8,128]{2,1,0:T(8,128)(2,1)}, bf16[672,8,128]{2,1,0:T(8,128)(2,1)}, u32[]{:S(2)}, u32[]{:S(2)}) collective-permute-start(bf16[672,8,128]{2,1,0:T(8,128)(2,1)} %constant_dynamic-update-slice_fusion), channel_id=1, source_target_pairs={{0,6},{1,97},{2,0},{3,99},{4,2},{5,101},{6,4},{7,103},{8,14},{9,10... | collective-permute-start | bytes 4128776 | tf_op jit(solution)/shard_map/ppermute | solution.py:34
  65.8 5.7 %collective-permute-done.21 = bf16[352,8,128]{2,1,0:T(8,128)(2,1)S(1)} collective-permute-done((bf16[352,8,128]{2,1,0:T(8,128)(2,1)S(1)}, bf16[352,8,128]{2,1,0:T(8,128)(2,1)S(1)}, u32[]{:S(2)}, u32[]{:S(2)}) %collective-permute-start.21) | collective-permute-done | bytes 720928 | tf_op jit(solution)/shard_map/ppermute | solution.py:34
  71.5 1.2 collective-permute-start.10
  72.7 0.1 pad_maximum_fusion.3
  72.8 0.1 collective-permute-start.11
  72.9 6.7 %collective-permute-start.25 = (bf16[672,8,128]{2,1,0:T(8,128)(2,1)}, bf16[672,8,128]{2,1,0:T(8,128)(2,1)}, u32[]{:S(2)}, u32[]{:S(2)}) collective-permute-start(bf16[672,8,128]{2,1,0:T(8,128)(2,1)} %collective-permute-done.7), channel_id=1, source_target_pairs={{0,6},{1,97},{2,0},{3,99},{4,2},{5,101},{6,4},{7,103},{8,14},{9,10... | collective-permute-start | bytes 4128776 | tf_op jit(solution)/shard_map/ppermute | solution.py:34
  79.6 8.5 %collective-permute-done.10 = bf16[336,8,128]{2,1,0:T(8,128)(2,1)} collective-permute-done((bf16[336,8,128]{2,1,0:T(8,128)(2,1)S(1)}, bf16[336,8,128]{2,1,0:T(8,128)(2,1)}, u32[]{:S(2)}, u32[]{:S(2)}) %collective-permute-start.10) | collective-permute-done | bytes 688160 | tf_op jit(solution)/shard_map/ppermute | solution.py:34
  88.1 7.4 %collective-permute-done.11 = bf16[336,8,128]{2,1,0:T(8,128)(2,1)} collective-permute-done((bf16[336,8,128]{2,1,0:T(8,128)(2,1)S(1)}, bf16[336,8,128]{2,1,0:T(8,128)(2,1)}, u32[]{:S(2)}, u32[]{:S(2)}) %collective-permute-start.11) | collective-permute-done | bytes 688160 | tf_op jit(solution)/shard_map/ppermute | solution.py:34
  95.5 1.1 copy-done.4
  96.6 0.0 collective-permute-start.27
  96.6 0.1 collective-permute-start.30
  96.7 0.8 subtract_shift-right-arithmetic_fusion.starts
  97.5 0.8 dynamic_slice.7
  98.2 0.1 reshape.83
  98.4 0.2 shift-right-arithmetic_reduce_fusion
  98.6 7.4 %fetch_near.1 = (bf16[8192,128]{1,0:T(8,128)(2,1)S(1)}, bf16[8192,128]{1,0:T(8,128)(2,1)S(1)}, s32[128]{0:T(128)S(1)}) custom-call(s32[64]{0:T(128)S(1)} %fusion.5.codes, s32[9]{0:T(128)S(1)} %subtract_shift-right-arithmetic_fusion.starts, bf16[5376,128]{1,0:T(8,128)(2,1)} %bitcast.27, bf16[5376,128]{1,0:T(8,128)(2,1)} %bitcast.3.refs_1_, ...), custom_call_target="tpu_custom_call" | custom-call | tf_op jit(solution)/shard_map/fetch_near/pallas_call | solution.py:228
  106.0 0.6 collective-permute-done.30
  106.6 0.5 collective-permute-done.26
  107.1 7.4 %collective-permute-done.27 = bf16[336,8,128]{2,1,0:T(8,128)(2,1)} collective-permute-done((bf16[336,8,128]{2,1,0:T(8,128)(2,1)}, bf16[336,8,128]{2,1,0:T(8,128)(2,1)}, u32[]{:S(2)}, u32[]{:S(2)}) %collective-permute-start.27) | collective-permute-done | bytes 688160 | tf_op jit(solution)/shard_map/ppermute | solution.py:34
  114.5 20.9 %attend.1 = (bf16[512,1024]{1,0:T(8,128)(2,1)S(1)}, f32[512,128]{1,0:T(8,128)S(1)}, bf16[512,1024]{1,0:T(8,128)(2,1)S(1)}, f32[512,128]{1,0:T(8,128)S(1)}, bf16[...) custom-call(s32[1]{0:T(128)} %bitcast.place, ...), custom_call_target="tpu_custom_call", output_to_operand_aliasing={{4}: (12, {}), {5}: (13, {})} | custom-call | flops 8589934592 | bytes 8388608 | tf_op jit(solution)/shard_map/attend/pallas_call | solution.py:354
  135.4 3.5 %collective-permute-start.31 = (bf16[512,1024]{1,0:T(8,128)(2,1)S(1)}, bf16[512,1024]{1,0:T(8,128)(2,1)S(1)}, u32[]{:S(2)}, u32[]{:S(2)}) collective-permute-start(bf16[512,1024]{1,0:T(8,128)(2,1)S(1)} %get-tuple-element.61), channel_id=1, source_target_pairs={{0,1},{1,0},{2,3},{3,2},{4,5},{5,4},{6,7},{7,6},{8,9},{9,8},{10,11... | collective-permute-start | bytes 3145736 | tf_op jit(solution)/shard_map/ppermute | solution.py:39
  138.9 0.1 collective-permute-start.32
  139.0 2.6 %collective-permute-done.32.stat_b = f32[512,128]{1,0:T(8,128)S(1)} collective-permute-done((f32[512,128]{1,0:T(8,128)S(1)}, f32[512,128]{1,0:T(8,128)S(1)}, u32[]{:S(2)}, u32[]{:S(2)}) %collective-permute-start.32) | collective-permute-done | bytes 262176 | tf_op jit(solution)/shard_map/ppermute | solution.py:39
  141.6 13.5 %project.1 = bf16[512,8192]{1,0:T(8,128)(2,1)} custom-call(bf16[512,1024]{1,0:T(8,128)(2,1)S(1)} %get-tuple-element.59.o_a, f32[512,128]{1,0:T(8,128)S(1)} %get-tuple-element.60.stat_a, bf16[512,1024]{1,0:T(8,128)(2,1)S(1)} %collective-permute-done.31.o_b, f32[512,128]{1,0:T(8,128)S(1)} %collective-permute-done.32.stat_b, bf16[1024,8192]{1,0:T(8,128)(2,1)S(1)} %bitcast.26), custom_call_target="tpu_custom_call" | custom-call | tf_op jit(solution)/shard_map/project/pallas_call | solution.py:426
  (59 shorter events, 0.4 us)
Async XLA Ops:
  0.0 20.2 %copy-start = (bf16[512,1024]{1,0:T(8,128)(2,1)S(1)}, bf16[512,1024]{1,0:T(8,128)(2,1)}, u32[]{:S(2)}) copy-start(bf16[512,1024]{1,0:T(8,128)(2,1)} %own_queries.1) | copy-start | bytes 3145732
  1.0 10.5 %collective-permute-start.12 = (bf16[44,8,128]{2,1,0:T(8,128)(2,1)S(1)}, bf16[44,8,128]{2,1,0:T(8,128)(2,1)S(1)}, u32[]{:S(2)}, u32[]{:S(2)}) collective-permute-start(bf16[44,8,128]{2,1,0:T(8,128)(2,1)S(1)} %slice_bitcast_fusion), channel_id=1, source_target_pairs={{0,64},{1,65},{2,66},{3,67},{4,68},{5,69},{6,70},{7,71},{8,72},{9,... | collective-permute-start | bytes 270344 | tf_op jit(solution)/shard_map/ppermute | solution.py:34
  5.4 6.7 %collective-permute-start.13 = (bf16[44,8,128]{2,1,0:T(8,128)(2,1)S(1)}, bf16[44,8,128]{2,1,0:T(8,128)(2,1)S(1)}, u32[]{:S(2)}, u32[]{:S(2)}) collective-permute-start(bf16[44,8,128]{2,1,0:T(8,128)(2,1)S(1)} %slice_bitcast_fusion), channel_id=1, source_target_pairs={{0,96},{1,97},{2,98},{3,99},{4,100},{5,101},{6,102},{7,103},{8,104... | collective-permute-start | bytes 270344 | tf_op jit(solution)/shard_map/ppermute | solution.py:34
  5.8 6.3 %collective-permute-start.14 = (bf16[44,8,128]{2,1,0:T(8,128)(2,1)S(1)}, bf16[44,8,128]{2,1,0:T(8,128)(2,1)S(1)}, u32[]{:S(2)}, u32[]{:S(2)}) collective-permute-start(bf16[44,8,128]{2,1,0:T(8,128)(2,1)S(1)} %slice_bitcast_fusion), channel_id=1, source_target_pairs={{0,32},{1,33},{2,34},{3,35},{4,36},{5,37},{6,38},{7,39},{8,40},{9,... | collective-permute-start | bytes 270344 | tf_op jit(solution)/shard_map/ppermute | solution.py:34
  7.8 6.5 %collective-permute-start = (bf16[84,8,128]{2,1,0:T(8,128)(2,1)S(1)}, bf16[84,8,128]{2,1,0:T(8,128)(2,1)S(1)}, u32[]{:S(2)}, u32[]{:S(2)}) collective-permute-start(bf16[84,8,128]{2,1,0:T(8,128)(2,1)S(1)} %fusion), channel_id=1, source_target_pairs={{0,16},{1,5},{2,18},{3,7},{4,20},{5,1},{6,22},{7,3},{8,24},{9,13},... | collective-permute-start | bytes 516104 | tf_op jit(solution)/shard_map/ppermute | solution.py:34
  10.6 5.2 %collective-permute-start.1 = (bf16[84,8,128]{2,1,0:T(8,128)(2,1)S(1)}, bf16[84,8,128]{2,1,0:T(8,128)(2,1)S(1)}, u32[]{:S(2)}, u32[]{:S(2)}) collective-permute-start(bf16[84,8,128]{2,1,0:T(8,128)(2,1)S(1)} %fusion), channel_id=1, source_target_pairs={{0,24},{1,7},{2,26},{3,1},{4,28},{5,3},{6,30},{7,5},{8,0},{9,15},{... | collective-permute-start | bytes 516104 | tf_op jit(solution)/shard_map/ppermute | solution.py:34
  11.5 5.5 %collective-permute-start.2 = (bf16[84,8,128]{2,1,0:T(8,128)(2,1)S(1)}, bf16[84,8,128]{2,1,0:T(8,128)(2,1)S(1)}, u32[]{:S(2)}, u32[]{:S(2)}) collective-permute-start(bf16[84,8,128]{2,1,0:T(8,128)(2,1)S(1)} %fusion), channel_id=1, source_target_pairs={{0,8},{1,3},{2,10},{3,5},{4,12},{5,7},{6,14},{7,1},{8,16},{9,11},{... | collective-permute-start | bytes 516104 | tf_op jit(solution)/shard_map/ppermute | solution.py:34
  12.2 10.3 %collective-permute-start.15 = (bf16[176,8,128]{2,1,0:T(8,128)(2,1)S(1)}, bf16[176,8,128]{2,1,0:T(8,128)(2,1)S(1)}, u32[]{:S(2)}, u32[]{:S(2)}) collective-permute-start(bf16[176,8,128]{2,1,0:T(8,128)(2,1)S(1)} %pad_maximum_fusion.4), channel_id=1, source_target_pairs={{0,6},{1,7},{2,0},{3,1},{4,2},{5,3},{6,4},{7,5},{8,14},{9,15},{10,... | collective-permute-start | bytes 1081352 | tf_op jit(solution)/shard_map/ppermute | solution.py:34
  14.3 8.2 %collective-permute-start.16 = (bf16[176,8,128]{2,1,0:T(8,128)(2,1)S(1)}, bf16[176,8,128]{2,1,0:T(8,128)(2,1)S(1)}, u32[]{:S(2)}, u32[]{:S(2)}) collective-permute-start(bf16[176,8,128]{2,1,0:T(8,128)(2,1)S(1)} %pad_maximum_fusion.4), channel_id=1, source_target_pairs={{0,2},{1,3},{2,4},{3,5},{4,6},{5,7},{6,0},{7,1},{8,10},{9,11},{10,... | collective-permute-start | bytes 1081352 | tf_op jit(solution)/shard_map/ppermute | solution.py:34
  17.1 14.6 %collective-permute-start.3 = (bf16[336,8,128]{2,1,0:T(8,128)(2,1)S(1)}, bf16[336,8,128]{2,1,0:T(8,128)(2,1)S(1)}, u32[]{:S(2)}, u32[]{:S(2)}) collective-permute-start(bf16[336,8,128]{2,1,0:T(8,128)(2,1)S(1)} %pad_maximum_fusion.2), channel_id=1, source_target_pairs={{0,96},{1,25},{2,98},{3,27},{4,100},{5,29},{6,102},{7,31},{8,104},... | collective-permute-start | bytes 2064392 | tf_op jit(solution)/shard_map/ppermute | solution.py:34
  20.2 11.5 %collective-permute-start.4 = (bf16[336,8,128]{2,1,0:T(8,128)(2,1)S(1)}, bf16[336,8,128]{2,1,0:T(8,128)(2,1)S(1)}, u32[]{:S(2)}, u32[]{:S(2)}) collective-permute-start(bf16[336,8,128]{2,1,0:T(8,128)(2,1)S(1)} %pad_maximum_fusion.2), channel_id=1, source_target_pairs={{0,32},{1,9},{2,34},{3,11},{4,36},{5,13},{6,38},{7,15},{8,40},{9,1... | collective-permute-start | bytes 2064392 | tf_op jit(solution)/shard_map/ppermute | solution.py:34
  20.2 23.8 %collective-permute-start.24 = (bf16[512,1024]{1,0:T(8,128)(2,1)S(1)}, bf16[512,1024]{1,0:T(8,128)(2,1)S(1)}, u32[]{:S(2)}, u32[]{:S(2)}) collective-permute-start(bf16[512,1024]{1,0:T(8,128)(2,1)S(1)} %copy-done), channel_id=1, source_target_pairs={{0,1},{1,0},{2,3},{3,2},{4,5},{5,4},{6,7},{7,6},{8,9},{9,8},{10,11... | collective-permute-start | bytes 3145736 | tf_op jit(solution)/shard_map/ppermute | solution.py:39
  22.6 23.8 %copy-start.2 = (bf16[352,8,128]{2,1,0:T(8,128)(2,1)}, bf16[352,8,128]{2,1,0:T(8,128)(2,1)S(1)}, u32[]{:S(2)}) copy-start(bf16[352,8,128]{2,1,0:T(8,128)(2,1)S(1)} %pad_maximum_fusion.1) | copy-start | bytes 2162692
  22.6 5.0 %collective-permute-start.17 = (bf16[88,8,128]{2,1,0:T(8,128)(2,1)S(1)}, bf16[88,8,128]{2,1,0:T(8,128)(2,1)S(1)}, u32[]{:S(2)}, u32[]{:S(2)}) collective-permute-start(bf16[88,8,128]{2,1,0:T(8,128)(2,1)S(1)} %slice.30), channel_id=1, source_target_pairs={{0,6},{1,7},{2,0},{3,1},{4,2},{5,3},{6,4},{7,5},{8,14},{9,15},{10,... | collective-permute-start | bytes 540680 | tf_op jit(solution)/shard_map/ppermute | solution.py:34
  25.1 5.9 %collective-permute-start.18 = (bf16[88,8,128]{2,1,0:T(8,128)(2,1)S(1)}, bf16[88,8,128]{2,1,0:T(8,128)(2,1)S(1)}, u32[]{:S(2)}, u32[]{:S(2)}) collective-permute-start(bf16[88,8,128]{2,1,0:T(8,128)(2,1)S(1)} %slice.31), channel_id=1, source_target_pairs={{0,2},{1,3},{2,4},{3,5},{4,6},{5,7},{6,0},{7,1},{8,10},{9,11},{10,... | collective-permute-start | bytes 540680 | tf_op jit(solution)/shard_map/ppermute | solution.py:34
  27.6 10.3 %collective-permute-start.22 = (bf16[176,8,128]{2,1,0:T(8,128)(2,1)S(1)}, bf16[176,8,128]{2,1,0:T(8,128)(2,1)S(1)}, u32[]{:S(2)}, u32[]{:S(2)}) collective-permute-start(bf16[176,8,128]{2,1,0:T(8,128)(2,1)S(1)} %collective-permute-done.16), channel_id=1, source_target_pairs={{0,8},{1,9},{2,10},{3,11},{4,12},{5,13},{6,14},{7,15},{8,16},{9,17... | collective-permute-start | bytes 1081352 | tf_op jit(solution)/shard_map/ppermute | solution.py:34
  31.0 11.7 %collective-permute-start.23 = (bf16[176,8,128]{2,1,0:T(8,128)(2,1)S(1)}, bf16[176,8,128]{2,1,0:T(8,128)(2,1)S(1)}, u32[]{:S(2)}, u32[]{:S(2)}) collective-permute-start(bf16[176,8,128]{2,1,0:T(8,128)(2,1)S(1)} %pad_maximum_fusion.5), channel_id=1, source_target_pairs={{0,8},{1,9},{2,10},{3,11},{4,12},{5,13},{6,14},{7,15},{8,16},{9,17... | collective-permute-start | bytes 1081352 | tf_op jit(solution)/shard_map/ppermute | solution.py:34
  31.8 24.3 %copy-start.1 = (bf16[672,8,128]{2,1,0:T(8,128)(2,1)}, bf16[672,8,128]{2,1,0:T(8,128)(2,1)S(1)}, u32[]{:S(2)}) copy-start(bf16[672,8,128]{2,1,0:T(8,128)(2,1)S(1)} %pad_maximum_fusion) | copy-start | bytes 4128772
  31.8 41.1 %collective-permute-start.7 = (bf16[672,8,128]{2,1,0:T(8,128)(2,1)S(1)}, bf16[672,8,128]{2,1,0:T(8,128)(2,1)}, u32[]{:S(2)}, u32[]{:S(2)}) collective-permute-start(bf16[672,8,128]{2,1,0:T(8,128)(2,1)S(1)} %pad_maximum_fusion), channel_id=1, source_target_pairs={{0,6},{1,97},{2,0},{3,99},{4,2},{5,101},{6,4},{7,103},{8,14},{9,10... | collective-permute-start | bytes 4128776 | tf_op jit(solution)/shard_map/ppermute | solution.py:34
  35.2 11.1 %collective-permute-start.5 = (bf16[168,8,128]{2,1,0:T(8,128)(2,1)S(1)}, bf16[168,8,128]{2,1,0:T(8,128)(2,1)S(1)}, u32[]{:S(2)}, u32[]{:S(2)}) collective-permute-start(bf16[168,8,128]{2,1,0:T(8,128)(2,1)S(1)} %slice.27), channel_id=1, source_target_pairs={{0,96},{1,25},{2,98},{3,27},{4,100},{5,29},{6,102},{7,31},{8,104},... | collective-permute-start | bytes 1032200 | tf_op jit(solution)/shard_map/ppermute | solution.py:34
  37.9 15.6 %copy-start.7 = (bf16[176,8,128]{2,1,0:T(8,128)(2,1)}, bf16[176,8,128]{2,1,0:T(8,128)(2,1)S(1)}, u32[]{:S(2)}) copy-start(bf16[176,8,128]{2,1,0:T(8,128)(2,1)S(1)} %collective-permute-done.22) | copy-start | bytes 1081348
  37.9 20.9 %collective-permute-start.19 = (bf16[352,8,128]{2,1,0:T(8,128)(2,1)S(1)}, bf16[352,8,128]{2,1,0:T(8,128)(2,1)}, u32[]{:S(2)}, u32[]{:S(2)}) collective-permute-start(bf16[352,8,128]{2,1,0:T(8,128)(2,1)S(1)} %pad_maximum_fusion.1), channel_id=1, source_target_pairs={{0,24},{1,25},{2,26},{3,27},{4,28},{5,29},{6,30},{7,31},{8,0},{9,1... | collective-permute-start | bytes 2162696 | tf_op jit(solution)/shard_map/ppermute | solution.py:34
  42.7 53.9 %copy-start.8 = (bf16[176,8,128]{2,1,0:T(8,128)(2,1)}, bf16[176,8,128]{2,1,0:T(8,128)(2,1)S(1)}, u32[]{:S(2)}) copy-start(bf16[176,8,128]{2,1,0:T(8,128)(2,1)S(1)} %collective-permute-done.23) | copy-start | bytes 1081348
  42.7 8.0 %collective-permute-start.6 = (bf16[168,8,128]{2,1,0:T(8,128)(2,1)S(1)}, bf16[168,8,128]{2,1,0:T(8,128)(2,1)S(1)}, u32[]{:S(2)}, u32[]{:S(2)}) collective-permute-start(bf16[168,8,128]{2,1,0:T(8,128)(2,1)S(1)} %slice.28), channel_id=1, source_target_pairs={{0,32},{1,9},{2,34},{3,11},{4,36},{5,13},{6,38},{7,15},{8,40},{9,1... | collective-permute-start | bytes 1032200 | tf_op jit(solution)/shard_map/ppermute | solution.py:34
  44.0 12.1 %collective-permute-start.29 = (bf16[176,8,128]{2,1,0:T(8,128)(2,1)S(1)}, bf16[176,8,128]{2,1,0:T(8,128)(2,1)S(1)}, u32[]{:S(2)}, u32[]{:S(2)}) collective-permute-start(bf16[176,8,128]{2,1,0:T(8,128)(2,1)S(1)} %collective-permute-done.22), channel_id=1, source_target_pairs={{0,8},{1,9},{2,10},{3,11},{4,12},{5,13},{6,14},{7,15},{8,16},{9,17... | collective-permute-start | bytes 1081352 | tf_op jit(solution)/shard_map/ppermute | solution.py:34
  46.4 25.1 %collective-permute-start.21 = (bf16[352,8,128]{2,1,0:T(8,128)(2,1)S(1)}, bf16[352,8,128]{2,1,0:T(8,128)(2,1)S(1)}, u32[]{:S(2)}, u32[]{:S(2)}) collective-permute-start(bf16[352,8,128]{2,1,0:T(8,128)(2,1)S(1)} %pad_maximum_fusion.1), channel_id=1, source_target_pairs={{0,8},{1,9},{2,10},{3,11},{4,12},{5,13},{6,14},{7,15},{8,16},{9,17... | collective-permute-start | bytes 2162696 | tf_op jit(solution)/shard_map/ppermute | solution.py:34
  46.5 12.3 %copy-start.3 = (bf16[352,8,128]{2,1,0:T(8,128)(2,1)}, bf16[352,8,128]{2,1,0:T(8,128)(2,1)S(1)}, u32[]{:S(2)}) copy-start(bf16[352,8,128]{2,1,0:T(8,128)(2,1)S(1)} %constant_dynamic-update-slice_fusion.3) | copy-start | bytes 2162692
  50.7 22.1 %collective-permute-start.20 = (bf16[352,8,128]{2,1,0:T(8,128)(2,1)S(1)}, bf16[352,8,128]{2,1,0:T(8,128)(2,1)S(1)}, u32[]{:S(2)}, u32[]{:S(2)}) collective-permute-start(bf16[352,8,128]{2,1,0:T(8,128)(2,1)S(1)} %constant_dynamic-update-slice_fusion.3), channel_id=1, source_target_pairs={{0,24},{1,25},{2,26},{3,27},{4,28},{5,29},{6,30},{7,31},{8,0},{9,1... | collective-permute-start | bytes 2162696 | tf_op jit(solution)/shard_map/ppermute | solution.py:34
  56.1 16.7 %copy-start.10 = (bf16[176,8,128]{2,1,0:T(8,128)(2,1)}, bf16[176,8,128]{2,1,0:T(8,128)(2,1)S(1)}, u32[]{:S(2)}) copy-start(bf16[176,8,128]{2,1,0:T(8,128)(2,1)S(1)} %collective-permute-done.29) | copy-start | bytes 1081348
  56.1 39.4 %collective-permute-start.9 = (bf16[672,8,128]{2,1,0:T(8,128)(2,1)S(1)}, bf16[672,8,128]{2,1,0:T(8,128)(2,1)S(1)}, u32[]{:S(2)}, u32[]{:S(2)}) collective-permute-start(bf16[672,8,128]{2,1,0:T(8,128)(2,1)S(1)} %pad_maximum_fusion), channel_id=1, source_target_pairs={{0,2},{1,33},{2,4},{3,35},{4,6},{5,37},{6,0},{7,39},{8,10},{9,41},... | collective-permute-start | bytes 4128776 | tf_op jit(solution)/shard_map/ppermute | solution.py:34
  58.8 37.8 %collective-permute-start.8 = (bf16[672,8,128]{2,1,0:T(8,128)(2,1)}, bf16[672,8,128]{2,1,0:T(8,128)(2,1)}, u32[]{:S(2)}, u32[]{:S(2)}) collective-permute-start(bf16[672,8,128]{2,1,0:T(8,128)(2,1)} %constant_dynamic-update-slice_fusion), channel_id=1, source_target_pairs={{0,6},{1,97},{2,0},{3,99},{4,2},{5,101},{6,4},{7,103},{8,14},{9,10... | collective-permute-start | bytes 4128776 | tf_op jit(solution)/shard_map/ppermute | solution.py:34
  71.5 25.1 %copy-start.5 = (bf16[352,8,128]{2,1,0:T(8,128)(2,1)}, bf16[352,8,128]{2,1,0:T(8,128)(2,1)S(1)}, u32[]{:S(2)}) copy-start(bf16[352,8,128]{2,1,0:T(8,128)(2,1)S(1)} %collective-permute-done.21) | copy-start | bytes 2162692
  71.5 16.6 %collective-permute-start.10 = (bf16[336,8,128]{2,1,0:T(8,128)(2,1)S(1)}, bf16[336,8,128]{2,1,0:T(8,128)(2,1)}, u32[]{:S(2)}, u32[]{:S(2)}) collective-permute-start(bf16[336,8,128]{2,1,0:T(8,128)(2,1)S(1)} %collective-permute-done.4), channel_id=1, source_target_pairs={{0,2},{1,33},{2,4},{3,35},{4,6},{5,37},{6,0},{7,39},{8,10},{9,41},... | collective-permute-start | bytes 2064392 | tf_op jit(solution)/shard_map/ppermute | solution.py:34
  72.8 23.8 %copy-start.6 = (bf16[352,8,128]{2,1,0:T(8,128)(2,1)}, bf16[352,8,128]{2,1,0:T(8,128)(2,1)S(1)}, u32[]{:S(2)}) copy-start(bf16[352,8,128]{2,1,0:T(8,128)(2,1)S(1)} %collective-permute-done.20) | copy-start | bytes 2162692
  72.8 22.7 %collective-permute-start.11 = (bf16[336,8,128]{2,1,0:T(8,128)(2,1)S(1)}, bf16[336,8,128]{2,1,0:T(8,128)(2,1)}, u32[]{:S(2)}, u32[]{:S(2)}) collective-permute-start(bf16[336,8,128]{2,1,0:T(8,128)(2,1)S(1)} %pad_maximum_fusion.3), channel_id=1, source_target_pairs={{0,2},{1,33},{2,4},{3,35},{4,6},{5,37},{6,0},{7,39},{8,10},{9,41},... | collective-permute-start | bytes 2064392 | tf_op jit(solution)/shard_map/ppermute | solution.py:34
  72.9 41.6 %collective-permute-start.25 = (bf16[672,8,128]{2,1,0:T(8,128)(2,1)}, bf16[672,8,128]{2,1,0:T(8,128)(2,1)}, u32[]{:S(2)}, u32[]{:S(2)}) collective-permute-start(bf16[672,8,128]{2,1,0:T(8,128)(2,1)} %collective-permute-done.7), channel_id=1, source_target_pairs={{0,6},{1,97},{2,0},{3,99},{4,2},{5,101},{6,4},{7,103},{8,14},{9,10... | collective-permute-start | bytes 4128776 | tf_op jit(solution)/shard_map/ppermute | solution.py:34
  88.1 18.5 %collective-permute-start.28 = (bf16[352,8,128]{2,1,0:T(8,128)(2,1)}, bf16[352,8,128]{2,1,0:T(8,128)(2,1)S(1)}, u32[]{:S(2)}, u32[]{:S(2)}) collective-permute-start(bf16[352,8,128]{2,1,0:T(8,128)(2,1)} %collective-permute-done.19), channel_id=1, source_target_pairs={{0,24},{1,25},{2,26},{3,27},{4,28},{5,29},{6,30},{7,31},{8,0},{9,1... | collective-permute-start | bytes 2162696 | tf_op jit(solution)/shard_map/ppermute | solution.py:34
  95.5 11.6 %collective-permute-start.26 = (bf16[336,8,128]{2,1,0:T(8,128)(2,1)}, bf16[336,8,128]{2,1,0:T(8,128)(2,1)}, u32[]{:S(2)}, u32[]{:S(2)}) collective-permute-start(bf16[336,8,128]{2,1,0:T(8,128)(2,1)} %collective-permute-done.10), channel_id=1, source_target_pairs={{0,2},{1,33},{2,4},{3,35},{4,6},{5,37},{6,0},{7,39},{8,10},{9,41},... | collective-permute-start | bytes 2064392 | tf_op jit(solution)/shard_map/ppermute | solution.py:34
  95.5 1.1 copy-start.4
  96.6 17.9 %collective-permute-start.27 = (bf16[336,8,128]{2,1,0:T(8,128)(2,1)}, bf16[336,8,128]{2,1,0:T(8,128)(2,1)}, u32[]{:S(2)}, u32[]{:S(2)}) collective-permute-start(bf16[336,8,128]{2,1,0:T(8,128)(2,1)} %collective-permute-done.11), channel_id=1, source_target_pairs={{0,2},{1,33},{2,4},{3,35},{4,6},{5,37},{6,0},{7,39},{8,10},{9,41},... | collective-permute-start | bytes 2064392 | tf_op jit(solution)/shard_map/ppermute | solution.py:34
  96.6 10.0 %collective-permute-start.30 = (bf16[176,8,128]{2,1,0:T(8,128)(2,1)S(1)}, bf16[176,8,128]{2,1,0:T(8,128)(2,1)}, u32[]{:S(2)}, u32[]{:S(2)}) collective-permute-start(bf16[176,8,128]{2,1,0:T(8,128)(2,1)S(1)} %collective-permute-done.23), channel_id=1, source_target_pairs={{0,8},{1,9},{2,10},{3,11},{4,12},{5,13},{6,14},{7,15},{8,16},{9,17... | collective-permute-start | bytes 1081352 | tf_op jit(solution)/shard_map/ppermute | solution.py:34
  106.6 7.9 %copy-start.9 = (bf16[352,8,128]{2,1,0:T(8,128)(2,1)}, bf16[352,8,128]{2,1,0:T(8,128)(2,1)S(1)}, u32[]{:S(2)}) copy-start(bf16[352,8,128]{2,1,0:T(8,128)(2,1)S(1)} %collective-permute-done.28) | copy-start | bytes 2162692
  114.5 27.1 %slice-start = ((s8[16777216]{0:T(1024)(128)(4,1)}), s8[4194304]{0:T(1024)(128)(4,1)S(1)}, s32[]{:S(2)}) async-start(s8[16777216]{0:T(1024)(128)(4,1)} %bitcast.25), calls=%async_computation | async-start | bytes 8388608
  114.5 27.1 %slice-start.1 = ((s8[16777216]{0:T(1024)(128)(4,1)}), s8[4194304]{0:T(1024)(128)(4,1)S(1)}, s32[]{:S(2)}) async-start(s8[16777216]{0:T(1024)(128)(4,1)} %bitcast.25), calls=%async_computation.1 | async-start | bytes 8388608
  114.5 27.1 %slice-start.2 = ((s8[16777216]{0:T(1024)(128)(4,1)}), s8[4194304]{0:T(1024)(128)(4,1)S(1)}, s32[]{:S(2)}) async-start(s8[16777216]{0:T(1024)(128)(4,1)} %bitcast.25), calls=%async_computation.2 | async-start | bytes 8388608
  114.5 27.1 %slice-start.3 = ((s8[16777216]{0:T(1024)(128)(4,1)}), s8[4194304]{0:T(1024)(128)(4,1)S(1)}, s32[]{:S(2)}) async-start(s8[16777216]{0:T(1024)(128)(4,1)} %bitcast.25), calls=%async_computation.3 | async-start | bytes 8388608
  135.4 6.1 %collective-permute-start.31 = (bf16[512,1024]{1,0:T(8,128)(2,1)S(1)}, bf16[512,1024]{1,0:T(8,128)(2,1)S(1)}, u32[]{:S(2)}, u32[]{:S(2)}) collective-permute-start(bf16[512,1024]{1,0:T(8,128)(2,1)S(1)} %get-tuple-element.61), channel_id=1, source_target_pairs={{0,1},{1,0},{2,3},{3,2},{4,5},{5,4},{6,7},{7,6},{8,9},{9,8},{10,11... | collective-permute-start | bytes 3145736 | tf_op jit(solution)/shard_map/ppermute | solution.py:39
  138.9 2.7 %collective-permute-start.32 = (f32[512,128]{1,0:T(8,128)S(1)}, f32[512,128]{1,0:T(8,128)S(1)}, u32[]{:S(2)}, u32[]{:S(2)}) collective-permute-start(f32[512,128]{1,0:T(8,128)S(1)} %get-tuple-element.62), channel_id=1, source_target_pairs={{0,1},{1,0},{2,3},{3,2},{4,5},{5,4},{6,7},{7,6},{8,9},{9,8},{10,11... | collective-permute-start | bytes 786440 | tf_op jit(solution)/shard_map/ppermute | solution.py:39

commit v4 on v3

--- a/solution.py
+++ b/solution.py
@@ -67,10 +67,11 @@
             join(own, after), before, after[:half], before[half:]
         )
         low, high = back(low, ring), forth(high, ring)
-        first_after, before_before = back(first_half, last), forth(before, last)
+        first_after = back(first_half, last)
+        before_before = forth(before, last)
         first_before = forth(first_half, last)
-        low, high = together(low, high)
-        rest, second = join(low, high), join(before, low, high)
+        low, high, kept = together(low, high, before)
+        rest, second = join(low, high), join(kept, low, high)
         rest_before = forth(rest, last)
         second_after = back(second, last)
         first_far, before_far = back(first_after, last), forth(before_before, last)

time: 156 us -> 160 us (1.026)
  starting transfers between devices: 54.1 us -> 62.2 us
  waiting for transfers between devices: 50.9 us -> 47.8 us
    ppermute x3, starting transfers between devices: 5.87 us -> 17.2 us  [swap(): return lax.ppermute(array, ('row', 'col'), pairs)]
    ppermute x30, starting transfers between devices: 48.3 us -> 45 us  [send(): return lax.ppermute(array, ('row', 'col'), pairs)]
    ppermute x30, waiting for transfers between devices: 48.3 us -> 45.2 us  [send(): return lax.ppermute(array, ('row', 'col'), pairs)]
where the time goes in v4:
time: 160 us
  starting transfers between devices  62.2 us (39%)
  waiting for transfers between devices  47.8 us (30%)
  Pallas kernels  41.8 us (26%)
  local copies, waits for them, and re-layouts  5.61 us (4%)
  other arithmetic  2.34 us (1%)
    ppermute x30, waiting for transfers between devices, send(): return lax.ppermute(array, ('row', 'col'), pairs)  45.2 us
    ppermute x30, starting transfers between devices, send(): return lax.ppermute(array, ('row', 'col'), pairs)  45 us
    pallas_call x1, Pallas kernels, attention_call(): pl.pallas_call(attend, name='attend', out_shape=(out, stat, out, stat, bl...  20.9 us
    ppermute x3, starting transfers between devices, swap(): return lax.ppermute(array, ('row', 'col'), pairs)  17.2 us
    pallas_call x1, Pallas kernels, projection_call(): pl.pallas_call(project, name='project', grid=(width // tile,), out_shape=...  13.5 us
    pallas_call x1, Pallas kernels, fetched(): pl.pallas_call(fetch_near, name='fetch_near', in_specs=[smem, smem, *[hbm...  7.37 us
  transfers between devices with their start and end apart: 33, of which 14 were waited for; matrix products, arithmetic and copies ran while one was open for 4% of the time, Pallas kernels for 5%

profile of v4, /device:TPU:1, one launch (start us, length us, event | category | flops | bytes accessed | tf_op | source)
XLA Modules:
  0.0 160.1 jit_solution(18403984584240250454)
XLA Ops:
  0.0 1.0 slice_bitcast_fusion
  1.0 4.4 %collective-permute-start.12 = (bf16[44,8,128]{2,1,0:T(8,128)(2,1)S(1)}, bf16[44,8,128]{2,1,0:T(8,128)(2,1)S(1)}, u32[]{:S(2)}, u32[]{:S(2)}) collective-permute-start(bf16[44,8,128]{2,1,0:T(8,128)(2,1)S(1)} %slice_bitcast_fusion), channel_id=1, source_target_pairs={{0,64},{1,65},{2,66},{3,67},{4,68},{5,69},{6,70},{7,71},{8,72},{9,... | collective-permute-start | bytes 270344 | tf_op jit(solution)/shard_map/ppermute | solution.py:34
  5.4 0.4 collective-permute-start.13
  5.8 1.0 collective-permute-start.14
  6.9 0.9 fusion
  7.8 2.8 %collective-permute-start = (bf16[84,8,128]{2,1,0:T(8,128)(2,1)S(1)}, bf16[84,8,128]{2,1,0:T(8,128)(2,1)S(1)}, u32[]{:S(2)}, u32[]{:S(2)}) collective-permute-start(bf16[84,8,128]{2,1,0:T(8,128)(2,1)S(1)} %fusion), channel_id=1, source_target_pairs={{0,16},{1,5},{2,18},{3,7},{4,20},{5,1},{6,22},{7,3},{8,24},{9,13},... | collective-permute-start | bytes 516104 | tf_op jit(solution)/shard_map/ppermute | solution.py:34
  10.6 0.9 collective-permute-start.1
  11.5 0.0 collective-permute-done.12
  11.5 0.6 collective-permute-start.2
  12.1 0.0 collective-permute-done.13
  12.1 0.0 collective-permute-done.14
  12.2 2.1 %collective-permute-start.15 = (bf16[176,8,128]{2,1,0:T(8,128)(2,1)S(1)}, bf16[176,8,128]{2,1,0:T(8,128)(2,1)S(1)}, u32[]{:S(2)}, u32[]{:S(2)}) collective-permute-start(bf16[176,8,128]{2,1,0:T(8,128)(2,1)S(1)} %pad_maximum_fusion.4), channel_id=1, source_target_pairs={{0,6},{1,7},{2,0},{3,1},{4,2},{5,3},{6,4},{7,5},{8,14},{9,15},{10,... | collective-permute-start | bytes 1081352 | tf_op jit(solution)/shard_map/ppermute | solution.py:34
  14.3 1.6 collective-permute-done.1
  15.9 1.1 collective-permute-done.2
  17.0 0.1 pad_maximum_fusion.2
  17.1 3.1 %collective-permute-start.3 = (bf16[336,8,128]{2,1,0:T(8,128)(2,1)S(1)}, bf16[336,8,128]{2,1,0:T(8,128)(2,1)S(1)}, u32[]{:S(2)}, u32[]{:S(2)}) collective-permute-start(bf16[336,8,128]{2,1,0:T(8,128)(2,1)S(1)} %pad_maximum_fusion.2), channel_id=1, source_target_pairs={{0,96},{1,25},{2,98},{3,27},{4,100},{5,29},{6,102},{7,31},{8,104},... | collective-permute-start | bytes 2064392 | tf_op jit(solution)/shard_map/ppermute | solution.py:34
  20.2 2.3 %collective-permute-start.24 = (bf16[512,1024]{1,0:T(8,128)(2,1)S(1)}, bf16[512,1024]{1,0:T(8,128)(2,1)S(1)}, u32[]{:S(2)}, u32[]{:S(2)}) collective-permute-start(bf16[512,1024]{1,0:T(8,128)(2,1)S(1)} %copy-done), channel_id=1, source_target_pairs={{0,1},{1,0},{2,3},{3,2},{4,5},{5,4},{6,7},{7,6},{8,9},{9,8},{10,11... | collective-permute-start | bytes 3145736 | tf_op jit(solution)/shard_map/ppermute | solution.py:39
  22.5 0.1 pad_maximum_fusion.1
  22.6 2.5 %collective-permute-start.17 = (bf16[88,8,128]{2,1,0:T(8,128)(2,1)S(1)}, bf16[88,8,128]{2,1,0:T(8,128)(2,1)S(1)}, u32[]{:S(2)}, u32[]{:S(2)}) collective-permute-start(bf16[88,8,128]{2,1,0:T(8,128)(2,1)S(1)} %slice.30), channel_id=1, source_target_pairs={{0,6},{1,7},{2,0},{3,1},{4,2},{5,3},{6,4},{7,5},{8,14},{9,15},{10,... | collective-permute-start | bytes 540680 | tf_op jit(solution)/shard_map/ppermute | solution.py:34
  25.2 2.4 %collective-permute-done.17 = bf16[88,8,128]{2,1,0:T(8,128)(2,1)S(1)} collective-permute-done((bf16[88,8,128]{2,1,0:T(8,128)(2,1)S(1)}, bf16[88,8,128]{2,1,0:T(8,128)(2,1)S(1)}, u32[]{:S(2)}, u32[]{:S(2)}) %collective-permute-start.17) | collective-permute-done | bytes 180256 | tf_op jit(solution)/shard_map/ppermute | solution.py:34
  27.6 1.7 %collective-permute-start.22 = (bf16[176,8,128]{2,1,0:T(8,128)(2,1)S(1)}, bf16[176,8,128]{2,1,0:T(8,128)(2,1)S(1)}, u32[]{:S(2)}, u32[]{:S(2)}) collective-permute-start(bf16[176,8,128]{2,1,0:T(8,128)(2,1)S(1)} %collective-permute-done.16), channel_id=1, source_target_pairs={{0,8},{1,9},{2,10},{3,11},{4,12},{5,13},{6,14},{7,15},{8,16},{9,17... | collective-permute-start | bytes 1081352 | tf_op jit(solution)/shard_map/ppermute | solution.py:34
  29.3 1.7 %collective-permute-done.18 = bf16[88,8,128]{2,1,0:T(8,128)(2,1)S(1)} collective-permute-done((bf16[88,8,128]{2,1,0:T(8,128)(2,1)S(1)}, bf16[88,8,128]{2,1,0:T(8,128)(2,1)S(1)}, u32[]{:S(2)}, u32[]{:S(2)}) %collective-permute-start.18) | collective-permute-done | bytes 180256 | tf_op jit(solution)/shard_map/ppermute | solution.py:34
  31.0 0.6 collective-permute-start.23
  31.7 0.1 pad_maximum_fusion
  31.8 0.0 copy-start.1
  31.8 2.2 %collective-permute-start.5 = (bf16[168,8,128]{2,1,0:T(8,128)(2,1)S(1)}, bf16[168,8,128]{2,1,0:T(8,128)(2,1)S(1)}, u32[]{:S(2)}, u32[]{:S(2)}) collective-permute-start(bf16[168,8,128]{2,1,0:T(8,128)(2,1)S(1)} %slice.27), channel_id=1, source_target_pairs={{0,96},{1,25},{2,98},{3,27},{4,100},{5,29},{6,102},{7,31},{8,104},... | collective-permute-start | bytes 1032200 | tf_op jit(solution)/shard_map/ppermute | solution.py:34
  34.1 3.8 %collective-permute-start.7 = (bf16[672,8,128]{2,1,0:T(8,128)(2,1)S(1)}, bf16[672,8,128]{2,1,0:T(8,128)(2,1)}, u32[]{:S(2)}, u32[]{:S(2)}) collective-permute-start(bf16[672,8,128]{2,1,0:T(8,128)(2,1)S(1)} %pad_maximum_fusion), channel_id=1, source_target_pairs={{0,6},{1,97},{2,0},{3,99},{4,2},{5,101},{6,4},{7,103},{8,14},{9,10... | collective-permute-start | bytes 4128776 | tf_op jit(solution)/shard_map/ppermute | solution.py:34
  37.9 4.8 %collective-permute-done.23 = bf16[176,8,128]{2,1,0:T(8,128)(2,1)S(1)} collective-permute-done((bf16[176,8,128]{2,1,0:T(8,128)(2,1)S(1)}, bf16[176,8,128]{2,1,0:T(8,128)(2,1)S(1)}, u32[]{:S(2)}, u32[]{:S(2)}) %collective-permute-start.23) | collective-permute-done | bytes 360480 | tf_op jit(solution)/shard_map/ppermute | solution.py:34
  42.7 1.7 %collective-permute-start.19 = (bf16[352,8,128]{2,1,0:T(8,128)(2,1)S(1)}, bf16[352,8,128]{2,1,0:T(8,128)(2,1)}, u32[]{:S(2)}, u32[]{:S(2)}) collective-permute-start(bf16[352,8,128]{2,1,0:T(8,128)(2,1)S(1)} %pad_maximum_fusion.1), channel_id=1, source_target_pairs={{0,24},{1,25},{2,26},{3,27},{4,28},{5,29},{6,30},{7,31},{8,0},{9,1... | collective-permute-start | bytes 2162696 | tf_op jit(solution)/shard_map/ppermute | solution.py:34
  44.4 0.1 collective-permute-start.29
  44.5 5.5 %collective-permute-done.6 = bf16[168,8,128]{2,1,0:T(8,128)(2,1)S(1)} collective-permute-done((bf16[168,8,128]{2,1,0:T(8,128)(2,1)S(1)}, bf16[168,8,128]{2,1,0:T(8,128)(2,1)S(1)}, u32[]{:S(2)}, u32[]{:S(2)}) %collective-permute-start.6) | collective-permute-done | bytes 344096 | tf_op jit(solution)/shard_map/ppermute | solution.py:34
  50.1 1.2 collective-permute-start.21
  51.3 1.6 collective-permute-start.20
  52.9 0.9 constant_dynamic-update-slice_fusion.2
  53.8 0.8 collective-permute-done.29
  54.5 0.7 collective-permute-start.9
  55.3 0.8 constant_dynamic-update-slice_fusion.1
  56.0 0.8 constant_dynamic-update-slice_fusion
  56.8 4.3 %collective-permute-start.8 = (bf16[672,8,128]{2,1,0:T(8,128)(2,1)}, bf16[672,8,128]{2,1,0:T(8,128)(2,1)}, u32[]{:S(2)}, u32[]{:S(2)}) collective-permute-start(bf16[672,8,128]{2,1,0:T(8,128)(2,1)} %constant_dynamic-update-slice_fusion), channel_id=1, source_target_pairs={{0,6},{1,97},{2,0},{3,99},{4,2},{5,101},{6,4},{7,103},{8,14},{9,10... | collective-permute-start | bytes 4128776 | tf_op jit(solution)/shard_map/ppermute | solution.py:34
  61.1 5.5 %collective-permute-done.21 = bf16[352,8,128]{2,1,0:T(8,128)(2,1)S(1)} collective-permute-done((bf16[352,8,128]{2,1,0:T(8,128)(2,1)S(1)}, bf16[352,8,128]{2,1,0:T(8,128)(2,1)S(1)}, u32[]{:S(2)}, u32[]{:S(2)}) %collective-permute-start.21) | collective-permute-done | bytes 720928 | tf_op jit(solution)/shard_map/ppermute | solution.py:34
  66.6 0.7 collective-permute-start.10
  67.3 0.1 pad_maximum_fusion.3
  67.4 2.4 %collective-permute-done.20 = bf16[352,8,128]{2,1,0:T(8,128)(2,1)S(1)} collective-permute-done((bf16[352,8,128]{2,1,0:T(8,128)(2,1)S(1)}, bf16[352,8,128]{2,1,0:T(8,128)(2,1)S(1)}, u32[]{:S(2)}, u32[]{:S(2)}) %collective-permute-start.20) | collective-permute-done | bytes 720928 | tf_op jit(solution)/shard_map/ppermute | solution.py:34
  69.8 1.8 %collective-permute-start.11 = (bf16[336,8,128]{2,1,0:T(8,128)(2,1)S(1)}, bf16[336,8,128]{2,1,0:T(8,128)(2,1)}, u32[]{:S(2)}, u32[]{:S(2)}) collective-permute-start(bf16[336,8,128]{2,1,0:T(8,128)(2,1)S(1)} %pad_maximum_fusion.3), channel_id=1, source_target_pairs={{0,2},{1,33},{2,4},{3,35},{4,6},{5,37},{6,0},{7,39},{8,10},{9,41},... | collective-permute-start | bytes 2064392 | tf_op jit(solution)/shard_map/ppermute | solution.py:34
  71.7 5.0 %collective-permute-start.25 = (bf16[672,8,128]{2,1,0:T(8,128)(2,1)}, bf16[672,8,128]{2,1,0:T(8,128)(2,1)}, u32[]{:S(2)}, u32[]{:S(2)}) collective-permute-start(bf16[672,8,128]{2,1,0:T(8,128)(2,1)} %collective-permute-done.7), channel_id=1, source_target_pairs={{0,6},{1,97},{2,0},{3,99},{4,2},{5,101},{6,4},{7,103},{8,14},{9,10... | collective-permute-start | bytes 4128776 | tf_op jit(solution)/shard_map/ppermute | solution.py:34
  76.6 5.1 %collective-permute-done.10 = bf16[336,8,128]{2,1,0:T(8,128)(2,1)} collective-permute-done((bf16[336,8,128]{2,1,0:T(8,128)(2,1)S(1)}, bf16[336,8,128]{2,1,0:T(8,128)(2,1)}, u32[]{:S(2)}, u32[]{:S(2)}) %collective-permute-start.10) | collective-permute-done | bytes 688160 | tf_op jit(solution)/shard_map/ppermute | solution.py:34
  81.7 0.8 collective-permute-start.28
  82.5 6.6 %collective-permute-done.11 = bf16[336,8,128]{2,1,0:T(8,128)(2,1)} collective-permute-done((bf16[336,8,128]{2,1,0:T(8,128)(2,1)S(1)}, bf16[336,8,128]{2,1,0:T(8,128)(2,1)}, u32[]{:S(2)}, u32[]{:S(2)}) %collective-permute-start.11) | collective-permute-done | bytes 688160 | tf_op jit(solution)/shard_map/ppermute | solution.py:34
  89.2 1.1 copy-done.4
  90.3 0.0 collective-permute-start.27
  90.3 0.8 collective-permute-start.30
  91.1 0.8 subtract_shift-right-arithmetic_fusion.starts
  91.9 0.8 dynamic_slice.7
  92.7 0.1 reshape.83
  92.8 0.2 shift-right-arithmetic_reduce_fusion
  93.0 7.4 %fetch_near.1 = (bf16[8192,128]{1,0:T(8,128)(2,1)S(1)}, bf16[8192,128]{1,0:T(8,128)(2,1)S(1)}, s32[128]{0:T(128)S(1)}) custom-call(s32[64]{0:T(128)S(1)} %fusion.5.codes, s32[9]{0:T(128)S(1)} %subtract_shift-right-arithmetic_fusion.starts, bf16[5376,128]{1,0:T(8,128)(2,1)} %bitcast.27, bf16[5376,128]{1,0:T(8,128)(2,1)} %bitcast.3.refs_1_, ...), custom_call_target="tpu_custom_call" | custom-call | tf_op jit(solution)/shard_map/fetch_near/pallas_call | solution.py:229
  100.4 0.0 copy-start.9
  100.4 0.2 collective-permute-done.26
  100.6 7.5 %collective-permute-done.27 = bf16[336,8,128]{2,1,0:T(8,128)(2,1)} collective-permute-done((bf16[336,8,128]{2,1,0:T(8,128)(2,1)}, bf16[336,8,128]{2,1,0:T(8,128)(2,1)}, u32[]{:S(2)}, u32[]{:S(2)}) %collective-permute-start.27) | collective-permute-done | bytes 688160 | tf_op jit(solution)/shard_map/ppermute | solution.py:34
  108.2 20.9 %attend.1 = (bf16[512,1024]{1,0:T(8,128)(2,1)S(1)}, f32[512,128]{1,0:T(8,128)S(1)}, bf16[512,1024]{1,0:T(8,128)(2,1)S(1)}, f32[512,128]{1,0:T(8,128)S(1)}, bf16[...) custom-call(s32[1]{0:T(128)} %bitcast.place, ...), custom_call_target="tpu_custom_call", output_to_operand_aliasing={{4}: (12, {}), {5}: (13, {})} | custom-call | flops 8589934592 | bytes 8388608 | tf_op jit(solution)/shard_map/attend/pallas_call | solution.py:355
  129.1 14.8 %collective-permute-start.31 = (bf16[512,1024]{1,0:T(8,128)(2,1)S(1)}, bf16[512,1024]{1,0:T(8,128)(2,1)S(1)}, u32[]{:S(2)}, u32[]{:S(2)}) collective-permute-start(bf16[512,1024]{1,0:T(8,128)(2,1)S(1)} %get-tuple-element.65), channel_id=1, source_target_pairs={{0,1},{1,0},{2,3},{3,2},{4,5},{5,4},{6,7},{7,6},{8,9},{9,8},{10,11... | collective-permute-start | bytes 3145736 | tf_op jit(solution)/shard_map/ppermute | solution.py:39
  143.9 0.1 collective-permute-start.32
  144.0 2.6 %collective-permute-done.32.stat_b = f32[512,128]{1,0:T(8,128)S(1)} collective-permute-done((f32[512,128]{1,0:T(8,128)S(1)}, f32[512,128]{1,0:T(8,128)S(1)}, u32[]{:S(2)}, u32[]{:S(2)}) %collective-permute-start.32) | collective-permute-done | bytes 262176 | tf_op jit(solution)/shard_map/ppermute | solution.py:39
  146.6 13.5 %project.1 = bf16[512,8192]{1,0:T(8,128)(2,1)} custom-call(bf16[512,1024]{1,0:T(8,128)(2,1)S(1)} %get-tuple-element.63.o_a, f32[512,128]{1,0:T(8,128)S(1)} %get-tuple-element.64.stat_a, bf16[512,1024]{1,0:T(8,128)(2,1)S(1)} %collective-permute-done.31.o_b, f32[512,128]{1,0:T(8,128)S(1)} %collective-permute-done.32.stat_b, bf16[1024,8192]{1,0:T(8,128)(2,1)S(1)} %bitcast.26), custom_call_target="tpu_custom_call" | custom-call | tf_op jit(solution)/shard_map/project/pallas_call | solution.py:427
  (59 shorter events, 0.4 us)
Async XLA Ops:
  0.0 20.2 %copy-start = (bf16[512,1024]{1,0:T(8,128)(2,1)S(1)}, bf16[512,1024]{1,0:T(8,128)(2,1)}, u32[]{:S(2)}) copy-start(bf16[512,1024]{1,0:T(8,128)(2,1)} %own_queries.1) | copy-start | bytes 3145732
  1.0 10.5 %collective-permute-start.12 = (bf16[44,8,128]{2,1,0:T(8,128)(2,1)S(1)}, bf16[44,8,128]{2,1,0:T(8,128)(2,1)S(1)}, u32[]{:S(2)}, u32[]{:S(2)}) collective-permute-start(bf16[44,8,128]{2,1,0:T(8,128)(2,1)S(1)} %slice_bitcast_fusion), channel_id=1, source_target_pairs={{0,64},{1,65},{2,66},{3,67},{4,68},{5,69},{6,70},{7,71},{8,72},{9,... | collective-permute-start | bytes 270344 | tf_op jit(solution)/shard_map/ppermute | solution.py:34
  5.4 6.7 %collective-permute-start.13 = (bf16[44,8,128]{2,1,0:T(8,128)(2,1)S(1)}, bf16[44,8,128]{2,1,0:T(8,128)(2,1)S(1)}, u32[]{:S(2)}, u32[]{:S(2)}) collective-permute-start(bf16[44,8,128]{2,1,0:T(8,128)(2,1)S(1)} %slice_bitcast_fusion), channel_id=1, source_target_pairs={{0,96},{1,97},{2,98},{3,99},{4,100},{5,101},{6,102},{7,103},{8,104... | collective-permute-start | bytes 270344 | tf_op jit(solution)/shard_map/ppermute | solution.py:34
  5.8 6.3 %collective-permute-start.14 = (bf16[44,8,128]{2,1,0:T(8,128)(2,1)S(1)}, bf16[44,8,128]{2,1,0:T(8,128)(2,1)S(1)}, u32[]{:S(2)}, u32[]{:S(2)}) collective-permute-start(bf16[44,8,128]{2,1,0:T(8,128)(2,1)S(1)} %slice_bitcast_fusion), channel_id=1, source_target_pairs={{0,32},{1,33},{2,34},{3,35},{4,36},{5,37},{6,38},{7,39},{8,40},{9,... | collective-permute-start | bytes 270344 | tf_op jit(solution)/shard_map/ppermute | solution.py:34
  7.8 6.5 %collective-permute-start = (bf16[84,8,128]{2,1,0:T(8,128)(2,1)S(1)}, bf16[84,8,128]{2,1,0:T(8,128)(2,1)S(1)}, u32[]{:S(2)}, u32[]{:S(2)}) collective-permute-start(bf16[84,8,128]{2,1,0:T(8,128)(2,1)S(1)} %fusion), channel_id=1, source_target_pairs={{0,16},{1,5},{2,18},{3,7},{4,20},{5,1},{6,22},{7,3},{8,24},{9,13},... | collective-permute-start | bytes 516104 | tf_op jit(solution)/shard_map/ppermute | solution.py:34
  10.6 5.2 %collective-permute-start.1 = (bf16[84,8,128]{2,1,0:T(8,128)(2,1)S(1)}, bf16[84,8,128]{2,1,0:T(8,128)(2,1)S(1)}, u32[]{:S(2)}, u32[]{:S(2)}) collective-permute-start(bf16[84,8,128]{2,1,0:T(8,128)(2,1)S(1)} %fusion), channel_id=1, source_target_pairs={{0,24},{1,7},{2,26},{3,1},{4,28},{5,3},{6,30},{7,5},{8,0},{9,15},{... | collective-permute-start | bytes 516104 | tf_op jit(solution)/shard_map/ppermute | solution.py:34
  11.5 5.5 %collective-permute-start.2 = (bf16[84,8,128]{2,1,0:T(8,128)(2,1)S(1)}, bf16[84,8,128]{2,1,0:T(8,128)(2,1)S(1)}, u32[]{:S(2)}, u32[]{:S(2)}) collective-permute-start(bf16[84,8,128]{2,1,0:T(8,128)(2,1)S(1)} %fusion), channel_id=1, source_target_pairs={{0,8},{1,3},{2,10},{3,5},{4,12},{5,7},{6,14},{7,1},{8,16},{9,11},{... | collective-permute-start | bytes 516104 | tf_op jit(solution)/shard_map/ppermute | solution.py:34
  12.2 10.3 %collective-permute-start.15 = (bf16[176,8,128]{2,1,0:T(8,128)(2,1)S(1)}, bf16[176,8,128]{2,1,0:T(8,128)(2,1)S(1)}, u32[]{:S(2)}, u32[]{:S(2)}) collective-permute-start(bf16[176,8,128]{2,1,0:T(8,128)(2,1)S(1)} %pad_maximum_fusion.4), channel_id=1, source_target_pairs={{0,6},{1,7},{2,0},{3,1},{4,2},{5,3},{6,4},{7,5},{8,14},{9,15},{10,... | collective-permute-start | bytes 1081352 | tf_op jit(solution)/shard_map/ppermute | solution.py:34
  14.3 8.2 %collective-permute-start.16 = (bf16[176,8,128]{2,1,0:T(8,128)(2,1)S(1)}, bf16[176,8,128]{2,1,0:T(8,128)(2,1)S(1)}, u32[]{:S(2)}, u32[]{:S(2)}) collective-permute-start(bf16[176,8,128]{2,1,0:T(8,128)(2,1)S(1)} %pad_maximum_fusion.4), channel_id=1, source_target_pairs={{0,2},{1,3},{2,4},{3,5},{4,6},{5,7},{6,0},{7,1},{8,10},{9,11},{10,... | collective-permute-start | bytes 1081352 | tf_op jit(solution)/shard_map/ppermute | solution.py:34
  17.1 14.6 %collective-permute-start.3 = (bf16[336,8,128]{2,1,0:T(8,128)(2,1)S(1)}, bf16[336,8,128]{2,1,0:T(8,128)(2,1)S(1)}, u32[]{:S(2)}, u32[]{:S(2)}) collective-permute-start(bf16[336,8,128]{2,1,0:T(8,128)(2,1)S(1)} %pad_maximum_fusion.2), channel_id=1, source_target_pairs={{0,96},{1,25},{2,98},{3,27},{4,100},{5,29},{6,102},{7,31},{8,104},... | collective-permute-start | bytes 2064392 | tf_op jit(solution)/shard_map/ppermute | solution.py:34
  20.2 11.5 %collective-permute-start.4 = (bf16[336,8,128]{2,1,0:T(8,128)(2,1)S(1)}, bf16[336,8,128]{2,1,0:T(8,128)(2,1)S(1)}, u32[]{:S(2)}, u32[]{:S(2)}) collective-permute-start(bf16[336,8,128]{2,1,0:T(8,128)(2,1)S(1)} %pad_maximum_fusion.2), channel_id=1, source_target_pairs={{0,32},{1,9},{2,34},{3,11},{4,36},{5,13},{6,38},{7,15},{8,40},{9,1... | collective-permute-start | bytes 2064392 | tf_op jit(solution)/shard_map/ppermute | solution.py:34
  20.2 31.1 %collective-permute-start.24 = (bf16[512,1024]{1,0:T(8,128)(2,1)S(1)}, bf16[512,1024]{1,0:T(8,128)(2,1)S(1)}, u32[]{:S(2)}, u32[]{:S(2)}) collective-permute-start(bf16[512,1024]{1,0:T(8,128)(2,1)S(1)} %copy-done), channel_id=1, source_target_pairs={{0,1},{1,0},{2,3},{3,2},{4,5},{5,4},{6,7},{7,6},{8,9},{9,8},{10,11... | collective-permute-start | bytes 3145736 | tf_op jit(solution)/shard_map/ppermute | solution.py:39
  22.5 27.5 %copy-start.2 = (bf16[352,8,128]{2,1,0:T(8,128)(2,1)}, bf16[352,8,128]{2,1,0:T(8,128)(2,1)S(1)}, u32[]{:S(2)}) copy-start(bf16[352,8,128]{2,1,0:T(8,128)(2,1)S(1)} %pad_maximum_fusion.1) | copy-start | bytes 2162692
  22.6 5.0 %collective-permute-start.17 = (bf16[88,8,128]{2,1,0:T(8,128)(2,1)S(1)}, bf16[88,8,128]{2,1,0:T(8,128)(2,1)S(1)}, u32[]{:S(2)}, u32[]{:S(2)}) collective-permute-start(bf16[88,8,128]{2,1,0:T(8,128)(2,1)S(1)} %slice.30), channel_id=1, source_target_pairs={{0,6},{1,7},{2,0},{3,1},{4,2},{5,3},{6,4},{7,5},{8,14},{9,15},{10,... | collective-permute-start | bytes 540680 | tf_op jit(solution)/shard_map/ppermute | solution.py:34
  25.1 5.9 %collective-permute-start.18 = (bf16[88,8,128]{2,1,0:T(8,128)(2,1)S(1)}, bf16[88,8,128]{2,1,0:T(8,128)(2,1)S(1)}, u32[]{:S(2)}, u32[]{:S(2)}) collective-permute-start(bf16[88,8,128]{2,1,0:T(8,128)(2,1)S(1)} %slice.31), channel_id=1, source_target_pairs={{0,2},{1,3},{2,4},{3,5},{4,6},{5,7},{6,0},{7,1},{8,10},{9,11},{10,... | collective-permute-start | bytes 540680 | tf_op jit(solution)/shard_map/ppermute | solution.py:34
  27.6 10.3 %collective-permute-start.22 = (bf16[176,8,128]{2,1,0:T(8,128)(2,1)S(1)}, bf16[176,8,128]{2,1,0:T(8,128)(2,1)S(1)}, u32[]{:S(2)}, u32[]{:S(2)}) collective-permute-start(bf16[176,8,128]{2,1,0:T(8,128)(2,1)S(1)} %collective-permute-done.16), channel_id=1, source_target_pairs={{0,8},{1,9},{2,10},{3,11},{4,12},{5,13},{6,14},{7,15},{8,16},{9,17... | collective-permute-start | bytes 1081352 | tf_op jit(solution)/shard_map/ppermute | solution.py:34
  31.0 11.7 %collective-permute-start.23 = (bf16[176,8,128]{2,1,0:T(8,128)(2,1)S(1)}, bf16[176,8,128]{2,1,0:T(8,128)(2,1)S(1)}, u32[]{:S(2)}, u32[]{:S(2)}) collective-permute-start(bf16[176,8,128]{2,1,0:T(8,128)(2,1)S(1)} %pad_maximum_fusion.5), channel_id=1, source_target_pairs={{0,8},{1,9},{2,10},{3,11},{4,12},{5,13},{6,14},{7,15},{8,16},{9,17... | collective-permute-start | bytes 1081352 | tf_op jit(solution)/shard_map/ppermute | solution.py:34
  31.8 22.7 %copy-start.1 = (bf16[672,8,128]{2,1,0:T(8,128)(2,1)}, bf16[672,8,128]{2,1,0:T(8,128)(2,1)S(1)}, u32[]{:S(2)}) copy-start(bf16[672,8,128]{2,1,0:T(8,128)(2,1)S(1)} %pad_maximum_fusion) | copy-start | bytes 4128772
  31.8 12.6 %collective-permute-start.5 = (bf16[168,8,128]{2,1,0:T(8,128)(2,1)S(1)}, bf16[168,8,128]{2,1,0:T(8,128)(2,1)S(1)}, u32[]{:S(2)}, u32[]{:S(2)}) collective-permute-start(bf16[168,8,128]{2,1,0:T(8,128)(2,1)S(1)} %slice.27), channel_id=1, source_target_pairs={{0,96},{1,25},{2,98},{3,27},{4,100},{5,29},{6,102},{7,31},{8,104},... | collective-permute-start | bytes 1032200 | tf_op jit(solution)/shard_map/ppermute | solution.py:34
  34.1 37.6 %collective-permute-start.7 = (bf16[672,8,128]{2,1,0:T(8,128)(2,1)S(1)}, bf16[672,8,128]{2,1,0:T(8,128)(2,1)}, u32[]{:S(2)}, u32[]{:S(2)}) collective-permute-start(bf16[672,8,128]{2,1,0:T(8,128)(2,1)S(1)} %pad_maximum_fusion), channel_id=1, source_target_pairs={{0,6},{1,97},{2,0},{3,99},{4,2},{5,101},{6,4},{7,103},{8,14},{9,10... | collective-permute-start | bytes 4128776 | tf_op jit(solution)/shard_map/ppermute | solution.py:34
  37.9 15.9 %copy-start.7 = (bf16[176,8,128]{2,1,0:T(8,128)(2,1)}, bf16[176,8,128]{2,1,0:T(8,128)(2,1)S(1)}, u32[]{:S(2)}) copy-start(bf16[176,8,128]{2,1,0:T(8,128)(2,1)S(1)} %collective-permute-done.22) | copy-start | bytes 1081348
  37.9 12.2 %collective-permute-start.6 = (bf16[168,8,128]{2,1,0:T(8,128)(2,1)S(1)}, bf16[168,8,128]{2,1,0:T(8,128)(2,1)S(1)}, u32[]{:S(2)}, u32[]{:S(2)}) collective-permute-start(bf16[168,8,128]{2,1,0:T(8,128)(2,1)S(1)} %slice.28), channel_id=1, source_target_pairs={{0,32},{1,9},{2,34},{3,11},{4,36},{5,13},{6,38},{7,15},{8,40},{9,1... | collective-permute-start | bytes 1032200 | tf_op jit(solution)/shard_map/ppermute | solution.py:34
  42.7 47.6 %copy-start.8 = (bf16[176,8,128]{2,1,0:T(8,128)(2,1)}, bf16[176,8,128]{2,1,0:T(8,128)(2,1)S(1)}, u32[]{:S(2)}) copy-start(bf16[176,8,128]{2,1,0:T(8,128)(2,1)S(1)} %collective-permute-done.23) | copy-start | bytes 1081348
  42.7 14.1 %collective-permute-start.19 = (bf16[352,8,128]{2,1,0:T(8,128)(2,1)S(1)}, bf16[352,8,128]{2,1,0:T(8,128)(2,1)}, u32[]{:S(2)}, u32[]{:S(2)}) collective-permute-start(bf16[352,8,128]{2,1,0:T(8,128)(2,1)S(1)} %pad_maximum_fusion.1), channel_id=1, source_target_pairs={{0,24},{1,25},{2,26},{3,27},{4,28},{5,29},{6,30},{7,31},{8,0},{9,1... | collective-permute-start | bytes 2162696 | tf_op jit(solution)/shard_map/ppermute | solution.py:34
  44.4 10.1 %collective-permute-start.29 = (bf16[176,8,128]{2,1,0:T(8,128)(2,1)S(1)}, bf16[176,8,128]{2,1,0:T(8,128)(2,1)S(1)}, u32[]{:S(2)}, u32[]{:S(2)}) collective-permute-start(bf16[176,8,128]{2,1,0:T(8,128)(2,1)S(1)} %collective-permute-done.22), channel_id=1, source_target_pairs={{0,8},{1,9},{2,10},{3,11},{4,12},{5,13},{6,14},{7,15},{8,16},{9,17... | collective-permute-start | bytes 1081352 | tf_op jit(solution)/shard_map/ppermute | solution.py:34
  50.1 16.5 %collective-permute-start.21 = (bf16[352,8,128]{2,1,0:T(8,128)(2,1)S(1)}, bf16[352,8,128]{2,1,0:T(8,128)(2,1)S(1)}, u32[]{:S(2)}, u32[]{:S(2)}) collective-permute-start(bf16[352,8,128]{2,1,0:T(8,128)(2,1)S(1)} %pad_maximum_fusion.1), channel_id=1, source_target_pairs={{0,8},{1,9},{2,10},{3,11},{4,12},{5,13},{6,14},{7,15},{8,16},{9,17... | collective-permute-start | bytes 2162696 | tf_op jit(solution)/shard_map/ppermute | solution.py:34
  51.3 5.5 %copy-start.3 = (bf16[352,8,128]{2,1,0:T(8,128)(2,1)}, bf16[352,8,128]{2,1,0:T(8,128)(2,1)S(1)}, u32[]{:S(2)}) copy-start(bf16[352,8,128]{2,1,0:T(8,128)(2,1)S(1)} %constant_dynamic-update-slice_fusion.3) | copy-start | bytes 2162692
  51.3 18.5 %collective-permute-start.20 = (bf16[352,8,128]{2,1,0:T(8,128)(2,1)S(1)}, bf16[352,8,128]{2,1,0:T(8,128)(2,1)S(1)}, u32[]{:S(2)}, u32[]{:S(2)}) collective-permute-start(bf16[352,8,128]{2,1,0:T(8,128)(2,1)S(1)} %constant_dynamic-update-slice_fusion.3), channel_id=1, source_target_pairs={{0,24},{1,25},{2,26},{3,27},{4,28},{5,29},{6,30},{7,31},{8,0},{9,1... | collective-permute-start | bytes 2162696 | tf_op jit(solution)/shard_map/ppermute | solution.py:34
  54.5 12.8 %copy-start.10 = (bf16[176,8,128]{2,1,0:T(8,128)(2,1)}, bf16[176,8,128]{2,1,0:T(8,128)(2,1)S(1)}, u32[]{:S(2)}) copy-start(bf16[176,8,128]{2,1,0:T(8,128)(2,1)S(1)} %collective-permute-done.29) | copy-start | bytes 1081348
  54.5 34.6 %collective-permute-start.9 = (bf16[672,8,128]{2,1,0:T(8,128)(2,1)S(1)}, bf16[672,8,128]{2,1,0:T(8,128)(2,1)S(1)}, u32[]{:S(2)}, u32[]{:S(2)}) collective-permute-start(bf16[672,8,128]{2,1,0:T(8,128)(2,1)S(1)} %pad_maximum_fusion), channel_id=1, source_target_pairs={{0,2},{1,33},{2,4},{3,35},{4,6},{5,37},{6,0},{7,39},{8,10},{9,41},... | collective-permute-start | bytes 4128776 | tf_op jit(solution)/shard_map/ppermute | solution.py:34
  56.8 33.5 %collective-permute-start.8 = (bf16[672,8,128]{2,1,0:T(8,128)(2,1)}, bf16[672,8,128]{2,1,0:T(8,128)(2,1)}, u32[]{:S(2)}, u32[]{:S(2)}) collective-permute-start(bf16[672,8,128]{2,1,0:T(8,128)(2,1)} %constant_dynamic-update-slice_fusion), channel_id=1, source_target_pairs={{0,6},{1,97},{2,0},{3,99},{4,2},{5,101},{6,4},{7,103},{8,14},{9,10... | collective-permute-start | bytes 4128776 | tf_op jit(solution)/shard_map/ppermute | solution.py:34
  66.6 23.7 %copy-start.5 = (bf16[352,8,128]{2,1,0:T(8,128)(2,1)}, bf16[352,8,128]{2,1,0:T(8,128)(2,1)S(1)}, u32[]{:S(2)}) copy-start(bf16[352,8,128]{2,1,0:T(8,128)(2,1)S(1)} %collective-permute-done.21) | copy-start | bytes 2162692
  66.6 15.1 %collective-permute-start.10 = (bf16[336,8,128]{2,1,0:T(8,128)(2,1)S(1)}, bf16[336,8,128]{2,1,0:T(8,128)(2,1)}, u32[]{:S(2)}, u32[]{:S(2)}) collective-permute-start(bf16[336,8,128]{2,1,0:T(8,128)(2,1)S(1)} %collective-permute-done.4), channel_id=1, source_target_pairs={{0,2},{1,33},{2,4},{3,35},{4,6},{5,37},{6,0},{7,39},{8,10},{9,41},... | collective-permute-start | bytes 2064392 | tf_op jit(solution)/shard_map/ppermute | solution.py:34
  69.8 20.5 %copy-start.6 = (bf16[352,8,128]{2,1,0:T(8,128)(2,1)}, bf16[352,8,128]{2,1,0:T(8,128)(2,1)S(1)}, u32[]{:S(2)}) copy-start(bf16[352,8,128]{2,1,0:T(8,128)(2,1)S(1)} %collective-permute-done.20) | copy-start | bytes 2162692
  69.8 19.3 %collective-permute-start.11 = (bf16[336,8,128]{2,1,0:T(8,128)(2,1)S(1)}, bf16[336,8,128]{2,1,0:T(8,128)(2,1)}, u32[]{:S(2)}, u32[]{:S(2)}) collective-permute-start(bf16[336,8,128]{2,1,0:T(8,128)(2,1)S(1)} %pad_maximum_fusion.3), channel_id=1, source_target_pairs={{0,2},{1,33},{2,4},{3,35},{4,6},{5,37},{6,0},{7,39},{8,10},{9,41},... | collective-permute-start | bytes 2064392 | tf_op jit(solution)/shard_map/ppermute | solution.py:34
  71.7 36.5 %collective-permute-start.25 = (bf16[672,8,128]{2,1,0:T(8,128)(2,1)}, bf16[672,8,128]{2,1,0:T(8,128)(2,1)}, u32[]{:S(2)}, u32[]{:S(2)}) collective-permute-start(bf16[672,8,128]{2,1,0:T(8,128)(2,1)} %collective-permute-done.7), channel_id=1, source_target_pairs={{0,6},{1,97},{2,0},{3,99},{4,2},{5,101},{6,4},{7,103},{8,14},{9,10... | collective-permute-start | bytes 4128776 | tf_op jit(solution)/shard_map/ppermute | solution.py:34
  81.7 18.7 %collective-permute-start.28 = (bf16[352,8,128]{2,1,0:T(8,128)(2,1)}, bf16[352,8,128]{2,1,0:T(8,128)(2,1)S(1)}, u32[]{:S(2)}, u32[]{:S(2)}) collective-permute-start(bf16[352,8,128]{2,1,0:T(8,128)(2,1)} %collective-permute-done.19), channel_id=1, source_target_pairs={{0,24},{1,25},{2,26},{3,27},{4,28},{5,29},{6,30},{7,31},{8,0},{9,1... | collective-permute-start | bytes 2162696 | tf_op jit(solution)/shard_map/ppermute | solution.py:34
  89.2 11.5 %collective-permute-start.26 = (bf16[336,8,128]{2,1,0:T(8,128)(2,1)}, bf16[336,8,128]{2,1,0:T(8,128)(2,1)}, u32[]{:S(2)}, u32[]{:S(2)}) collective-permute-start(bf16[336,8,128]{2,1,0:T(8,128)(2,1)} %collective-permute-done.10), channel_id=1, source_target_pairs={{0,2},{1,33},{2,4},{3,35},{4,6},{5,37},{6,0},{7,39},{8,10},{9,41},... | collective-permute-start | bytes 2064392 | tf_op jit(solution)/shard_map/ppermute | solution.py:34
  89.2 1.1 copy-start.4
  90.3 17.9 %collective-permute-start.27 = (bf16[336,8,128]{2,1,0:T(8,128)(2,1)}, bf16[336,8,128]{2,1,0:T(8,128)(2,1)}, u32[]{:S(2)}, u32[]{:S(2)}) collective-permute-start(bf16[336,8,128]{2,1,0:T(8,128)(2,1)} %collective-permute-done.11), channel_id=1, source_target_pairs={{0,2},{1,33},{2,4},{3,35},{4,6},{5,37},{6,0},{7,39},{8,10},{9,41},... | collective-permute-start | bytes 2064392 | tf_op jit(solution)/shard_map/ppermute | solution.py:34
  90.3 10.1 %collective-permute-start.30 = (bf16[176,8,128]{2,1,0:T(8,128)(2,1)S(1)}, bf16[176,8,128]{2,1,0:T(8,128)(2,1)}, u32[]{:S(2)}, u32[]{:S(2)}) collective-permute-start(bf16[176,8,128]{2,1,0:T(8,128)(2,1)S(1)} %collective-permute-done.23), channel_id=1, source_target_pairs={{0,8},{1,9},{2,10},{3,11},{4,12},{5,13},{6,14},{7,15},{8,16},{9,17... | collective-permute-start | bytes 1081352 | tf_op jit(solution)/shard_map/ppermute | solution.py:34
  100.4 7.7 %copy-start.9 = (bf16[352,8,128]{2,1,0:T(8,128)(2,1)}, bf16[352,8,128]{2,1,0:T(8,128)(2,1)S(1)}, u32[]{:S(2)}) copy-start(bf16[352,8,128]{2,1,0:T(8,128)(2,1)S(1)} %collective-permute-done.28) | copy-start | bytes 2162692
  108.1 38.4 %slice-start = ((s8[16777216]{0:T(1024)(128)(4,1)}), s8[4194304]{0:T(1024)(128)(4,1)S(1)}, s32[]{:S(2)}) async-start(s8[16777216]{0:T(1024)(128)(4,1)} %bitcast.25), calls=%async_computation | async-start | bytes 8388608
  108.1 38.4 %slice-start.1 = ((s8[16777216]{0:T(1024)(128)(4,1)}), s8[4194304]{0:T(1024)(128)(4,1)S(1)}, s32[]{:S(2)}) async-start(s8[16777216]{0:T(1024)(128)(4,1)} %bitcast.25), calls=%async_computation.1 | async-start | bytes 8388608
  108.2 38.4 %slice-start.2 = ((s8[16777216]{0:T(1024)(128)(4,1)}), s8[4194304]{0:T(1024)(128)(4,1)S(1)}, s32[]{:S(2)}) async-start(s8[16777216]{0:T(1024)(128)(4,1)} %bitcast.25), calls=%async_computation.2 | async-start | bytes 8388608
  108.2 38.4 %slice-start.3 = ((s8[16777216]{0:T(1024)(128)(4,1)}), s8[4194304]{0:T(1024)(128)(4,1)S(1)}, s32[]{:S(2)}) async-start(s8[16777216]{0:T(1024)(128)(4,1)} %bitcast.25), calls=%async_computation.3 | async-start | bytes 8388608
  129.1 17.4 %collective-permute-start.31 = (bf16[512,1024]{1,0:T(8,128)(2,1)S(1)}, bf16[512,1024]{1,0:T(8,128)(2,1)S(1)}, u32[]{:S(2)}, u32[]{:S(2)}) collective-permute-start(bf16[512,1024]{1,0:T(8,128)(2,1)S(1)} %get-tuple-element.65), channel_id=1, source_target_pairs={{0,1},{1,0},{2,3},{3,2},{4,5},{5,4},{6,7},{7,6},{8,9},{9,8},{10,11... | collective-permute-start | bytes 3145736 | tf_op jit(solution)/shard_map/ppermute | solution.py:39
  143.9 2.7 %collective-permute-start.32 = (f32[512,128]{1,0:T(8,128)S(1)}, f32[512,128]{1,0:T(8,128)S(1)}, u32[]{:S(2)}, u32[]{:S(2)}) collective-permute-start(f32[512,128]{1,0:T(8,128)S(1)} %get-tuple-element.66), channel_id=1, source_target_pairs={{0,1},{1,0},{2,3},{3,2},{4,5},{5,4},{6,7},{7,6},{8,9},{9,8},{10,11... | collective-permute-start | bytes 786440 | tf_op jit(solution)/shard_map/ppermute | solution.py:39
